TPU v7x, 32 devices: a whole 2x2x4 slice. The times are simulated.
32 devices in a mesh: gx: 8 (over y, x, core), gy: 4 (over z).
Axes of the slice: x: 2, y: 2, z: 4, core: 2. Of those that a mesh axis runs over, the one named last changes fastest.
Arguments:
- leaf_multipoles: bfloat16 [36, 32, 32, 128], P(None, 'gx', 'gy'), may hold values from -6 to 6
- positions: float32 [3, 8, 32, 32, 128], P(None, None, 'gx', 'gy'), may hold values from 0 to 1
- masses: float32 [8, 32, 32, 128], P(None, 'gx', 'gy'), may hold values from 0.1 to 1
- counts: int32 [32, 32, 128], P('gx', 'gy'), may hold values from 0 to 8
- up_operator: bfloat16 [288, 36], replicated, may hold values from -0.375 to 0.375
- far_operator: bfloat16 [36, 11376], replicated, may hold values from -0.078125 to 0.078125
- down_operator: bfloat16 [36, 288], replicated, may hold values from -1 to 1
Outputs:
- local_expansion: float32 [36, 32, 32, 128], P(None, 'gx', 'gy')
- near_potential: float32 [8, 32, 32, 128], P(None, 'gx', 'gy')
Inputs may be any that keep to these rules, and one draw needn't show every extreme that they name: Slots 0 to counts - 1 of a cell hold its particles, the others are empty.
All inputs are finite; a program needn't handle non-finite values.
Results may differ from a plain program's by a relative error of at most 0.0042.
Values may be sent and summed in bfloat16 or wider, within the bound.
No kernel may reach another device: no remote copies, remote signals or barrier semaphores. Data moves between devices by JAX's collectives and lax.ppermute only.
A program may use at most 128 MiB of HBM per device.

v0:
```python
import functools

import jax
import jax.numpy as jnp
import numpy as np
from jax import lax
from jax.experimental import pallas as pl
from jax.experimental.pallas import tpu as pltpu
from jax.sharding import PartitionSpec as P

SOFTENING = 0.05
EPS = SOFTENING * SOFTENING
F32 = jnp.float32
BF16 = jnp.bfloat16
COEF = 36
GROUP = 4 * COEF
NEAR_ROWS = 256
Y_LEAF = NEAR_ROWS
Y_SIX = Y_LEAF + 2 * GROUP
Y_FIVE = Y_SIX + GROUP
Y_ROWS = Y_FIVE + 80
X_NEAR = 320
X_LEAF = 2 * X_NEAR
X_SIX = X_LEAF + 6 * GROUP
X_HALO = X_SIX + GROUP
X_FIVE = X_HALO + GROUP
X_ROWS = X_FIVE + 80

VMEM = pl.BlockSpec(memory_space=pltpu.VMEM)
SMEM = pl.BlockSpec(memory_space=pltpu.SMEM)


def shape(dims, dtype):
    return jax.ShapeDtypeStruct(dims, dtype)


def kernel_call(body, outs, inputs, scratch=(), scalars=0, limit=48):
    return pl.pallas_call(
        body,
        out_shape=outs,
        in_specs=[SMEM] * scalars + [VMEM] * (len(inputs) - scalars),
        out_specs=[VMEM] * len(outs),
        scratch_shapes=list(scratch),
        compiler_params=pltpu.CompilerParams(vmem_limit_bytes=limit * 1024 * 1024),
    )(*inputs)


def iota(dims, axis):
    return lax.broadcasted_iota(jnp.int32, dims, axis)


def dot(lhs, rhs):
    return lax.dot_general(lhs, rhs, (((1,), (0,)), ((), ())), preferred_element_type=F32)


def dot_nt(lhs, rhs):
    return lax.dot_general(lhs, rhs, (((1,), (1,)), ((), ())), preferred_element_type=F32)


def one_hot(mask):
    return jnp.where(mask, F32(1.0), F32(0.0)).astype(BF16)


def parts(value):
    high = value.astype(BF16)
    return high, (value - high.astype(F32)).astype(BF16)


def lane_roll(value, shift):
    return pltpu.roll(value, shift % 128, 1) if shift % 128 else value


def up_blocks(up_ref):
    eye = one_hot(iota((COEF, COEF), 0) == iota((COEF, COEF), 1))
    whole = up_ref[...].astype(F32)
    halves = []
    for bit in range(2):
        rows = jnp.concatenate(
            [whole[(2 * k + bit) * COEF : (2 * k + bit + 1) * COEF] for k in range(4)], axis=0
        )
        halves.append(dot_nt(eye, rows.astype(BF16)).astype(BF16))
    return halves


def prep_kernel(
    place, m_ref, pos_ref, mass_ref, count_ref, up_ref,
    grid_ref, up_msg, down_msg, five_ref, live_ref, m32, x32, six32, five32,
):
    m32[...] = m_ref[...].astype(F32)
    for x in range(4):
        for y in range(8):
            start = ((x // 2) * 4 + y // 2) * GROUP + (2 * (x % 2) + y % 2) * COEF
            x32[start : start + COEF, :] = m32[pl.ds(x * 8 + y, COEF, stride=32), :]
    grid = x32[...].astype(BF16)
    grid_ref[...] = grid
    count = count_ref[...]
    for slot in range(8):
        live_ref[slot * 32 : slot * 32 + 32, :] = jnp.where(
            count > slot, mass_ref[slot * 32 : slot * 32 + 32, :], F32(0.0)
        )
    for msg, y, parent in ((up_msg, 7, 3), (down_msg, 0, 0)):
        rows = []
        for x in range(4):
            rows.append(pos_ref[pl.ds(x * 8 + y, 24, stride=32), :])
            rows.append(live_ref[pl.ds(x * 8 + y, 8, stride=32), :])
        high, low = parts(jnp.concatenate(rows, axis=0))
        msg[0:128, :] = high
        msg[128:256, :] = low
        for xp in range(2):
            msg[Y_LEAF + xp * GROUP : Y_LEAF + (xp + 1) * GROUP, :] = grid_ref[
                (xp * 4 + parent) * GROUP : (xp * 4 + parent + 1) * GROUP, :
            ]
    low_half = iota((COEF, 128), 1) < 64
    even_up, odd_up = up_blocks(up_ref)
    row, col = iota((128, 128), 0), iota((128, 128), 1)
    split_z = one_hot(row == 2 * (col % 64) + col // 64)
    split = dot(grid, split_z).astype(BF16)
    columns = jnp.concatenate([split[k * GROUP : (k + 1) * GROUP] for k in range(8)], axis=1)
    even, odd = dot(even_up, columns), dot(odd_up, columns)
    for xp in range(2):
        for y in range(2):
            first, second = (xp * 4 + y) * 128, (xp * 4 + 2 + y) * 128
            near_part = even[:, first : first + 128] + lane_roll(odd[:, first : first + 128], 64)
            far_part = lane_roll(even[:, second : second + 128], 64) + odd[:, second : second + 128]
            start = (2 * xp + y) * COEF
            six32[start : start + COEF, :] = jnp.where(low_half, near_part, far_part)
    six = six32[...].astype(BF16)
    split_six = one_hot(row == ((col // 32) % 2) * 64 + 2 * (col % 32) + col // 64)
    split = dot(six, split_six).astype(BF16)
    five = dot(even_up, split) + lane_roll(dot(odd_up, split), 64)
    five32[...] = jnp.zeros_like(five32)
    mine = iota((COEF, 128), 1) // 32 == place[1]
    for y in range(2):
        moved = pltpu.roll(five, (32 * place[1] + 96 * y) % 128, 1)
        five32[y * COEF : (y + 1) * COEF, :] = jnp.where(mine, moved, F32(0.0))
    five_ref[...] = five32[...].astype(BF16)
    for msg in (up_msg, down_msg):
        msg[Y_SIX:Y_FIVE, :] = six
        msg[Y_FIVE:Y_ROWS, :] = five_ref[...]


def prepare(place, leaf, positions, masses, counts, up_operator):
    return kernel_call(
        prep_kernel,
        (
            shape((8 * GROUP, 128), BF16),
            shape((Y_ROWS, 128), BF16),
            shape((Y_ROWS, 128), BF16),
            shape((80, 128), BF16),
            shape((256, 128), F32),
        ),
        (place, leaf, positions, masses, counts, up_operator),
        (
            pltpu.VMEM((1152, 128), F32),
            pltpu.VMEM((1152, 128), F32),
            pltpu.VMEM((GROUP, 128), F32),
            pltpu.VMEM((80, 128), F32),
        ),
        scalars=1,
    )


def cross_kernel(
    below, above, two, mine, grid_ref, pos_ref, live_ref, to_low, to_high, near32
):
    five = (
        mine[Y_FIVE:Y_ROWS, :].astype(F32)
        + below[Y_FIVE:Y_ROWS, :].astype(F32)
        + above[Y_FIVE:Y_ROWS, :].astype(F32)
        + two[...].astype(F32)
    ).astype(BF16)
    low_half = iota((GROUP, 128), 1) < 64
    halo = jnp.where(
        low_half, above[Y_SIX:Y_FIVE, :].astype(F32), below[Y_SIX:Y_FIVE, :].astype(F32)
    ).astype(BF16)
    for msg, x, xp in ((to_low, 0, 0), (to_high, 3, 1)):
        for slot in range(8):
            for axis in range(3):
                start = (axis * 8 + slot) * 32 + x * 8
                near32[pl.ds(axis * 8 + slot, 8, stride=32), :] = pos_ref[start : start + 8, :]
            start = slot * 32 + x * 8
            near32[pl.ds(24 + slot, 8, stride=32), :] = live_ref[start : start + 8, :]
        high, low = parts(near32[...])
        for half, value in ((0, high), (1, low)):
            base = half * X_NEAR
            msg[base + 32 : base + 288, :] = value
            source = half * 128 + x * 32
            msg[base : base + 32, :] = below[source : source + 32, :]
            msg[base + 288 : base + 320, :] = above[source : source + 32, :]
        source = Y_LEAF + xp * GROUP
        msg[X_LEAF : X_LEAF + GROUP, :] = below[source : source + GROUP, :]
        msg[X_LEAF + GROUP : X_LEAF + 5 * GROUP, :] = grid_ref[
            xp * 4 * GROUP : (xp + 1) * 4 * GROUP, :
        ]
        msg[X_LEAF + 5 * GROUP : X_SIX, :] = above[source : source + GROUP, :]
        msg[X_SIX:X_HALO, :] = mine[Y_SIX:Y_FIVE, :]
        msg[X_HALO:X_FIVE, :] = halo
        msg[X_FIVE:X_ROWS, :] = five


def cross(below, above, two, mine, grid, positions, live):
    return kernel_call(
        cross_kernel,
        (shape((X_ROWS, 128), BF16), shape((X_ROWS, 128), BF16)),
        (below, above, two, mine, grid, positions, live),
        (pltpu.VMEM((256, 128), F32),),
    )


def inverse_distance(target, source):
    squared = F32(EPS)
    for axis in range(3):
        separation = source[axis] - target[axis]
        squared = squared + separation * separation
    return lax.rsqrt(squared)


def inner_kernel(pos_ref, live_ref, out_ref, shifted, sums):
    row = iota((8, 128), 0)
    sums[...] = jnp.zeros_like(sums)

    def fill(x, carry):
        for slot in range(8):
            values = [pos_ref[axis, slot, x] for axis in range(3)] + [live_ref[slot, x]]
            for index, step in enumerate((-1, 0, 1)):
                moved = [lane_roll(value, -step) for value in values]
                if step:
                    moved[2] = moved[2] + F32(step)
                for k in range(4):
                    shifted[index, k, slot, x] = moved[k]
        return carry

    lax.fori_loop(0, 4, fill, 0)

    def targets(x):
        return [[shifted[1, k, slot, x] for k in range(4)] for slot in range(8)]

    def pairs(goals, x, step, totals):
        step_x, step_y, step_z = step
        edge = row == (7 if step_y > 0 else 0)
        for slot in range(8):
            source = [shifted[step_z + 1, k, slot, x] for k in range(4)]
            if step_y:
                source = [pltpu.roll(value, (-step_y) % 8, 0) for value in source]
                source[1] = source[1] + F32(step_y)
                source[3] = jnp.where(edge, F32(0.0), source[3])
            if step_x:
                source[0] = source[0] + F32(step_x)
            back = None
            for goal in range(8):
                inverse = inverse_distance(goals[goal], source)
                totals[goal] = totals[goal] + source[3] * inverse
                term = goals[goal][3] * inverse
                back = term if back is None else back + term
            if step_y:
                back = pltpu.roll(jnp.where(edge, F32(0.0), back), step_y % 8, 0)
            sums[step_z + 1, slot, x] = sums[step_z + 1, slot, x] + back

    def plane(x, carry):
        goals = targets(x)
        totals = [jnp.zeros((8, 128), F32) for slot in range(8)]
        for slot in range(8):
            for goal in range(slot):
                inverse = inverse_distance(goals[goal], goals[slot])
                totals[goal] = totals[goal] + goals[slot][3] * inverse
                totals[slot] = totals[slot] + goals[goal][3] * inverse
        for step in ((0, 0, 1), (0, 1, -1), (0, 1, 0), (0, 1, 1)):
            pairs(goals, x, step, totals)
        for slot in range(8):
            sums[1, slot, x] = sums[1, slot, x] + totals[slot]
        return carry

    def planes(x, carry):
        for step_y in (-1, 0, 1):
            goals = targets(x)
            totals = [sums[1, slot, x] for slot in range(8)]
            for step_z in (-1, 0, 1):
                pairs(goals, x + 1, (1, step_y, step_z), totals)
            for slot in range(8):
                sums[1, slot, x] = totals[slot]
        return carry

    lax.fori_loop(0, 4, plane, 0)
    lax.fori_loop(0, 3, planes, 0)

    def finish(x, carry):
        for slot in range(8):
            out_ref[slot, x] = (
                sums[1, slot, x] + lane_roll(sums[0, slot, x], -1) + lane_roll(sums[2, slot, x], 1)
            )
        return carry

    lax.fori_loop(0, 4, finish, 0)


def inner_pairs(positions, live):
    return kernel_call(
        inner_kernel,
        (shape((8, 4, 8, 128), F32),),
        (positions, live),
        (pltpu.VMEM((3, 4, 8, 4, 8, 128), F32), pltpu.VMEM((3, 8, 4, 8, 128), F32)),
    )[0]


def edge_kernel(
    inner_ref, pos_ref, live_ref, count_ref, below, above, low, high, out_ref,
    sides, near32, shifted, sums,
):
    row = iota((8, 128), 0)
    for index, msg in enumerate((low, high)):
        sides[index] = msg[0:X_NEAR, :].astype(F32) + msg[X_NEAR : 2 * X_NEAR, :].astype(F32)
    for index, msg in enumerate((below, above)):
        near32[index] = msg[0:128, :].astype(F32) + msg[128:256, :].astype(F32)

    def fill_face(index, carry):
        for slot in range(8):
            for step_y in range(3):
                values = [
                    sides[index, pl.ds(step_y * 32 + 8 * k + slot, 8, stride=32), :]
                    for k in range(4)
                ]
                values[0] = values[0] + (2 * index - 1).astype(F32)
                values[1] = values[1] + F32(step_y - 1)
                for step_z in range(3):
                    moved = [lane_roll(value, 1 - step_z) for value in values]
                    moved[2] = moved[2] + F32(step_z - 1)
                    for k in range(4):
                        shifted[step_y * 3 + step_z, k, slot] = moved[k]
        return carry

    def gather(goals, totals):
        def body(index, carry):
            carry = list(carry)
            for slot in range(8):
                source = [shifted[index, k, slot] for k in range(4)]
                for goal in range(8):
                    carry[goal] = carry[goal] + source[3] * inverse_distance(goals[goal], source)
            return tuple(carry)

        return lax.fori_loop(0, 9, body, tuple(totals))

    def face(index, carry):
        fill_face(index, 0)
        x = 3 * index
        goals = [[pos_ref[axis, slot, x] for axis in range(3)] for slot in range(8)]
        totals = gather(goals, [inner_ref[slot, x] for slot in range(8)])
        for slot in range(8):
            sums[slot, x] = totals[slot]
        return carry

    lax.fori_loop(0, 2, face, 0)
    for x in (1, 2):
        for slot in range(8):
            sums[slot, x] = inner_ref[slot, x]
    upper = row >= 4
    turn = jnp.where(upper, F32(1.0), F32(-1.0))
    for slot in range(8):
        for k in range(4):
            r = 8 * k + slot
            none = jnp.zeros((1, 128), F32)
            source = [
                [none] + [near32[side, pl.ds(x * 32 + r, 1), :] for x in range(4)] + [none]
                for side in range(2)
            ]
            for step_x in range(3):
                value = jnp.concatenate(
                    source[0][step_x : step_x + 4] + source[1][step_x : step_x + 4], axis=0
                )
                if k == 0:
                    value = value + F32(step_x - 1)
                if k == 1:
                    value = value + turn
                for step_z in range(3):
                    moved = lane_roll(value, 1 - step_z)
                    if k == 2:
                        moved = moved + F32(step_z - 1)
                    shifted[step_x * 3 + step_z, k, slot] = moved

    def edge_rows(ref, lead):
        return jnp.concatenate(
            [ref[lead + (x, pl.ds(0, 1))] for x in range(4)]
            + [ref[lead + (x, pl.ds(7, 1))] for x in range(4)],
            axis=0,
        )

    goals = [[edge_rows(pos_ref, (axis, slot)) for axis in range(3)] for slot in range(8)]
    totals = gather(goals, [jnp.zeros((8, 128), F32) for slot in range(8)])
    for slot in range(8):
        for x in range(4):
            sums[slot, x, pl.ds(0, 1)] = sums[slot, x, pl.ds(0, 1)] + totals[slot][x : x + 1]
            sums[slot, x, pl.ds(7, 1)] = sums[slot, x, pl.ds(7, 1)] + totals[slot][x + 4 : x + 5]
    for slot in range(8):
        out_ref[slot] = jnp.where(count_ref[...] > slot, -sums[slot] / 8, F32(0.0))


def edge_pairs(inner, positions, live, counts, below, above, low, high):
    return kernel_call(
        edge_kernel,
        (shape((8, 4, 8, 128), F32),),
        (inner, positions, live, counts, below, above, low, high),
        (
            pltpu.VMEM((2, X_NEAR, 128), F32),
            pltpu.VMEM((2, 128, 128), F32),
            pltpu.VMEM((9, 4, 8, 8, 128), F32),
            pltpu.VMEM((8, 4, 8, 128), F32),
        ),
    )[0]


def far_starts():
    starts, count = {}, 0
    for step_x in range(-3, 4):
        for step_y in range(-3, 4):
            starts[step_x, step_y] = count * COEF
            count += 7 if max(abs(step_x), abs(step_y)) >= 2 else 4
    return starts


def operator_kernel(far_ref, out_ref, far32, stack):
    far32[:, 0:11264] = far_ref[:, 0:11264].astype(F32)
    far32[:, 11264:11520] = jnp.zeros((COEF, 256), F32)
    far32[:, 11264:11376] = far_ref[:, 11264:11376].astype(F32)
    lane = iota((COEF, 256), 1)

    def window(start):
        base = start // 128 * 128
        value = far32[:, base : base + 384]
        shift = start - base
        return (pltpu.roll(value, 384 - shift, 1) if shift else value)[:, 0:256]

    starts = far_starts()
    for step_x in range(-3, 4):
        for step_y in range(-3, 4):
            start = starts[step_x, step_y]
            if max(abs(step_x), abs(step_y)) >= 2:
                block = jnp.where(lane < 7 * COEF, window(start), F32(0.0))
            else:
                block = jnp.where(
                    lane < 2 * COEF,
                    window(start),
                    jnp.where(
                        (lane >= 5 * COEF) & (lane < 7 * COEF), window(start - 3 * COEF), F32(0.0)
                    ),
                )
            for bit_x in range(2):
                for bit_y in range(2):
                    source_x, source_y = step_x + bit_x, step_y + bit_y
                    if -2 <= source_x <= 3 and -2 <= source_y <= 3:
                        shift_x, child_x = source_x // 2 + 1, source_x % 2
                        shift_y, child_y = source_y // 2 + 1, source_y % 2
                        first = shift_y * GROUP + (2 * child_x + child_y) * COEF
                        bits = (2 * bit_x + bit_y) * 256
                        stack[shift_x, first : first + COEF, bits : bits + 256] = block
    for shift_x in range(3):
        for k in range(8):
            out_ref[shift_x, k * 128 : (k + 1) * 128, :] = jnp.transpose(
                stack[shift_x, :, k * 128 : (k + 1) * 128]
            ).astype(BF16)


def far_matrix(far_operator):
    return kernel_call(
        operator_kernel,
        (shape((3, 1024, 3 * GROUP), BF16),),
        (far_operator,),
        (pltpu.VMEM((COEF, 11520), F32), pltpu.VMEM((3, 3 * GROUP, 1024), F32)),
    )[0]


def z_sum(products, bits, lanes, roll):
    odd = iota((COEF, 128), 1) % 2 == 1
    total = None
    for step in range(-3, 4):
        first = bits * 256 + (step + 3) * COEF
        value = roll(products[first : first + COEF, lanes], step)
        if step == 3:
            value = jnp.where(odd, F32(0.0), value)
        if step == -3:
            value = jnp.where(odd, value, F32(0.0))
        total = value if total is None else total + value
    return total


def leaf_roll(value, step):
    return lane_roll(value, -step)


def six_roll(value, step):
    if not step:
        return value
    cell = iota(value.shape, 1) % 64 + step
    inside = (cell >= 0) & (cell < 64)
    return jnp.where(inside, lane_roll(value, -step), lane_roll(value, 64 - step))


def coarse_roll(value, step):
    if not step:
        return value
    lane = iota(value.shape, 1)
    period = jnp.where(lane < 32, 32, jnp.where(lane < 48, 16, 8))
    cell = jnp.where(lane < 32, lane, jnp.where(lane < 48, lane - 32, lane - 48))
    inside = (cell + step >= 0) & (cell + step < period)
    sign = 1 if step > 0 else -1
    wrapped = jnp.where(
        period == 32,
        lane_roll(value, sign * 32 - step),
        jnp.where(period == 16, lane_roll(value, sign * 16 - step), lane_roll(value, sign * 8 - step)),
    )
    return jnp.where(inside, lane_roll(value, -step), wrapped)


def far_kernel(
    place, matrix, grid_ref, mine, below, above, low, high, near_three, up_three, down_three,
    up_ref, down_ref, out_ref, cells, fives, fours, three32, products, coarse, down32, downs, expand,
    lifted,
):
    gx, gy = place[0], place[1]
    row, col = iota((128, 128), 0), iota((128, 128), 1)
    cells[:, 0:128] = low[X_LEAF:X_SIX, :]
    cells[:, 384:512] = high[X_LEAF:X_SIX, :]
    for xp in range(2):
        lanes = slice(128 + 128 * xp, 256 + 128 * xp)
        source = Y_LEAF + xp * GROUP
        cells[0:GROUP, lanes] = below[source : source + GROUP, :]
        cells[GROUP : 5 * GROUP, lanes] = grid_ref[xp * 4 * GROUP : (xp + 1) * 4 * GROUP, :]
        cells[5 * GROUP : 6 * GROUP, lanes] = above[source : source + GROUP, :]
    size = lax.axis_size("gx")
    for shift, msg, first in (
        (-1, near_three, 0), (0, near_three, 80), (1, near_three, 160),
        (-4, up_three, 0), (-3, up_three, 80), (-2, up_three, 160),
        (2, down_three, 0), (3, down_three, 80), (4, down_three, 160),
    ):
        at = pl.multiple_of(lax.rem(gx + shift + size, size) * 72, 8)
        fives[pl.ds(at, 72), :] = msg[first : first + 72, :].astype(F32)
    even_up, odd_up = up_blocks(up_ref)

    def upward(grouped, split):
        children = dot(grouped.astype(BF16), split).astype(BF16)
        value = dot(even_up, children) + lane_roll(dot(odd_up, children), 64)
        return value.astype(BF16).astype(F32)

    lane = col % 64
    split_five = one_hot(
        (row == ((lane // 16 % 2) * 2 + lane // 32) * 32 + 2 * (lane % 16) + col // 64)
    )
    for x in range(4):
        value = upward(fives[x * GROUP : (x + 1) * GROUP, :], split_five)
        first = (x // 2) * GROUP + (x % 2) * 2 * COEF
        fours[first : first + COEF, :] = value
        fours[first + COEF : first + 2 * COEF, :] = lane_roll(value, 96)
    split_four = one_hot((row == (lane // 8) * 16 + 2 * (lane % 8) + col // 64) & (lane < 16))
    for x in range(2):
        value = upward(fours[x * GROUP : (x + 1) * GROUP, :], split_four)
        three32[x * 2 * COEF : x * 2 * COEF + COEF, :] = value
        three32[x * 2 * COEF + COEF : (x + 1) * 2 * COEF, :] = lane_roll(value, 120)
    three = dot(three32[...].astype(BF16), one_hot((row == col - 48) & (col >= 48) & (col < 56)))
    halo = jnp.where(
        iota((GROUP, 128), 1) < 64,
        above[Y_SIX:Y_FIVE, :].astype(F32),
        below[Y_SIX:Y_FIVE, :].astype(F32),
    )
    wide_low = iota((GROUP, 128), 1) < 64
    total = None
    for shift_x in range(3):
        if shift_x == 1:
            own, other = mine[Y_SIX:Y_FIVE, :].astype(F32), halo
        else:
            msg = low if shift_x == 0 else high
            own = msg[X_SIX:X_HALO, :].astype(F32)
            other = msg[X_HALO:X_FIVE, :].astype(F32)
        six = [
            lane_roll(jnp.where(wide_low, own, other), 64),
            own,
            lane_roll(jnp.where(wide_low, other, own), 64),
        ]
        at = pl.multiple_of(lax.rem(gx // 2 + shift_x + 3, 4) * GROUP, 8)
        five = fives[pl.ds(at, GROUP), :].astype(BF16)
        at = pl.multiple_of(lax.rem(gx // 4 + shift_x + 1, 2) * GROUP, 8)
        four = fours[pl.ds(at, GROUP), :].astype(BF16)
        blocks = []
        for shift_y in range(3):
            y_five = lax.rem(gy + shift_y + 3, 4)
            y_four = lax.rem(gy // 2 + shift_y + 1, 2)
            part = dot(five, one_hot((row == y_five * 32 + col) & (col < 32)))
            part = part + dot(
                four, one_hot((row == y_four * 16 + col - 32) & (col >= 32) & (col < 48))
            )
            blocks.append(jnp.concatenate([six[shift_y], part + three], axis=1))
        window = jnp.concatenate(blocks, axis=0).astype(BF16)
        term = dot(matrix[shift_x], window)
        total = term if total is None else total + term
    products[...] = total
    for bits in range(4):
        coarse[bits, 0:COEF, 0:128] = z_sum(products, bits, slice(0, 128), six_roll)
        coarse[bits, 0:COEF, 128:256] = z_sum(products, bits, slice(128, 256), coarse_roll)
    eye = one_hot(iota((8 * COEF, 8 * COEF), 0) == iota((8 * COEF, 8 * COEF), 1))
    down32[...] = dot_nt(eye, down_ref[...])
    downs[...] = jnp.zeros_like(downs)
    for bits in range(4):
        for bit in range(2):
            first = (2 * bits + bit) * COEF
            downs[bit, bits * 40 : bits * 40 + COEF, :] = down32[first : first + COEF, :]
    operators = [downs[bit].astype(BF16) for bit in range(2)]

    def spread(value, mask):
        return [dot(part, one_hot(mask)).astype(BF16) for part in parts(value)]

    def lift(wide, lanes):
        halves = [dot(value, wide[0]) + dot(value, wide[1]) for value in operators]
        lifted[:, lanes] = jnp.where(iota(halves[0].shape, 1) % 2 == 1, halves[1], halves[0])

    def child(bits, lanes):
        first = bits * 40 if isinstance(bits, int) else pl.multiple_of(bits * 40, 8)
        return lifted[pl.ds(first, COEF), lanes]

    first_lanes = slice(0, 128)

    right = slice(128, 256)
    bits = 2 * lax.rem(gx // 4, 2) + lax.rem(gy // 2, 2)
    value = coarse[bits, 0:COEF, right]
    wide = spread(value, (row == 48 + (col - 32) // 2) & (col >= 32) & (col < 48))
    bits = 2 * lax.rem(gx // 2, 2) + lax.rem(gy, 2)
    lift(wide, first_lanes)
    value = coarse[bits, 0:COEF, right] + child(bits, first_lanes)
    wide = spread(value, (row == 32 + col // 2) & (col < 32))
    lift(wide, first_lanes)
    wides = []
    for y in range(2):
        bits = 2 * lax.rem(gx, 2) + y
        value = coarse[bits, 0:COEF, right] + child(bits, first_lanes)
        wides.append(spread(value, (row == (col % 64) // 2) & (col // 64 == y)))
    wide = [(a.astype(F32) + b.astype(F32)).astype(BF16) for a, b in zip(*wides)]
    lift(wide, first_lanes)
    for bits in range(4):
        value = coarse[bits, 0:COEF, 0:128] + child(bits, first_lanes)
        for y in range(2):
            for k, part in enumerate(spread(value, row == y * 64 + col // 2)):
                at = ((bits // 2) * 4 + 2 * y + bits % 2) * 128
                expand[k, :, at : at + 128] = part
    lift([expand[k] for k in range(2)], slice(0, 1024))
    for parent in range(4):
        rows = slice(parent * GROUP, (parent + 3) * GROUP)
        total = None
        for shift_x in range(3):
            lanes = slice(shift_x * 128, shift_x * 128 + 256)
            term = dot(matrix[shift_x], cells[rows, lanes])
            total = term if total is None else total + term
        products[...] = total
        for xp in range(2):
            at = (xp * 4 + parent) * 128
            for bits in range(4):
                value = z_sum(products, bits, slice(xp * 128, xp * 128 + 128), leaf_roll)
                value = value + child(bits, slice(at, at + 128))
                x, y = 2 * xp + bits // 2, 2 * parent + bits % 2
                out_ref[pl.ds(x * 8 + y, COEF, stride=32), :] = value


def all_levels(*inputs):
    return kernel_call(
        far_kernel,
        (shape((1152, 128), F32),),
        inputs,
        (
            pltpu.VMEM((6 * GROUP, 512), BF16),
            pltpu.VMEM((576, 128), F32),
            pltpu.VMEM((2 * GROUP, 128), F32),
            pltpu.VMEM((GROUP, 128), F32),
            pltpu.VMEM((1024, 256), F32),
            pltpu.VMEM((4, 40, 256), F32),
            pltpu.VMEM((8 * COEF, COEF), F32),
            pltpu.VMEM((2, 160, COEF), F32),
            pltpu.VMEM((2, COEF, 1024), BF16),
            pltpu.VMEM((160, 1024), F32),
        ),
        scalars=1,
    )[0]


def moved(value, step_x, step_y):
    size_x, size_y = lax.axis_size("gx"), lax.axis_size("gy")
    table = [
        (x * size_y + y, (x + step_x) % size_x * size_y + (y + step_y) % size_y)
        for x in range(size_x)
        for y in range(size_y)
    ]
    return lax.ppermute(value, ("gx", "gy"), table)


def per_device(
    leaf_multipoles, positions, masses, counts, up_operator, far_operator, down_operator
):
    place = jnp.stack([lax.axis_index("gx"), lax.axis_index("gy")]).astype(jnp.int32)
    flat_positions = positions.reshape(768, 128)
    flat_counts = counts.reshape(32, 128)
    grid, up_msg, down_msg, five, live = prepare(
        place, leaf_multipoles.reshape(1152, 128), flat_positions, masses.reshape(256, 128),
        flat_counts, up_operator,
    )
    below = moved(up_msg, 0, 1)
    above = moved(down_msg, 0, -1)
    two = moved(five, 0, 2)
    live_cells = live.reshape(8, 4, 8, 128)
    matrix = far_matrix(far_operator)
    below, above, two, matrix = lax.optimization_barrier((below, above, two, matrix))
    to_low, to_high = cross(below, above, two, up_msg, grid, flat_positions, live)
    low = moved(to_high, 1, 0)
    high = moved(to_low, -1, 0)
    inner = inner_pairs(positions, live_cells)
    low, high, inner = lax.optimization_barrier((low, high, inner))
    own_five = to_low[X_FIVE:]
    three = jnp.concatenate([low[X_FIVE:], own_five, high[X_FIVE:]], axis=0)
    up_three = moved(three, 3, 0)
    down_three = moved(three, -3, 0)
    potential = edge_pairs(inner, positions, live_cells, counts, below, above, low, high)
    up_three, down_three, potential = lax.optimization_barrier((up_three, down_three, potential))
    expansion = all_levels(
        place, matrix, grid, up_msg, below, above, low, high, three, up_three, down_three,
        up_operator, down_operator,
    )
    return expansion.reshape(36, 4, 8, 128), potential


def extended(cells, sides, width):
    for axis, dim in sides:
        count = lax.axis_size(axis)
        head = lax.slice_in_dim(cells, 0, width, axis=dim)
        tail = lax.slice_in_dim(cells, cells.shape[dim] - width, cells.shape[dim], axis=dim)
        cells = jnp.concatenate(
            [
                lax.ppermute(tail, axis, [(i, (i + 1) % count) for i in range(count)]),
                cells,
                lax.ppermute(head, axis, [((i + 1) % count, i) for i in range(count)]),
            ],
            axis=dim,
        )
    return cells


def shift_list():
    return [
        (step_x, step_y, step_z)
        for step_x in (-1, 0, 1)
        for step_y in (-1, 0, 1)
        for step_z in (-1, 0, 1)
    ]


def child_bits(number):
    return (number // 4, number // 2 % 2, number % 2)


def offset_table():
    vectors = [
        (step_x, step_y, step_z)
        for step_x in range(-3, 4)
        for step_y in range(-3, 4)
        for step_z in range(-3, 4)
        if max(abs(step_x), abs(step_y), abs(step_z)) >= 2
    ]
    lookup = np.full((27, 8, 8), len(vectors), dtype=np.int32)
    for shift_id, offset in enumerate(shift_list()):
        for source in range(8):
            for target in range(8):
                vector = tuple(
                    (
                        2 * offset[axis_id]
                        + child_bits(source)[axis_id]
                        - child_bits(target)[axis_id]
                        for axis_id in range(3)
                    )
                )
                if max(abs(vector[0]), abs(vector[1]), abs(vector[2])) >= 2:
                    lookup[shift_id, source, target] = vectors.index(vector)
    return lookup


def assemble(far_operator):
    coeff_count = far_operator.shape[0]
    blocks = far_operator.reshape(coeff_count, -1, coeff_count)
    blocks = jnp.concatenate(
        [blocks, jnp.zeros((coeff_count, 1, coeff_count), blocks.dtype)], axis=1
    )
    picked = jnp.take(blocks, jnp.asarray(offset_table().reshape(-1), dtype=jnp.int32), axis=1)
    picked = picked.reshape(coeff_count, 27, 8, 8, coeff_count).transpose(1, 2, 0, 3, 4)
    return picked.reshape(27, 8 * coeff_count, 8 * coeff_count)


def group_cells(volume):
    size_x, size_y, size_z, coeff_count = volume.shape
    reshaped = volume.reshape(size_x // 2, 2, size_y // 2, 2, size_z // 2, 2, coeff_count)
    return reshaped.transpose(0, 2, 4, 1, 3, 5, 6).reshape(
        size_x // 2, size_y // 2, size_z // 2, 8 * coeff_count
    )


def spread_cells(grouped):
    size_x, size_y, size_z, total_rows = grouped.shape
    coeff_count = total_rows // 8
    reshaped = grouped.reshape(size_x, size_y, size_z, 2, 2, 2, coeff_count)
    return reshaped.transpose(0, 3, 1, 4, 2, 5, 6).reshape(
        2 * size_x, 2 * size_y, 2 * size_z, coeff_count
    )


def wrap_pad(volume, axis_id):
    extent = volume.shape[axis_id]
    lower = lax.slice_in_dim(volume, extent - 1, extent, axis=axis_id)
    upper = lax.slice_in_dim(volume, 0, 1, axis=axis_id)
    return jnp.concatenate([lower, volume, upper], axis=axis_id)


def wrap_window(volume, axis_id, anchor, extent):
    return lax.dynamic_slice_in_dim(wrap_pad(volume, axis_id), anchor, extent + 2, axis_id)


def region(index_now, cells, levels_up):
    anchor = index_now * cells // 2**levels_up
    extent = max(cells // 2**levels_up, 1)
    return (anchor, extent)


def cut(children, index_x, index_y, cells_x, cells_y, levels_up):
    anchor_x, extent_x = region(index_x, cells_x, levels_up)
    parent_x = region(index_x, cells_x, levels_up + 1)[0]
    anchor_y, extent_y = region(index_y, cells_y, levels_up)
    parent_y = region(index_y, cells_y, levels_up + 1)[0]
    children = lax.dynamic_slice_in_dim(children, anchor_x - 2 * parent_x, extent_x, 0)
    return lax.dynamic_slice_in_dim(children, anchor_y - 2 * parent_y, extent_y, 1)


def coarse_window(grouped, index_x, index_y, cells_x, cells_y, levels_up):
    anchor_x, extent_x = region(index_x, cells_x, levels_up)
    anchor_y, extent_y = region(index_y, cells_y, levels_up)
    windowed = wrap_window(grouped, 0, anchor_x, extent_x)
    windowed = wrap_window(windowed, 1, anchor_y, extent_y)
    return wrap_pad(windowed, 2)


def upward(up_operator, grouped):
    parent = jnp.einsum("xyzs,sj->xyzj", grouped, up_operator, preferred_element_type=jnp.float32)
    return parent.astype(jnp.bfloat16)


def downward(down_operator, parent):
    children = jnp.einsum(
        "xyzi,it->xyzt", parent, down_operator.astype(jnp.float32), precision=lax.Precision.HIGHEST
    )
    return spread_cells(children)


def far_field(padded, kernel):
    size_x = padded.shape[0] - 2
    size_y = padded.shape[1] - 2
    size_z = padded.shape[2] - 2
    running = None
    for shift_id, offset in enumerate(shift_list()):
        window_piece = padded[
            1 + offset[0] : 1 + offset[0] + size_x, 1 + offset[1] : 1 + offset[1] + size_y
        ]
        product_term = jnp.einsum(
            "xyzs,st->xyzt", window_piece, kernel[shift_id], preferred_element_type=jnp.float32
        )
        product_term = product_term[:, :, 1 + offset[2] : 1 + offset[2] + size_z]
        running = product_term if running is None else running + product_term
    return running


def near_field(positions, masses, counts):
    slot_count = masses.shape[0]
    size_x, size_y, size_z = (masses.shape[1], masses.shape[2], masses.shape[3])
    live_slot = lax.broadcasted_iota(jnp.int32, masses.shape, 0) < counts[None]
    live_mass = jnp.where(live_slot, masses, jnp.float32(0.0))
    stacked = jnp.concatenate([positions, live_mass[None]], axis=0)
    padded = wrap_pad(extended(stacked, (("gx", 2), ("gy", 3)), 1), 4)
    block_size = min(8, slot_count)
    same_slot = lax.broadcasted_iota(
        jnp.int32, (block_size, slot_count, 1, 1, 1), 0
    ) + 0 == lax.broadcasted_iota(jnp.int32, (block_size, slot_count, 1, 1, 1), 1)
    running = jnp.zeros((block_size, size_x, size_y, size_z), jnp.float32)
    for offset in shift_list():
        source = padded[
            :,
            :,
            1 + offset[0] : 1 + offset[0] + size_x,
            1 + offset[1] : 1 + offset[1] + size_y,
            1 + offset[2] : 1 + offset[2] + size_z,
        ]
        squared = jnp.float32(SOFTENING * SOFTENING)
        for axis_id in range(3):
            separation = (
                source[axis_id][None] + jnp.float32(offset[axis_id]) - positions[axis_id][:, None]
            )
            squared = squared + separation * separation
        pair_terms = source[3][None] * lax.rsqrt(squared)
        if offset == (0, 0, 0):
            pair_terms = jnp.where(same_slot, jnp.float32(0.0), pair_terms)
        running = running + jnp.sum(pair_terms, axis=1)
    results = running
    running = results
    return jnp.where(live_slot, -running / slot_count, jnp.float32(0.0))


def general_device(
    leaf_multipoles, positions, masses, counts, up_operator, far_operator, down_operator
):
    potential = near_field(positions, masses, counts)
    kernel = assemble(far_operator)
    index_x = lax.axis_index("gx")
    index_y = lax.axis_index("gy")
    cells_x = leaf_multipoles.shape[1]
    cells_y = leaf_multipoles.shape[2]
    leaf_cells = jnp.transpose(leaf_multipoles, (1, 2, 3, 0))
    grouped_leaf = group_cells(leaf_cells)
    padded = wrap_pad(extended(grouped_leaf, (("gx", 0), ("gy", 1)), 1), 2)
    far_leaf = spread_cells(far_field(padded, kernel))
    grouped_six = group_cells(upward(up_operator, grouped_leaf))
    padded = wrap_pad(extended(grouped_six, (("gx", 0), ("gy", 1)), 1), 2)
    far_six = spread_cells(far_field(padded, kernel))
    moments_five = upward(up_operator, grouped_six)
    columns = lax.all_gather(moments_five, "gy", axis=1, tiled=True)
    whole_five = lax.all_gather(columns, "gx", axis=0, tiled=True)
    grouped_five = group_cells(whole_five)
    window_five = coarse_window(grouped_five, index_x, index_y, cells_x, cells_y, 3)
    moments_four = upward(up_operator, grouped_five)
    far_five = cut(
        spread_cells(far_field(window_five, kernel)), index_x, index_y, cells_x, cells_y, 2
    )
    grouped_four = group_cells(moments_four)
    window_four = coarse_window(grouped_four, index_x, index_y, cells_x, cells_y, 4)
    far_four = cut(
        spread_cells(far_field(window_four, kernel)), index_x, index_y, cells_x, cells_y, 3
    )
    grouped_three = group_cells(upward(up_operator, grouped_four))
    window_three = coarse_window(grouped_three, index_x, index_y, cells_x, cells_y, 5)
    far_three = cut(
        spread_cells(far_field(window_three, kernel)), index_x, index_y, cells_x, cells_y, 4
    )
    expansion = far_three
    expansion = far_four + cut(
        downward(down_operator, expansion), index_x, index_y, cells_x, cells_y, 3
    )
    expansion = far_five + cut(
        downward(down_operator, expansion), index_x, index_y, cells_x, cells_y, 2
    )
    expansion = far_six + cut(
        downward(down_operator, expansion), index_x, index_y, cells_x, cells_y, 1
    )
    expansion = far_leaf + cut(
        downward(down_operator, expansion), index_x, index_y, cells_x, cells_y, 0
    )
    return (jnp.transpose(expansion, (3, 0, 1, 2)), potential)


def solution(mesh):
    small = (mesh.shape["gx"], mesh.shape["gy"]) == (8, 4)
    return jax.shard_map(
        per_device if small else general_device,
        mesh=mesh,
        in_specs=(
            P(None, "gx", "gy", None),
            P(None, None, "gx", "gy", None),
            P(None, "gx", "gy", None),
            P("gx", "gy", None),
            P(),
            P(),
            P(),
        ),
        out_specs=(P(None, "gx", "gy", None), P(None, "gx", "gy", None)),
        check_vma=False,
    )
```

profile of v0, /device:TPU:1, one launch (start us, length us, event | category | flops | bytes accessed | tf_op | source)
XLA Modules:
  0.0 52.8 jit_solution(14940544621661771545)
XLA Ops:
  0.6 0.9 %copy.9.up_ref = bf16[288,36]{1,0:T(8,128)(2,1)S(1)} copy(bf16[288,36]{0,1:T(8,128)(2,1)} %param.11) | data formatting | bytes 41472 | tf_op args[4]
  1.5 0.1 pad_add_fusion.place
  1.6 1.0 %copy-done = f32[3,8,4,8,128]{4,3,2,1,0:T(8,128)S(1)} copy-done((f32[3,8,4,8,128]{4,3,2,1,0:T(8,128)S(1)}, f32[3,8,4,8,128]{4,3,2,1,0:T(8,128)}, u32[]{:S(2)}) %copy-start) | copy-done | bytes 393240
  2.6 1.0 %copy-done.3 = bf16[36,4,8,128]{3,2,1,0:T(8,128)(2,1)S(1)} copy-done((bf16[36,4,8,128]{3,2,1,0:T(8,128)(2,1)S(1)}, bf16[36,4,8,128]{3,2,1,0:T(8,128)(2,1)}, u32[]{:S(2)}) %copy-start.3) | copy-done | bytes 294936
  3.6 0.9 %copy-done.4 = f32[8,4,8,128]{3,2,1,0:T(8,128)S(1)} copy-done((f32[8,4,8,128]{3,2,1,0:T(8,128)S(1)}, f32[8,4,8,128]{3,2,1,0:T(8,128)}, u32[]{:S(2)}) %copy-start.4) | copy-done | bytes 131096
  4.5 0.7 %copy-done.5 = s32[4,8,128]{2,1,0:T(8,128)S(1)} copy-done((s32[4,8,128]{2,1,0:T(8,128)S(1)}, s32[4,8,128]{2,1,0:T(8,128)}, u32[]{:S(2)}) %copy-start.5) | copy-done | bytes 16408
  5.2 1.9 %shard_map.86 = (bf16[1152,128]{1,0:T(8,128)(2,1)S(1)}, bf16[768,128]{1,0:T(8,128)(2,1)S(1)}, bf16[768,128]{1,0:T(8,128)(2,1)S(1)}, bf16[80,128]{1,0:T(8,128)(2,1)S(1)}, f32[256,128]{1,0:T(8,128)S(1)}) custom-call(s32[2]{0:T(128)S(1)} %pad_add_fusion.place, bf16[1152,128]{1,0:T(8,128)(2,1)S(1)} %bitcast.12, f32[768,128]{1,0:T(8,128)S(1)} %bitcast.8, ...), custom_call_target="tpu_custom_call" | custom-call | tf_op jit(solution)/shard_map/pallas_call | solution.py:38
  7.1 4.2 %collective-permute-start.1 = (bf16[768,128]{1,0:T(8,128)(2,1)S(1)}, bf16[768,128]{1,0:T(8,128)(2,1)S(1)}, u32[]{:S(2)}, u32[]{:S(2)}) collective-permute-start(bf16[768,128]{1,0:T(8,128)(2,1)S(1)} %get-tuple-element.20), channel_id=1, source_target_pairs={{0,3},{1,0},{2,1},{3,2},{4,7},{5,4},{6,5},{7,6},{8,11},{9,8},{10,9... | collective-permute-start | bytes 589832 | tf_op jit(solution)/shard_map/ppermute | solution.py:686
  11.3 0.5 collective-permute-start.2
  11.8 1.2 %copy-done.2 = bf16[36,11376]{1,0:T(8,128)(2,1)S(1)} copy-done((bf16[36,11376]{1,0:T(8,128)(2,1)S(1)}, bf16[36,11376]{1,0:T(8,128)(2,1)}, u32[]{:S(2)}) %copy-start.2) | copy-done | bytes 819096
  13.0 1.5 %shard_map.87.matrix = bf16[3,1024,432]{2,1,0:T(8,128)(2,1)S(1)} custom-call(bf16[36,11376]{1,0:T(8,128)(2,1)S(1)} %copy-done.2), custom_call_target="tpu_custom_call" | custom-call | tf_op jit(solution)/shard_map/pallas_call | solution.py:38
  14.4 0.0 copy-start.6
  14.4 5.2 %collective-permute-done.2.two = bf16[80,128]{1,0:T(8,128)(2,1)S(1)} collective-permute-done((bf16[80,128]{1,0:T(8,128)(2,1)S(1)}, bf16[80,128]{1,0:T(8,128)(2,1)S(1)}, u32[]{:S(2)}, u32[]{:S(2)}) %collective-permute-start.2) | collective-permute-done | bytes 20512 | tf_op jit(solution)/shard_map/ppermute | solution.py:686
  19.6 0.5 collective-permute-done.below
  20.1 0.2 shard_map.88
  20.4 2.8 %collective-permute-start.3 = (bf16[1872,128]{1,0:T(8,128)(2,1)S(1)}, bf16[1872,128]{1,0:T(8,128)(2,1)S(1)}, u32[]{:S(2)}, u32[]{:S(2)}) collective-permute-start(bf16[1872,128]{1,0:T(8,128)(2,1)S(1)} %get-tuple-element.28), channel_id=1, source_target_pairs={{0,4},{1,5},{2,6},{3,7},{4,8},{5,9},{6,10},{7,11},{8,12},{9,13},{1... | collective-permute-start | bytes 1437704 | tf_op jit(solution)/shard_map/ppermute | solution.py:686
  23.2 6.7 %shard_map.89.inner_ref = f32[8,4,8,128]{3,2,1,0:T(8,128)S(1)} custom-call(f32[3,8,4,8,128]{4,3,2,1,0:T(8,128)S(1)} %copy-done.1, f32[8,4,8,128]{3,2,1,0:T(8,128)S(1)} %bitcast.10), custom_call_target="tpu_custom_call" | custom-call | tf_op jit(solution)/shard_map/pallas_call | solution.py:38
  29.9 2.3 %collective-permute-done.3.low = bf16[1872,128]{1,0:T(8,128)(2,1)S(1)} collective-permute-done((bf16[1872,128]{1,0:T(8,128)(2,1)S(1)}, bf16[1872,128]{1,0:T(8,128)(2,1)S(1)}, u32[]{:S(2)}, u32[]{:S(2)}) %collective-permute-start.3) | collective-permute-done | bytes 479264 | tf_op jit(solution)/shard_map/ppermute | solution.py:686
  32.2 3.4 %collective-permute-done.4.high = bf16[1872,128]{1,0:T(8,128)(2,1)S(1)} collective-permute-done((bf16[1872,128]{1,0:T(8,128)(2,1)S(1)}, bf16[1872,128]{1,0:T(8,128)(2,1)S(1)}, u32[]{:S(2)}, u32[]{:S(2)}) %collective-permute-start.4) | collective-permute-done | bytes 479264 | tf_op jit(solution)/shard_map/ppermute | solution.py:686
  35.6 0.1 collective-permute-start.6
  35.7 1.7 %collective-permute-start.5 = (bf16[240,128]{1,0:T(8,128)(2,1)S(1)}, bf16[240,128]{1,0:T(8,128)(2,1)S(1)}, u32[]{:S(2)}, u32[]{:S(2)}) collective-permute-start(bf16[240,128]{1,0:T(8,128)(2,1)S(1)} %pad_maximum_fusion.near_three), channel_id=1, source_target_pairs={{0,12},{1,13},{2,14},{3,15},{4,16},{5,17},{6,18},{7,19},{8,20},{9,... | collective-permute-start | bytes 184328 | tf_op jit(solution)/shard_map/ppermute | solution.py:686
  37.4 4.6 %shard_map.90 = f32[8,4,8,128]{3,2,1,0:T(8,128)} custom-call(f32[8,4,8,128]{3,2,1,0:T(8,128)S(1)} %shard_map.89.inner_ref, f32[3,8,4,8,128]{4,3,2,1,0:T(8,128)S(1)} %copy-done.1, f32[8,4,8,128]{3,2,1,0:T(8,128)S(1)} %bitcast.11, s32[4,8,128]{2,1,0:T(8,128)S(1)} %copy-done.5, bf16[768,128]{1,0:T(8,128)(2,1)S(1)} %collective-permute-done.below, ...), custom_call_target="tpu_custom_call" | custom-call | tf_op jit(solution)/shard_map/pallas_call | solution.py:38
  42.1 0.0 collective-permute-done.6.down_three
  42.1 10.7 %shard_map.91 = f32[1152,128]{1,0:T(8,128)} custom-call(s32[2]{0:T(128)S(1)} %pad_add_fusion.place, bf16[3,1024,432]{2,1,0:T(8,128)(2,1)S(1)} %shard_map.87.matrix, bf16[1152,128]{1,0:T(8,128)(2,1)S(1)} %get-tuple-element.23.grid_ref, bf16[768,128]{1,0:T(8,128)(2,1)S(1)} %get-tuple-element.19.mine, bf16[768,128]{1,0:T(8,128)(2,1)S(1)} %collective-permute-done.below, ...), custom_call_target="tpu_custom_call" | custom-call | tf_op jit(solution)/shard_map/pallas_call | solution.py:38
  (16 shorter events, 0.0 us)
Async XLA Ops:
  1.6 1.0 %copy-start = (f32[3,8,4,8,128]{4,3,2,1,0:T(8,128)S(1)}, f32[3,8,4,8,128]{4,3,2,1,0:T(8,128)}, u32[]{:S(2)}) copy-start(f32[3,8,4,8,128]{4,3,2,1,0:T(8,128)} %pos_ref.3) | copy-start | bytes 1179652
  2.6 1.0 %copy-start.3 = (bf16[36,4,8,128]{3,2,1,0:T(8,128)(2,1)S(1)}, bf16[36,4,8,128]{3,2,1,0:T(8,128)(2,1)}, u32[]{:S(2)}) copy-start(bf16[36,4,8,128]{3,2,1,0:T(8,128)(2,1)} %param.7) | copy-start | bytes 884740
  3.6 0.9 %copy-start.4 = (f32[8,4,8,128]{3,2,1,0:T(8,128)S(1)}, f32[8,4,8,128]{3,2,1,0:T(8,128)}, u32[]{:S(2)}) copy-start(f32[8,4,8,128]{3,2,1,0:T(8,128)} %param.9) | copy-start | bytes 393220
  4.5 0.7 %copy-start.5 = (s32[4,8,128]{2,1,0:T(8,128)S(1)}, s32[4,8,128]{2,1,0:T(8,128)}, u32[]{:S(2)}) copy-start(s32[4,8,128]{2,1,0:T(8,128)} %count_ref.1) | copy-start | bytes 49156
  5.2 14.9 %copy-start.1 = (f32[3,8,4,8,128]{4,3,2,1,0:T(8,128)S(1)}, f32[3,8,4,8,128]{4,3,2,1,0:T(8,128)}, u32[]{:S(2)}) copy-start(f32[3,8,4,8,128]{4,3,2,1,0:T(8,128)} %pos_ref.3) | copy-start | bytes 1179652
  7.1 12.5 %collective-permute-start.1 = (bf16[768,128]{1,0:T(8,128)(2,1)S(1)}, bf16[768,128]{1,0:T(8,128)(2,1)S(1)}, u32[]{:S(2)}, u32[]{:S(2)}) collective-permute-start(bf16[768,128]{1,0:T(8,128)(2,1)S(1)} %get-tuple-element.20), channel_id=1, source_target_pairs={{0,3},{1,0},{2,1},{3,2},{4,7},{5,4},{6,5},{7,6},{8,11},{9,8},{10,9... | collective-permute-start | bytes 589832 | tf_op jit(solution)/shard_map/ppermute | solution.py:686
  11.3 8.8 %collective-permute-start = (bf16[768,128]{1,0:T(8,128)(2,1)S(1)}, bf16[768,128]{1,0:T(8,128)(2,1)S(1)}, u32[]{:S(2)}, u32[]{:S(2)}) collective-permute-start(bf16[768,128]{1,0:T(8,128)(2,1)S(1)} %get-tuple-element.19.mine), channel_id=1, source_target_pairs={{0,1},{1,2},{2,3},{3,0},{4,5},{5,6},{6,7},{7,4},{8,9},{9,10},{10,1... | collective-permute-start | bytes 589832 | tf_op jit(solution)/shard_map/ppermute | solution.py:686
  11.3 8.3 %collective-permute-start.2 = (bf16[80,128]{1,0:T(8,128)(2,1)S(1)}, bf16[80,128]{1,0:T(8,128)(2,1)S(1)}, u32[]{:S(2)}, u32[]{:S(2)}) collective-permute-start(bf16[80,128]{1,0:T(8,128)(2,1)S(1)} %get-tuple-element.21), channel_id=1, source_target_pairs={{0,2},{1,3},{2,0},{3,1},{4,6},{5,7},{6,4},{7,5},{8,10},{9,11},{10,... | collective-permute-start | bytes 61448 | tf_op jit(solution)/shard_map/ppermute | solution.py:686
  11.8 1.2 %copy-start.2 = (bf16[36,11376]{1,0:T(8,128)(2,1)S(1)}, bf16[36,11376]{1,0:T(8,128)(2,1)}, u32[]{:S(2)}) copy-start(bf16[36,11376]{1,0:T(8,128)(2,1)} %far_ref.1) | copy-start | bytes 2457220
  14.4 27.6 %copy-start.6 = (bf16[36,288]{1,0:T(8,128)(2,1)S(1)}, bf16[36,288]{1,0:T(8,128)(2,1)}, u32[]{:S(2)}) copy-start(bf16[36,288]{1,0:T(8,128)(2,1)} %down_ref.1) | copy-start | bytes 62212
  20.4 11.8 %collective-permute-start.3 = (bf16[1872,128]{1,0:T(8,128)(2,1)S(1)}, bf16[1872,128]{1,0:T(8,128)(2,1)S(1)}, u32[]{:S(2)}, u32[]{:S(2)}) collective-permute-start(bf16[1872,128]{1,0:T(8,128)(2,1)S(1)} %get-tuple-element.28), channel_id=1, source_target_pairs={{0,4},{1,5},{2,6},{3,7},{4,8},{5,9},{6,10},{7,11},{8,12},{9,13},{1... | collective-permute-start | bytes 1437704 | tf_op jit(solution)/shard_map/ppermute | solution.py:686
  23.2 12.4 %collective-permute-start.4 = (bf16[1872,128]{1,0:T(8,128)(2,1)S(1)}, bf16[1872,128]{1,0:T(8,128)(2,1)S(1)}, u32[]{:S(2)}, u32[]{:S(2)}) collective-permute-start(bf16[1872,128]{1,0:T(8,128)(2,1)S(1)} %get-tuple-element.29), channel_id=1, source_target_pairs={{0,28},{1,29},{2,30},{3,31},{4,0},{5,1},{6,2},{7,3},{8,4},{9,5},{1... | collective-permute-start | bytes 1437704 | tf_op jit(solution)/shard_map/ppermute | solution.py:686
  35.6 6.4 %collective-permute-start.6 = (bf16[240,128]{1,0:T(8,128)(2,1)S(1)}, bf16[240,128]{1,0:T(8,128)(2,1)S(1)}, u32[]{:S(2)}, u32[]{:S(2)}) collective-permute-start(bf16[240,128]{1,0:T(8,128)(2,1)S(1)} %pad_maximum_fusion.near_three), channel_id=1, source_target_pairs={{0,20},{1,21},{2,22},{3,23},{4,24},{5,25},{6,26},{7,27},{8,28},{9,... | collective-permute-start | bytes 184328 | tf_op jit(solution)/shard_map/ppermute | solution.py:686
  35.7 6.4 %collective-permute-start.5 = (bf16[240,128]{1,0:T(8,128)(2,1)S(1)}, bf16[240,128]{1,0:T(8,128)(2,1)S(1)}, u32[]{:S(2)}, u32[]{:S(2)}) collective-permute-start(bf16[240,128]{1,0:T(8,128)(2,1)S(1)} %pad_maximum_fusion.near_three), channel_id=1, source_target_pairs={{0,12},{1,13},{2,14},{3,15},{4,16},{5,17},{6,18},{7,19},{8,20},{9,... | collective-permute-start | bytes 184328 | tf_op jit(solution)/shard_map/ppermute | solution.py:686
where the time goes:
time: 53.2 us; the launch traced here: 52.8 us
  Pallas kernels  25.7 us (48%)
  waiting for transfers between devices  11.4 us (21%)
  starting transfers between devices  9.27 us (17%)
  local copies, waits for them, and re-layouts  5.66 us (11%)
  between operations  0.7 us (1%)
    pallas_call x6, Pallas kernels, kernel_call(): pl.pallas_call(body, out_shape=outs, in_specs=[SMEM] * scalars + [VMEM] *...  25.7 us
    ppermute x7, waiting for transfers between devices, moved(): return lax.ppermute(value, ('gx', 'gy'), table)  11.4 us
    ppermute x7, starting transfers between devices, moved(): return lax.ppermute(value, ('gx', 'gy'), table)  9.27 us
    unnamed x15, local copies, waits for them, and re-layouts  5.65 us
  transfers between devices with their start and end apart: 7, of which 4 were waited for; matrix products, arithmetic and copies ran while one was open for 0% of the time, Pallas kernels for 24%

commit v1 on v0

--- a/solution.py
+++ b/solution.py
@@ -14,31 +14,32 @@
 BF16 = jnp.bfloat16
 COEF = 36
 GROUP = 4 * COEF
-NEAR_ROWS = 256
-Y_LEAF = NEAR_ROWS
+Y_LEAF = 256
 Y_SIX = Y_LEAF + 2 * GROUP
-Y_FIVE = Y_SIX + GROUP
-Y_ROWS = Y_FIVE + 80
-X_NEAR = 320
-X_LEAF = 2 * X_NEAR
-X_SIX = X_LEAF + 6 * GROUP
-X_HALO = X_SIX + GROUP
-X_FIVE = X_HALO + GROUP
-X_ROWS = X_FIVE + 80
+Y_FIVE = Y_SIX + GROUP // 2
+Y_ROWS = Y_FIVE + 40
+X_LEAF = 512
+X_SIX = X_LEAF + 4 * GROUP
+X_ROWS = X_SIX + GROUP
+C_LEAF = 128
+C_SIX = C_LEAF + 2 * GROUP
+C_FIVE = C_SIX + GROUP
+C_ROWS = C_FIVE + 80
 
 VMEM = pl.BlockSpec(memory_space=pltpu.VMEM)
 SMEM = pl.BlockSpec(memory_space=pltpu.SMEM)
+HBM = pl.BlockSpec(memory_space=pltpu.MemorySpace.HBM)
 
 
 def shape(dims, dtype):
     return jax.ShapeDtypeStruct(dims, dtype)
 
 
-def kernel_call(body, outs, inputs, scratch=(), scalars=0, limit=48):
+def kernel_call(body, outs, inputs, scratch=(), scalars=0, space=VMEM, limit=48):
     return pl.pallas_call(
         body,
         out_shape=outs,
-        in_specs=[SMEM] * scalars + [VMEM] * (len(inputs) - scalars),
+        in_specs=[SMEM] * scalars + [space] * (len(inputs) - scalars),
         out_specs=[VMEM] * len(outs),
         scratch_shapes=list(scratch),
         compiler_params=pltpu.CompilerParams(vmem_limit_bytes=limit * 1024 * 1024),
@@ -71,34 +72,53 @@
 
 
 def up_blocks(up_ref):
-    eye = one_hot(iota((COEF, COEF), 0) == iota((COEF, COEF), 1))
-    whole = up_ref[...].astype(F32)
-    halves = []
-    for bit in range(2):
-        rows = jnp.concatenate(
-            [whole[(2 * k + bit) * COEF : (2 * k + bit + 1) * COEF] for k in range(4)], axis=0
+    row, col = iota((8 * COEF, GROUP), 0), iota((8 * COEF, GROUP), 1)
+    return [
+        dot(up_ref[...], one_hot(row == (col // COEF * 2 + bit) * COEF + col % COEF)).astype(BF16)
+        for bit in range(2)
+    ]
+
+
+def prep_kernel(
+    leaf_hbm, pos_hbm, mass_hbm, count_hbm, up_hbm, down_hbm, far_hbm,
+    grid_ref, up_msg, down_msg, low_msg, high_msg, six_ref, five_ref, live_ref,
+    pos_ref, count_ref, up_ref, down_ref, far_ref,
+    leaf_ref, mass_ref, m32, x32, six32, near32, sems,
+):
+    copies = [
+        pltpu.make_async_copy(source, target, sems.at[k])
+        for k, (source, target) in enumerate(
+            (
+                (leaf_hbm, leaf_ref), (pos_hbm, pos_ref), (mass_hbm, mass_ref),
+                (count_hbm, count_ref), (up_hbm, up_ref), (down_hbm, down_ref), (far_hbm, far_ref),
+            )
         )
-        halves.append(dot_nt(eye, rows.astype(BF16)).astype(BF16))
-    return halves
-
-
-def prep_kernel(
-    place, m_ref, pos_ref, mass_ref, count_ref, up_ref,
-    grid_ref, up_msg, down_msg, five_ref, live_ref, m32, x32, six32, five32,
-):
-    m32[...] = m_ref[...].astype(F32)
+    ]
+    for copy in copies:
+        copy.start()
+    copies[0].wait()
+    m32[...] = leaf_ref[...].astype(F32)
     for x in range(4):
         for y in range(8):
             start = ((x // 2) * 4 + y // 2) * GROUP + (2 * (x % 2) + y % 2) * COEF
             x32[start : start + COEF, :] = m32[pl.ds(x * 8 + y, COEF, stride=32), :]
     grid = x32[...].astype(BF16)
     grid_ref[...] = grid
+    for msg, parent in ((up_msg, 3), (down_msg, 0)):
+        for xp in range(2):
+            msg[Y_LEAF + xp * GROUP : Y_LEAF + (xp + 1) * GROUP, :] = grid_ref[
+                (xp * 4 + parent) * GROUP : (xp * 4 + parent + 1) * GROUP, :
+            ]
+    low_msg[X_LEAF:X_SIX, :] = grid_ref[0 : 4 * GROUP, :]
+    high_msg[X_LEAF:X_SIX, :] = grid_ref[4 * GROUP : 8 * GROUP, :]
+    for copy in copies[1:5]:
+        copy.wait()
     count = count_ref[...]
     for slot in range(8):
         live_ref[slot * 32 : slot * 32 + 32, :] = jnp.where(
             count > slot, mass_ref[slot * 32 : slot * 32 + 32, :], F32(0.0)
         )
-    for msg, y, parent in ((up_msg, 7, 3), (down_msg, 0, 0)):
+    for msg, y in ((up_msg, 7), (down_msg, 0)):
         rows = []
         for x in range(4):
             rows.append(pos_ref[pl.ds(x * 8 + y, 24, stride=32), :])
@@ -106,10 +126,16 @@
         high, low = parts(jnp.concatenate(rows, axis=0))
         msg[0:128, :] = high
         msg[128:256, :] = low
-        for xp in range(2):
-            msg[Y_LEAF + xp * GROUP : Y_LEAF + (xp + 1) * GROUP, :] = grid_ref[
-                (xp * 4 + parent) * GROUP : (xp * 4 + parent + 1) * GROUP, :
-            ]
+    for msg, x in ((low_msg, 0), (high_msg, 3)):
+        for slot in range(8):
+            for axis in range(3):
+                start = (axis * 8 + slot) * 32 + x * 8
+                near32[pl.ds(axis * 8 + slot, 8, stride=32), :] = pos_ref[start : start + 8, :]
+            start = slot * 32 + x * 8
+            near32[pl.ds(24 + slot, 8, stride=32), :] = live_ref[start : start + 8, :]
+        high, low = parts(near32[...])
+        msg[0:256, :] = high
+        msg[256:512, :] = low
     low_half = iota((COEF, 128), 1) < 64
     even_up, odd_up = up_blocks(up_ref)
     row, col = iota((128, 128), 0), iota((128, 128), 1)
@@ -125,85 +151,100 @@
             start = (2 * xp + y) * COEF
             six32[start : start + COEF, :] = jnp.where(low_half, near_part, far_part)
     six = six32[...].astype(BF16)
+    six_ref[...] = six
+    low_msg[X_SIX:X_ROWS, :] = six
+    high_msg[X_SIX:X_ROWS, :] = six
+    left = iota((72, 128), 1) < 64
+    first, second = six32[0:72, :], six32[72:144, :]
+    up_msg[Y_SIX:Y_FIVE, :] = jnp.where(left, lane_roll(first, 64), second).astype(BF16)
+    down_msg[Y_SIX:Y_FIVE, :] = jnp.where(left, first, lane_roll(second, 64)).astype(BF16)
     split_six = one_hot(row == ((col // 32) % 2) * 64 + 2 * (col % 32) + col // 64)
     split = dot(six, split_six).astype(BF16)
     five = dot(even_up, split) + lane_roll(dot(odd_up, split), 64)
-    five32[...] = jnp.zeros_like(five32)
-    mine = iota((COEF, 128), 1) // 32 == place[1]
-    for y in range(2):
-        moved = pltpu.roll(five, (32 * place[1] + 96 * y) % 128, 1)
-        five32[y * COEF : (y + 1) * COEF, :] = jnp.where(mine, moved, F32(0.0))
-    five_ref[...] = five32[...].astype(BF16)
+    five = jnp.concatenate([five, jnp.zeros((4, 128), F32)], axis=0).astype(BF16)
+    five_ref[...] = five
     for msg in (up_msg, down_msg):
-        msg[Y_SIX:Y_FIVE, :] = six
-        msg[Y_FIVE:Y_ROWS, :] = five_ref[...]
-
-
-def prepare(place, leaf, positions, masses, counts, up_operator):
+        msg[Y_FIVE:Y_ROWS, :] = five
+    for copy in copies[5:]:
+        copy.wait()
+
+
+def prepare(leaf, positions, masses, counts, up_operator, down_operator, far_operator):
+    inputs = (leaf, positions, masses, counts, up_operator, down_operator, far_operator)
     return kernel_call(
         prep_kernel,
         (
             shape((8 * GROUP, 128), BF16),
             shape((Y_ROWS, 128), BF16),
             shape((Y_ROWS, 128), BF16),
-            shape((80, 128), BF16),
+            shape((X_ROWS, 128), BF16),
+            shape((X_ROWS, 128), BF16),
+            shape((GROUP, 128), BF16),
+            shape((40, 128), BF16),
             shape((256, 128), F32),
+            shape((768, 128), F32),
+            shape((32, 128), jnp.int32),
+            shape(up_operator.shape, BF16),
+            shape(down_operator.shape, BF16),
+            shape(far_operator.shape, BF16),
         ),
-        (place, leaf, positions, masses, counts, up_operator),
+        [pltpu.with_memory_space_constraint(value, pltpu.MemorySpace.HBM) for value in inputs],
         (
+            pltpu.VMEM((1152, 128), BF16),
+            pltpu.VMEM((256, 128), F32),
             pltpu.VMEM((1152, 128), F32),
             pltpu.VMEM((1152, 128), F32),
             pltpu.VMEM((GROUP, 128), F32),
-            pltpu.VMEM((80, 128), F32),
+            pltpu.VMEM((256, 128), F32),
+            pltpu.SemaphoreType.DMA((7,)),
         ),
-        scalars=1,
-    )
-
-
-def cross_kernel(
-    below, above, two, mine, grid_ref, pos_ref, live_ref, to_low, to_high, near32
-):
-    five = (
-        mine[Y_FIVE:Y_ROWS, :].astype(F32)
-        + below[Y_FIVE:Y_ROWS, :].astype(F32)
-        + above[Y_FIVE:Y_ROWS, :].astype(F32)
-        + two[...].astype(F32)
-    ).astype(BF16)
-    low_half = iota((GROUP, 128), 1) < 64
-    halo = jnp.where(
-        low_half, above[Y_SIX:Y_FIVE, :].astype(F32), below[Y_SIX:Y_FIVE, :].astype(F32)
-    ).astype(BF16)
+        space=HBM,
+    )
+
+
+def halo_six(below, above):
+    upper, lower = above[Y_SIX:Y_FIVE, :].astype(F32), below[Y_SIX:Y_FIVE, :].astype(F32)
+    left = iota((72, 128), 1) < 64
+    return jnp.concatenate(
+        [
+            jnp.where(left, upper, lane_roll(lower, 64)),
+            jnp.where(left, lane_roll(upper, 64), lower),
+        ],
+        axis=0,
+    )
+
+
+def cross_kernel(place, below, above, two, own, to_low, to_high, five32):
+    lane = iota((COEF, 128), 1) // 32
+    five32[...] = jnp.zeros_like(five32)
+    for shift, ref, first in ((0, own, 0), (3, below, Y_FIVE), (1, above, Y_FIVE), (2, two, 0)):
+        at = lax.rem(place[1] + shift, 4)
+        value = ref[first : first + 40, :].astype(F32)
+        for y in range(2):
+            moved = pltpu.roll(value, lax.rem(32 * at + 96 * y, 128), 1)[0:COEF]
+            rows = slice(y * COEF, (y + 1) * COEF)
+            five32[rows, :] = jnp.where(lane == at, moved, five32[rows, :])
+    five = five32[...].astype(BF16)
+    halo = halo_six(below, above).astype(BF16)
     for msg, x, xp in ((to_low, 0, 0), (to_high, 3, 1)):
-        for slot in range(8):
-            for axis in range(3):
-                start = (axis * 8 + slot) * 32 + x * 8
-                near32[pl.ds(axis * 8 + slot, 8, stride=32), :] = pos_ref[start : start + 8, :]
-            start = slot * 32 + x * 8
-            near32[pl.ds(24 + slot, 8, stride=32), :] = live_ref[start : start + 8, :]
-        high, low = parts(near32[...])
-        for half, value in ((0, high), (1, low)):
-            base = half * X_NEAR
-            msg[base + 32 : base + 288, :] = value
-            source = half * 128 + x * 32
-            msg[base : base + 32, :] = below[source : source + 32, :]
-            msg[base + 288 : base + 320, :] = above[source : source + 32, :]
-        source = Y_LEAF + xp * GROUP
-        msg[X_LEAF : X_LEAF + GROUP, :] = below[source : source + GROUP, :]
-        msg[X_LEAF + GROUP : X_LEAF + 5 * GROUP, :] = grid_ref[
-            xp * 4 * GROUP : (xp + 1) * 4 * GROUP, :
-        ]
-        msg[X_LEAF + 5 * GROUP : X_SIX, :] = above[source : source + GROUP, :]
-        msg[X_SIX:X_HALO, :] = mine[Y_SIX:Y_FIVE, :]
-        msg[X_HALO:X_FIVE, :] = halo
-        msg[X_FIVE:X_ROWS, :] = five
-
-
-def cross(below, above, two, mine, grid, positions, live):
+        for side, ref in enumerate((below, above)):
+            for half in range(2):
+                source = half * 128 + x * 32
+                first = side * 64 + half * 32
+                msg[first : first + 32, :] = ref[source : source + 32, :]
+            source, first = Y_LEAF + xp * GROUP, C_LEAF + side * GROUP
+            msg[first : first + GROUP, :] = ref[source : source + GROUP, :]
+        msg[C_SIX:C_FIVE, :] = halo
+        msg[C_FIVE:C_ROWS, :] = five
+
+
+def cross(*inputs):
     return kernel_call(
         cross_kernel,
-        (shape((X_ROWS, 128), BF16), shape((X_ROWS, 128), BF16)),
-        (below, above, two, mine, grid, positions, live),
-        (pltpu.VMEM((256, 128), F32),),
+        (shape((C_ROWS, 128), BF16), shape((C_ROWS, 128), BF16)),
+        inputs,
+        (pltpu.VMEM((80, 128), F32),),
+        scalars=1,
     )
 
 
@@ -302,64 +343,28 @@
     )[0]
 
 
-def edge_kernel(
-    inner_ref, pos_ref, live_ref, count_ref, below, above, low, high, out_ref,
-    sides, near32, shifted, sums,
-):
+def gather(shifted, goals, totals):
+    def body(index, carry):
+        carry = list(carry)
+        for slot in range(8):
+            source = [shifted[index, k, slot] for k in range(4)]
+            for goal in range(8):
+                carry[goal] = carry[goal] + source[3] * inverse_distance(goals[goal], source)
+        return tuple(carry)
+
+    return lax.fori_loop(0, 9, body, tuple(totals))
+
+
+def rows_kernel(inner_ref, pos_ref, below, above, out_ref, near32, shifted):
     row = iota((8, 128), 0)
-    for index, msg in enumerate((low, high)):
-        sides[index] = msg[0:X_NEAR, :].astype(F32) + msg[X_NEAR : 2 * X_NEAR, :].astype(F32)
     for index, msg in enumerate((below, above)):
         near32[index] = msg[0:128, :].astype(F32) + msg[128:256, :].astype(F32)
-
-    def fill_face(index, carry):
-        for slot in range(8):
-            for step_y in range(3):
-                values = [
-                    sides[index, pl.ds(step_y * 32 + 8 * k + slot, 8, stride=32), :]
-                    for k in range(4)
-                ]
-                values[0] = values[0] + (2 * index - 1).astype(F32)
-                values[1] = values[1] + F32(step_y - 1)
-                for step_z in range(3):
-                    moved = [lane_roll(value, 1 - step_z) for value in values]
-                    moved[2] = moved[2] + F32(step_z - 1)
-                    for k in range(4):
-                        shifted[step_y * 3 + step_z, k, slot] = moved[k]
-        return carry
-
-    def gather(goals, totals):
-        def body(index, carry):
-            carry = list(carry)
-            for slot in range(8):
-                source = [shifted[index, k, slot] for k in range(4)]
-                for goal in range(8):
-                    carry[goal] = carry[goal] + source[3] * inverse_distance(goals[goal], source)
-            return tuple(carry)
-
-        return lax.fori_loop(0, 9, body, tuple(totals))
-
-    def face(index, carry):
-        fill_face(index, 0)
-        x = 3 * index
-        goals = [[pos_ref[axis, slot, x] for axis in range(3)] for slot in range(8)]
-        totals = gather(goals, [inner_ref[slot, x] for slot in range(8)])
-        for slot in range(8):
-            sums[slot, x] = totals[slot]
-        return carry
-
-    lax.fori_loop(0, 2, face, 0)
-    for x in (1, 2):
-        for slot in range(8):
-            sums[slot, x] = inner_ref[slot, x]
-    upper = row >= 4
-    turn = jnp.where(upper, F32(1.0), F32(-1.0))
+    turn = jnp.where(row >= 4, F32(1.0), F32(-1.0))
+    none = jnp.zeros((1, 128), F32)
     for slot in range(8):
         for k in range(4):
-            r = 8 * k + slot
-            none = jnp.zeros((1, 128), F32)
             source = [
-                [none] + [near32[side, pl.ds(x * 32 + r, 1), :] for x in range(4)] + [none]
+                [none] + [near32[side, pl.ds(x * 32 + 8 * k + slot, 1), :] for x in range(4)] + [none]
                 for side in range(2)
             ]
             for step_x in range(3):
@@ -384,23 +389,67 @@
         )
 
     goals = [[edge_rows(pos_ref, (axis, slot)) for axis in range(3)] for slot in range(8)]
-    totals = gather(goals, [jnp.zeros((8, 128), F32) for slot in range(8)])
+    totals = gather(shifted, goals, [jnp.zeros((8, 128), F32) for slot in range(8)])
+    out_ref[...] = inner_ref[...]
     for slot in range(8):
         for x in range(4):
-            sums[slot, x, pl.ds(0, 1)] = sums[slot, x, pl.ds(0, 1)] + totals[slot][x : x + 1]
-            sums[slot, x, pl.ds(7, 1)] = sums[slot, x, pl.ds(7, 1)] + totals[slot][x + 4 : x + 5]
+            for y, r in ((0, x), (7, x + 4)):
+                out_ref[slot, x, pl.ds(y, 1)] = out_ref[slot, x, pl.ds(y, 1)] + totals[slot][r : r + 1]
+
+
+def faces_kernel(
+    inner_ref, pos_ref, count_ref, low, high, low_corner, high_corner, out_ref, sides, shifted, sums
+):
+    for index, (msg, corner) in enumerate(((low, low_corner), (high, high_corner))):
+        sides[index, 0:32, :] = corner[0:32, :].astype(F32) + corner[32:64, :].astype(F32)
+        sides[index, 32:288, :] = msg[0:256, :].astype(F32) + msg[256:512, :].astype(F32)
+        sides[index, 288:320, :] = corner[64:96, :].astype(F32) + corner[96:128, :].astype(F32)
+
+    def face(index, carry):
+        for slot in range(8):
+            for step_y in range(3):
+                values = [
+                    sides[index, pl.ds(step_y * 32 + 8 * k + slot, 8, stride=32), :]
+                    for k in range(4)
+                ]
+                values[0] = values[0] + (2 * index - 1).astype(F32)
+                values[1] = values[1] + F32(step_y - 1)
+                for step_z in range(3):
+                    moved = [lane_roll(value, 1 - step_z) for value in values]
+                    moved[2] = moved[2] + F32(step_z - 1)
+                    for k in range(4):
+                        shifted[step_y * 3 + step_z, k, slot] = moved[k]
+        x = 3 * index
+        goals = [[pos_ref[axis, slot, x] for axis in range(3)] for slot in range(8)]
+        totals = gather(shifted, goals, [inner_ref[slot, x] for slot in range(8)])
+        for slot in range(8):
+            sums[slot, x] = totals[slot]
+        return carry
+
+    lax.fori_loop(0, 2, face, 0)
+    for x in (1, 2):
+        for slot in range(8):
+            sums[slot, x] = inner_ref[slot, x]
     for slot in range(8):
         out_ref[slot] = jnp.where(count_ref[...] > slot, -sums[slot] / 8, F32(0.0))
 
 
-def edge_pairs(inner, positions, live, counts, below, above, low, high):
+def row_pairs(*inputs):
     return kernel_call(
-        edge_kernel,
+        rows_kernel,
         (shape((8, 4, 8, 128), F32),),
-        (inner, positions, live, counts, below, above, low, high),
+        inputs,
+        (pltpu.VMEM((2, 128, 128), F32), pltpu.VMEM((9, 4, 8, 8, 128), F32)),
+    )[0]
+
+
+def face_pairs(*inputs):
+    return kernel_call(
+        faces_kernel,
+        (shape((8, 4, 8, 128), F32),),
+        inputs,
         (
-            pltpu.VMEM((2, X_NEAR, 128), F32),
-            pltpu.VMEM((2, 128, 128), F32),
+            pltpu.VMEM((2, 320, 128), F32),
             pltpu.VMEM((9, 4, 8, 8, 128), F32),
             pltpu.VMEM((8, 4, 8, 128), F32),
         ),
@@ -509,21 +558,51 @@
     return jnp.where(inside, lane_roll(value, -step), wrapped)
 
 
-def far_kernel(
-    place, matrix, grid_ref, mine, below, above, low, high, near_three, up_three, down_three,
-    up_ref, down_ref, out_ref, cells, fives, fours, three32, products, coarse, down32, downs, expand,
-    lifted,
+def leaf_kernel(
+    matrix, grid_ref, below, above, low, high, low_corner, high_corner, out_ref, cells, products
 ):
-    gx, gy = place[0], place[1]
-    row, col = iota((128, 128), 0), iota((128, 128), 1)
-    cells[:, 0:128] = low[X_LEAF:X_SIX, :]
-    cells[:, 384:512] = high[X_LEAF:X_SIX, :]
+    for first, msg, corner in ((0, low, low_corner), (384, high, high_corner)):
+        lanes = slice(first, first + 128)
+        cells[0:GROUP, lanes] = corner[C_LEAF : C_LEAF + GROUP, :]
+        cells[GROUP : 5 * GROUP, lanes] = msg[X_LEAF:X_SIX, :]
+        cells[5 * GROUP : 6 * GROUP, lanes] = corner[C_LEAF + GROUP : C_SIX, :]
     for xp in range(2):
         lanes = slice(128 + 128 * xp, 256 + 128 * xp)
         source = Y_LEAF + xp * GROUP
         cells[0:GROUP, lanes] = below[source : source + GROUP, :]
         cells[GROUP : 5 * GROUP, lanes] = grid_ref[xp * 4 * GROUP : (xp + 1) * 4 * GROUP, :]
         cells[5 * GROUP : 6 * GROUP, lanes] = above[source : source + GROUP, :]
+    for parent in range(4):
+        rows = slice(parent * GROUP, (parent + 3) * GROUP)
+        total = None
+        for shift_x in range(3):
+            lanes = slice(shift_x * 128, shift_x * 128 + 256)
+            term = dot(matrix[shift_x], cells[rows, lanes])
+            total = term if total is None else total + term
+        products[...] = total
+        for xp in range(2):
+            for bits in range(4):
+                value = z_sum(products, bits, slice(xp * 128, xp * 128 + 128), leaf_roll)
+                x, y = 2 * xp + bits // 2, 2 * parent + bits % 2
+                out_ref[pl.ds(x * 8 + y, COEF, stride=32), :] = value
+
+
+def leaf_level(*inputs):
+    return kernel_call(
+        leaf_kernel,
+        (shape((1152, 128), F32),),
+        inputs,
+        (pltpu.VMEM((6 * GROUP, 512), BF16), pltpu.VMEM((1024, 256), F32)),
+    )[0]
+
+
+def levels_kernel(
+    place, matrix, leaf_ref, six_ref, below, above, low, high, low_corner, high_corner,
+    near_three, up_three, down_three, up_ref, down_ref, out_ref,
+    fives, fours, three32, products, coarse, down32, downs, expand, lifted,
+):
+    gx, gy = place[0], place[1]
+    row, col = iota((128, 128), 0), iota((128, 128), 1)
     size = lax.axis_size("gx")
     for shift, msg, first in (
         (-1, near_three, 0), (0, near_three, 80), (1, near_three, 160),
@@ -554,20 +633,14 @@
         three32[x * 2 * COEF : x * 2 * COEF + COEF, :] = value
         three32[x * 2 * COEF + COEF : (x + 1) * 2 * COEF, :] = lane_roll(value, 120)
     three = dot(three32[...].astype(BF16), one_hot((row == col - 48) & (col >= 48) & (col < 56)))
-    halo = jnp.where(
-        iota((GROUP, 128), 1) < 64,
-        above[Y_SIX:Y_FIVE, :].astype(F32),
-        below[Y_SIX:Y_FIVE, :].astype(F32),
-    )
     wide_low = iota((GROUP, 128), 1) < 64
     total = None
     for shift_x in range(3):
         if shift_x == 1:
-            own, other = mine[Y_SIX:Y_FIVE, :].astype(F32), halo
+            own, other = six_ref[...].astype(F32), halo_six(below, above)
         else:
-            msg = low if shift_x == 0 else high
-            own = msg[X_SIX:X_HALO, :].astype(F32)
-            other = msg[X_HALO:X_FIVE, :].astype(F32)
+            own = (low if shift_x == 0 else high)[X_SIX:X_ROWS, :].astype(F32)
+            other = (low_corner if shift_x == 0 else high_corner)[C_SIX:C_FIVE, :].astype(F32)
         six = [
             lane_roll(jnp.where(wide_low, own, other), 64),
             own,
@@ -638,30 +711,19 @@
                 at = ((bits // 2) * 4 + 2 * y + bits % 2) * 128
                 expand[k, :, at : at + 128] = part
     lift([expand[k] for k in range(2)], slice(0, 1024))
-    for parent in range(4):
-        rows = slice(parent * GROUP, (parent + 3) * GROUP)
-        total = None
-        for shift_x in range(3):
-            lanes = slice(shift_x * 128, shift_x * 128 + 256)
-            term = dot(matrix[shift_x], cells[rows, lanes])
-            total = term if total is None else total + term
-        products[...] = total
-        for xp in range(2):
-            at = (xp * 4 + parent) * 128
-            for bits in range(4):
-                value = z_sum(products, bits, slice(xp * 128, xp * 128 + 128), leaf_roll)
-                value = value + child(bits, slice(at, at + 128))
-                x, y = 2 * xp + bits // 2, 2 * parent + bits % 2
-                out_ref[pl.ds(x * 8 + y, COEF, stride=32), :] = value
+    for x in range(4):
+        for y in range(8):
+            at = ((x // 2) * 4 + y // 2) * 128
+            rows = pl.ds(x * 8 + y, COEF, stride=32)
+            out_ref[rows, :] = leaf_ref[rows, :] + child(2 * (x % 2) + y % 2, slice(at, at + 128))
 
 
 def all_levels(*inputs):
     return kernel_call(
-        far_kernel,
+        levels_kernel,
         (shape((1152, 128), F32),),
         inputs,
         (
-            pltpu.VMEM((6 * GROUP, 512), BF16),
             pltpu.VMEM((576, 128), F32),
             pltpu.VMEM((2 * GROUP, 128), F32),
             pltpu.VMEM((GROUP, 128), F32),
@@ -690,32 +752,34 @@
     leaf_multipoles, positions, masses, counts, up_operator, far_operator, down_operator
 ):
     place = jnp.stack([lax.axis_index("gx"), lax.axis_index("gy")]).astype(jnp.int32)
-    flat_positions = positions.reshape(768, 128)
-    flat_counts = counts.reshape(32, 128)
-    grid, up_msg, down_msg, five, live = prepare(
-        place, leaf_multipoles.reshape(1152, 128), flat_positions, masses.reshape(256, 128),
-        flat_counts, up_operator,
-    )
-    below = moved(up_msg, 0, 1)
-    above = moved(down_msg, 0, -1)
-    two = moved(five, 0, 2)
-    live_cells = live.reshape(8, 4, 8, 128)
-    matrix = far_matrix(far_operator)
-    below, above, two, matrix = lax.optimization_barrier((below, above, two, matrix))
-    to_low, to_high = cross(below, above, two, up_msg, grid, flat_positions, live)
-    low = moved(to_high, 1, 0)
-    high = moved(to_low, -1, 0)
-    inner = inner_pairs(positions, live_cells)
-    low, high, inner = lax.optimization_barrier((low, high, inner))
-    own_five = to_low[X_FIVE:]
-    three = jnp.concatenate([low[X_FIVE:], own_five, high[X_FIVE:]], axis=0)
-    up_three = moved(three, 3, 0)
-    down_three = moved(three, -3, 0)
-    potential = edge_pairs(inner, positions, live_cells, counts, below, above, low, high)
-    up_three, down_three, potential = lax.optimization_barrier((up_three, down_three, potential))
+    (
+        grid, up_msg, down_msg, low_msg, high_msg, six, five, live,
+        positions, counts, up_operator, down_operator, far_operator,
+    ) = prepare(
+        leaf_multipoles.reshape(1152, 128), positions.reshape(768, 128), masses.reshape(256, 128),
+        counts.reshape(32, 128), up_operator.T, down_operator, far_operator,
+    )
+    positions = positions.reshape(3, 8, 4, 8, 128)
+    counts = counts.reshape(4, 8, 128)
+    below, above, two = moved(up_msg, 0, 1), moved(down_msg, 0, -1), moved(five, 0, 2)
+    low, high = moved(high_msg, 1, 0), moved(low_msg, -1, 0)
+    inner = inner_pairs(positions, live.reshape(8, 4, 8, 128))
+    below, above, two, inner = lax.optimization_barrier((below, above, two, inner))
+    to_low, to_high = cross(place, below, above, two, five)
+    low_corner, high_corner = moved(to_high, 1, 0), moved(to_low, -1, 0)
+    matrix = far_matrix(lax.optimization_barrier((far_operator, inner))[0])
+    inner = row_pairs(inner, positions, below, above)
+    low, high, low_corner, high_corner, inner, matrix = lax.optimization_barrier(
+        (low, high, low_corner, high_corner, inner, matrix)
+    )
+    three = jnp.concatenate([low_corner[C_FIVE:], to_low[C_FIVE:], high_corner[C_FIVE:]], axis=0)
+    up_three, down_three = moved(three, 3, 0), moved(three, -3, 0)
+    potential = face_pairs(inner, positions, counts, low, high, low_corner, high_corner)
+    leaf = leaf_level(matrix, grid, below, above, low, high, low_corner, high_corner)
+    up_three, down_three, leaf = lax.optimization_barrier((up_three, down_three, leaf))
     expansion = all_levels(
-        place, matrix, grid, up_msg, below, above, low, high, three, up_three, down_three,
-        up_operator, down_operator,
+        place, matrix, leaf, six, below, above, low, high, low_corner, high_corner,
+        three, up_three, down_three, up_operator, down_operator,
     )
     return expansion.reshape(36, 4, 8, 128), potential
 

time: 53.2 us -> 44.3 us (0.83)
  waiting for transfers between devices: 11.4 us -> 3.62 us
  local copies, waits for them, and re-layouts: 5.66 us -> 0.01 us
  Pallas kernels: 25.7 us -> 28.5 us
  starting transfers between devices: 9.27 us -> 11.2 us
    ppermute x7 -> x9, waiting for transfers between devices: 11.4 us -> 3.62 us  [moved(): return lax.ppermute(value, ('gx', 'gy'), table)]
    unnamed x15 -> x0, local copies, waits for them, and re-layouts: 5.65 us -> none
    pallas_call x6 -> x8, Pallas kernels: 25.7 us -> 28.5 us  [kernel_call(): pl.pallas_call(body, out_shape=outs, in_specs=[SMEM] * scalars + [space]...]
    ppermute x7 -> x9, starting transfers between devices: 9.27 us -> 11.2 us  [moved(): return lax.ppermute(value, ('gx', 'gy'), table)]
  transfers between devices with their start and end apart: 7 -> 9, of which waited for: 4 -> 1; matrix products, arithmetic and copies ran while one was open for 0% -> 0% of each run, Pallas kernels for 24% -> 40%
where the time goes in v1:
time: 44.3 us; the launch traced here: 44.2 us
  Pallas kernels  28.5 us (64%)
  starting transfers between devices  11.2 us (25%)
  waiting for transfers between devices  3.62 us (8%)
  between operations  0.76 us (2%)
    pallas_call x8, Pallas kernels, kernel_call(): pl.pallas_call(body, out_shape=outs, in_specs=[SMEM] * scalars + [space]...  28.5 us
    ppermute x9, starting transfers between devices, moved(): return lax.ppermute(value, ('gx', 'gy'), table)  11.2 us
    ppermute x9, waiting for transfers between devices, moved(): return lax.ppermute(value, ('gx', 'gy'), table)  3.62 us
  transfers between devices with their start and end apart: 9, of which 1 were waited for; matrix products, arithmetic and copies ran while one was open for 0% of the time, Pallas kernels for 40%

profile of v1, /device:TPU:1, one launch (start us, length us, event | category | flops | bytes accessed | tf_op | source)
XLA Modules:
  0.0 44.2 jit_solution(9112256882374069506)
XLA Ops:
  0.6 3.4 %shard_map.86 = (bf16[1152,128]{1,0:T(8,128)(2,1)S(1)}, bf16[656,128]{1,0:T(8,128)(2,1)}, bf16[656,128]{1,0:T(8,128)(2,1)}, bf16[1232,128]{1,0:T(8,128)(2,1)S(1)...) custom-call(bf16[1152,128]{1,0:T(8,128)(2,1)} %bitcast.18, ...), custom_call_target="tpu_custom_call" | custom-call | tf_op jit(solution)/shard_map/pallas_call | solution.py:39
  4.0 2.2 %collective-permute-start.2 = (bf16[656,128]{1,0:T(8,128)(2,1)}, bf16[656,128]{1,0:T(8,128)(2,1)S(1)}, u32[]{:S(2)}, u32[]{:S(2)}) collective-permute-start(bf16[656,128]{1,0:T(8,128)(2,1)} %get-tuple-element.33), channel_id=1, source_target_pairs={{0,1},{1,2},{2,3},{3,0},{4,5},{5,6},{6,7},{7,4},{8,9},{9,10},{10,1... | collective-permute-start | bytes 503816 | tf_op jit(solution)/shard_map/ppermute | solution.py:748
  6.2 2.1 %collective-permute-start.3 = (bf16[656,128]{1,0:T(8,128)(2,1)}, bf16[656,128]{1,0:T(8,128)(2,1)S(1)}, u32[]{:S(2)}, u32[]{:S(2)}) collective-permute-start(bf16[656,128]{1,0:T(8,128)(2,1)} %get-tuple-element.34), channel_id=1, source_target_pairs={{0,3},{1,0},{2,1},{3,2},{4,7},{5,4},{6,5},{7,6},{8,11},{9,8},{10,9... | collective-permute-start | bytes 503816 | tf_op jit(solution)/shard_map/ppermute | solution.py:748
  8.3 2.2 %collective-permute-start = (bf16[1232,128]{1,0:T(8,128)(2,1)S(1)}, bf16[1232,128]{1,0:T(8,128)(2,1)S(1)}, u32[]{:S(2)}, u32[]{:S(2)}) collective-permute-start(bf16[1232,128]{1,0:T(8,128)(2,1)S(1)} %get-tuple-element.31), channel_id=1, source_target_pairs={{0,4},{1,5},{2,6},{3,7},{4,8},{5,9},{6,10},{7,11},{8,12},{9,13},{1... | collective-permute-start | bytes 946184 | tf_op jit(solution)/shard_map/ppermute | solution.py:748
  10.5 0.0 collective-permute-start.1
  10.5 0.5 %collective-permute-start.4 = (bf16[40,128]{1,0:T(8,128)(2,1)S(1)}, bf16[40,128]{1,0:T(8,128)(2,1)S(1)}, u32[]{:S(2)}, u32[]{:S(2)}) collective-permute-start(bf16[40,128]{1,0:T(8,128)(2,1)S(1)} %get-tuple-element.35.own), channel_id=1, source_target_pairs={{0,2},{1,3},{2,0},{3,1},{4,6},{5,7},{6,4},{7,5},{8,10},{9,11},{10,... | collective-permute-start | bytes 30728 | tf_op jit(solution)/shard_map/ppermute | solution.py:748
  11.0 0.1 pad_add_fusion.place
  11.1 6.7 %shard_map.87.inner_ref = f32[8,4,8,128]{3,2,1,0:T(8,128)S(1)} custom-call(f32[3,8,4,8,128]{4,3,2,1,0:T(8,128)S(1)} %bitcast.11, f32[8,4,8,128]{3,2,1,0:T(8,128)S(1)} %bitcast.14), custom_call_target="tpu_custom_call" | custom-call | tf_op jit(solution)/shard_map/pallas_call | solution.py:39
  17.8 0.0 collective-permute-done.4.two
  17.8 0.0 collective-permute-done.2.below
  17.8 0.0 collective-permute-done.3.above
  17.8 0.7 %shard_map.88 = (bf16[640,128]{1,0:T(8,128)(2,1)S(1)}, bf16[640,128]{1,0:T(8,128)(2,1)S(1)}) custom-call(s32[2]{0:T(128)S(1)} %pad_add_fusion.place, bf16[656,128]{1,0:T(8,128)(2,1)S(1)} %collective-permute-done.2.below, bf16[656,128]{1,0:T(8,128)(2,1)S(1)} %collective-permute-done.3.above, bf16[40,128]{1,0:T(8,128)(2,1)S(1)} %collective-permute-done.4.two, ...), custom_call_target="tpu_custom_call" | custom-call | tf_op jit(solution)/shard_map/pallas_call | solution.py:39
  18.5 2.1 %collective-permute-start.5 = (bf16[640,128]{1,0:T(8,128)(2,1)S(1)}, bf16[640,128]{1,0:T(8,128)(2,1)S(1)}, u32[]{:S(2)}, u32[]{:S(2)}) collective-permute-start(bf16[640,128]{1,0:T(8,128)(2,1)S(1)} %get-tuple-element.41), channel_id=1, source_target_pairs={{0,4},{1,5},{2,6},{3,7},{4,8},{5,9},{6,10},{7,11},{8,12},{9,13},{1... | collective-permute-start | bytes 491528 | tf_op jit(solution)/shard_map/ppermute | solution.py:748
  20.6 1.3 %shard_map.89.inner_ref = f32[8,4,8,128]{3,2,1,0:T(8,128)S(1)} custom-call(f32[8,4,8,128]{3,2,1,0:T(8,128)S(1)} %shard_map.87.inner_ref, f32[3,8,4,8,128]{4,3,2,1,0:T(8,128)S(1)} %bitcast.12, bf16[656,128]{1,0:T(8,128)(2,1)S(1)} %collective-permute-done.2.below, bf16[656,128]{1,0:T(8,128)(2,1)S(1)} %collective-permute-done.3.above), custom_call_target="tpu_custom_call" | custom-call | tf_op jit(solution)/shard_map/pallas_call | solution.py:39
  21.9 1.5 %shard_map.90.matrix = bf16[3,1024,432]{2,1,0:T(8,128)(2,1)S(1)} custom-call(bf16[36,11376]{1,0:T(8,128)(2,1)S(1)} %get-tuple-element.45.far_ref), custom_call_target="tpu_custom_call" | custom-call | tf_op jit(solution)/shard_map/pallas_call | solution.py:39
  23.4 0.0 collective-permute-done.low
  23.4 0.0 collective-permute-done.1.high
  23.4 3.6 %collective-permute-done.6.high_corner = bf16[640,128]{1,0:T(8,128)(2,1)S(1)} collective-permute-done((bf16[640,128]{1,0:T(8,128)(2,1)S(1)}, bf16[640,128]{1,0:T(8,128)(2,1)S(1)}, u32[]{:S(2)}, u32[]{:S(2)}) %collective-permute-start.6) | collective-permute-done | bytes 163872 | tf_op jit(solution)/shard_map/ppermute | solution.py:748
  27.0 0.1 collective-permute-start.8
  27.1 2.1 %collective-permute-start.7 = (bf16[240,128]{1,0:T(8,128)(2,1)S(1)}, bf16[240,128]{1,0:T(8,128)(2,1)S(1)}, u32[]{:S(2)}, u32[]{:S(2)}) collective-permute-start(bf16[240,128]{1,0:T(8,128)(2,1)S(1)} %pad_maximum_fusion.near_three), channel_id=1, source_target_pairs={{0,12},{1,13},{2,14},{3,15},{4,16},{5,17},{6,18},{7,19},{8,20},{9,... | collective-permute-start | bytes 184328 | tf_op jit(solution)/shard_map/ppermute | solution.py:748
  29.2 3.3 %shard_map.93 = f32[8,4,8,128]{3,2,1,0:T(8,128)} custom-call(f32[8,4,8,128]{3,2,1,0:T(8,128)S(1)} %shard_map.89.inner_ref, f32[3,8,4,8,128]{4,3,2,1,0:T(8,128)S(1)} %bitcast.13, s32[4,8,128]{2,1,0:T(8,128)S(1)} %bitcast.15, bf16[1232,128]{1,0:T(8,128)(2,1)S(1)} %collective-permute-done.low, bf16[1232,128]{1,0:T(8,128)(2,1)S(1)} %collective-permute-done.1.high, ...), custom_call_target="tpu_custom_call" | custom-call | tf_op jit(solution)/shard_map/pallas_call | solution.py:39
  32.5 4.2 %shard_map.91.leaf_ref = f32[1152,128]{1,0:T(8,128)S(1)} custom-call(bf16[3,1024,432]{2,1,0:T(8,128)(2,1)S(1)} %shard_map.90.matrix, bf16[1152,128]{1,0:T(8,128)(2,1)S(1)} %get-tuple-element.49.grid_ref, bf16[656,128]{1,0:T(8,128)(2,1)S(1)} %collective-permute-done.2.below, bf16[656,128]{1,0:T(8,128)(2,1)S(1)} %collective-permute-done.3.above, ...), custom_call_target="tpu_custom_call" | custom-call | tf_op jit(solution)/shard_map/pallas_call | solution.py:39
  36.7 0.0 collective-permute-done.8.down_three
  36.7 7.5 %shard_map.92 = f32[1152,128]{1,0:T(8,128)} custom-call(s32[2]{0:T(128)S(1)} %pad_add_fusion.place, bf16[3,1024,432]{2,1,0:T(8,128)(2,1)S(1)} %shard_map.90.matrix, f32[1152,128]{1,0:T(8,128)S(1)} %shard_map.91.leaf_ref, bf16[144,128]{1,0:T(8,128)(2,1)S(1)} %get-tuple-element.53.six_ref, bf16[656,128]{1,0:T(8,128)(2,1)S(1)} %collective-permute-done.2.below, ...), custom_call_target="tpu_custom_call" | custom-call | tf_op jit(solution)/shard_map/pallas_call | solution.py:39
  (7 shorter events, 0.0 us)
Async XLA Ops:
  4.0 13.8 %collective-permute-start.2 = (bf16[656,128]{1,0:T(8,128)(2,1)}, bf16[656,128]{1,0:T(8,128)(2,1)S(1)}, u32[]{:S(2)}, u32[]{:S(2)}) collective-permute-start(bf16[656,128]{1,0:T(8,128)(2,1)} %get-tuple-element.33), channel_id=1, source_target_pairs={{0,1},{1,2},{2,3},{3,0},{4,5},{5,6},{6,7},{7,4},{8,9},{9,10},{10,1... | collective-permute-start | bytes 503816 | tf_op jit(solution)/shard_map/ppermute | solution.py:748
  6.2 11.6 %collective-permute-start.3 = (bf16[656,128]{1,0:T(8,128)(2,1)}, bf16[656,128]{1,0:T(8,128)(2,1)S(1)}, u32[]{:S(2)}, u32[]{:S(2)}) collective-permute-start(bf16[656,128]{1,0:T(8,128)(2,1)} %get-tuple-element.34), channel_id=1, source_target_pairs={{0,3},{1,0},{2,1},{3,2},{4,7},{5,4},{6,5},{7,6},{8,11},{9,8},{10,9... | collective-permute-start | bytes 503816 | tf_op jit(solution)/shard_map/ppermute | solution.py:748
  8.3 15.1 %collective-permute-start = (bf16[1232,128]{1,0:T(8,128)(2,1)S(1)}, bf16[1232,128]{1,0:T(8,128)(2,1)S(1)}, u32[]{:S(2)}, u32[]{:S(2)}) collective-permute-start(bf16[1232,128]{1,0:T(8,128)(2,1)S(1)} %get-tuple-element.31), channel_id=1, source_target_pairs={{0,4},{1,5},{2,6},{3,7},{4,8},{5,9},{6,10},{7,11},{8,12},{9,13},{1... | collective-permute-start | bytes 946184 | tf_op jit(solution)/shard_map/ppermute | solution.py:748
  10.5 12.9 %collective-permute-start.1 = (bf16[1232,128]{1,0:T(8,128)(2,1)S(1)}, bf16[1232,128]{1,0:T(8,128)(2,1)S(1)}, u32[]{:S(2)}, u32[]{:S(2)}) collective-permute-start(bf16[1232,128]{1,0:T(8,128)(2,1)S(1)} %get-tuple-element.32), channel_id=1, source_target_pairs={{0,28},{1,29},{2,30},{3,31},{4,0},{5,1},{6,2},{7,3},{8,4},{9,5},{1... | collective-permute-start | bytes 946184 | tf_op jit(solution)/shard_map/ppermute | solution.py:748
  10.5 7.3 %collective-permute-start.4 = (bf16[40,128]{1,0:T(8,128)(2,1)S(1)}, bf16[40,128]{1,0:T(8,128)(2,1)S(1)}, u32[]{:S(2)}, u32[]{:S(2)}) collective-permute-start(bf16[40,128]{1,0:T(8,128)(2,1)S(1)} %get-tuple-element.35.own), channel_id=1, source_target_pairs={{0,2},{1,3},{2,0},{3,1},{4,6},{5,7},{6,4},{7,5},{8,10},{9,11},{10,... | collective-permute-start | bytes 30728 | tf_op jit(solution)/shard_map/ppermute | solution.py:748
  18.5 4.9 %collective-permute-start.5 = (bf16[640,128]{1,0:T(8,128)(2,1)S(1)}, bf16[640,128]{1,0:T(8,128)(2,1)S(1)}, u32[]{:S(2)}, u32[]{:S(2)}) collective-permute-start(bf16[640,128]{1,0:T(8,128)(2,1)S(1)} %get-tuple-element.41), channel_id=1, source_target_pairs={{0,4},{1,5},{2,6},{3,7},{4,8},{5,9},{6,10},{7,11},{8,12},{9,13},{1... | collective-permute-start | bytes 491528 | tf_op jit(solution)/shard_map/ppermute | solution.py:748
  20.6 6.4 %collective-permute-start.6 = (bf16[640,128]{1,0:T(8,128)(2,1)S(1)}, bf16[640,128]{1,0:T(8,128)(2,1)S(1)}, u32[]{:S(2)}, u32[]{:S(2)}) collective-permute-start(bf16[640,128]{1,0:T(8,128)(2,1)S(1)} %get-tuple-element.42), channel_id=1, source_target_pairs={{0,28},{1,29},{2,30},{3,31},{4,0},{5,1},{6,2},{7,3},{8,4},{9,5},{1... | collective-permute-start | bytes 491528 | tf_op jit(solution)/shard_map/ppermute | solution.py:748
  27.0 9.7 %collective-permute-start.8 = (bf16[240,128]{1,0:T(8,128)(2,1)S(1)}, bf16[240,128]{1,0:T(8,128)(2,1)S(1)}, u32[]{:S(2)}, u32[]{:S(2)}) collective-permute-start(bf16[240,128]{1,0:T(8,128)(2,1)S(1)} %pad_maximum_fusion.near_three), channel_id=1, source_target_pairs={{0,20},{1,21},{2,22},{3,23},{4,24},{5,25},{6,26},{7,27},{8,28},{9,... | collective-permute-start | bytes 184328 | tf_op jit(solution)/shard_map/ppermute | solution.py:748
  27.1 9.6 %collective-permute-start.7 = (bf16[240,128]{1,0:T(8,128)(2,1)S(1)}, bf16[240,128]{1,0:T(8,128)(2,1)S(1)}, u32[]{:S(2)}, u32[]{:S(2)}) collective-permute-start(bf16[240,128]{1,0:T(8,128)(2,1)S(1)} %pad_maximum_fusion.near_three), channel_id=1, source_target_pairs={{0,12},{1,13},{2,14},{3,15},{4,16},{5,17},{6,18},{7,19},{8,20},{9,... | collective-permute-start | bytes 184328 | tf_op jit(solution)/shard_map/ppermute | solution.py:748

commit v2 on v1

--- a/solution.py
+++ b/solution.py
@@ -35,7 +35,7 @@
     return jax.ShapeDtypeStruct(dims, dtype)
 
 
-def kernel_call(body, outs, inputs, scratch=(), scalars=0, space=VMEM, limit=48):
+def kernel_call(body, outs, inputs, scratch=(), scalars=0, space=VMEM, limit=20):
     return pl.pallas_call(
         body,
         out_shape=outs,
@@ -54,6 +54,10 @@
     return lax.dot_general(lhs, rhs, (((1,), (0,)), ((), ())), preferred_element_type=F32)
 
 
+def dot_tn(lhs, rhs):
+    return lax.dot_general(lhs, rhs, (((0,), (0,)), ((), ())), preferred_element_type=F32)
+
+
 def dot_nt(lhs, rhs):
     return lax.dot_general(lhs, rhs, (((1,), (1,)), ((), ())), preferred_element_type=F32)
 
@@ -80,9 +84,9 @@
 
 
 def prep_kernel(
-    leaf_hbm, pos_hbm, mass_hbm, count_hbm, up_hbm, down_hbm, far_hbm,
+    leaf_hbm, pos_hbm, mass_hbm, count_hbm, up_hbm,
     grid_ref, up_msg, down_msg, low_msg, high_msg, six_ref, five_ref, live_ref,
-    pos_ref, count_ref, up_ref, down_ref, far_ref,
+    pos_ref, count_ref, up_ref,
     leaf_ref, mass_ref, m32, x32, six32, near32, sems,
 ):
     copies = [
@@ -90,7 +94,7 @@
         for k, (source, target) in enumerate(
             (
                 (leaf_hbm, leaf_ref), (pos_hbm, pos_ref), (mass_hbm, mass_ref),
-                (count_hbm, count_ref), (up_hbm, up_ref), (down_hbm, down_ref), (far_hbm, far_ref),
+                (count_hbm, count_ref), (up_hbm, up_ref),
             )
         )
     ]
@@ -111,7 +115,7 @@
             ]
     low_msg[X_LEAF:X_SIX, :] = grid_ref[0 : 4 * GROUP, :]
     high_msg[X_LEAF:X_SIX, :] = grid_ref[4 * GROUP : 8 * GROUP, :]
-    for copy in copies[1:5]:
+    for copy in copies[1:]:
         copy.wait()
     count = count_ref[...]
     for slot in range(8):
@@ -165,12 +169,14 @@
     five_ref[...] = five
     for msg in (up_msg, down_msg):
         msg[Y_FIVE:Y_ROWS, :] = five
-    for copy in copies[5:]:
-        copy.wait()
-
-
-def prepare(leaf, positions, masses, counts, up_operator, down_operator, far_operator):
-    inputs = (leaf, positions, masses, counts, up_operator, down_operator, far_operator)
+
+
+def in_hbm(value):
+    return pltpu.with_memory_space_constraint(value, pltpu.MemorySpace.HBM)
+
+
+def prepare(leaf, positions, masses, counts, up_operator):
+    inputs = (leaf, positions, masses, counts, up_operator)
     return kernel_call(
         prep_kernel,
         (
@@ -185,10 +191,8 @@
             shape((768, 128), F32),
             shape((32, 128), jnp.int32),
             shape(up_operator.shape, BF16),
-            shape(down_operator.shape, BF16),
-            shape(far_operator.shape, BF16),
         ),
-        [pltpu.with_memory_space_constraint(value, pltpu.MemorySpace.HBM) for value in inputs],
+        [in_hbm(value) for value in inputs],
         (
             pltpu.VMEM((1152, 128), BF16),
             pltpu.VMEM((256, 128), F32),
@@ -196,7 +200,7 @@
             pltpu.VMEM((1152, 128), F32),
             pltpu.VMEM((GROUP, 128), F32),
             pltpu.VMEM((256, 128), F32),
-            pltpu.SemaphoreType.DMA((7,)),
+            pltpu.SemaphoreType.DMA((5,)),
         ),
         space=HBM,
     )
@@ -256,11 +260,42 @@
     return lax.rsqrt(squared)
 
 
-def inner_kernel(pos_ref, live_ref, out_ref, shifted, sums):
-    row = iota((8, 128), 0)
+def pair_sums(shifted, sums, goals, x, step, totals):
+    step_x, step_y, step_z = step
+    edge = iota((8, 128), 0) == (7 if step_y > 0 else 0)
+    for slot in range(8):
+        source = [shifted[step_z + 1, k, slot, x] for k in range(4)]
+        if step_y:
+            source = [pltpu.roll(value, (-step_y) % 8, 0) for value in source]
+            source[1] = source[1] + F32(step_y)
+            source[3] = jnp.where(edge, F32(0.0), source[3])
+        if step_x:
+            source[0] = source[0] + F32(step_x)
+        back = None
+        for goal in range(8):
+            inverse = inverse_distance(goals[goal], source)
+            totals[goal] = totals[goal] + source[3] * inverse
+            term = goals[goal][3] * inverse
+            back = term if back is None else back + term
+        if step_y:
+            back = pltpu.roll(jnp.where(edge, F32(0.0), back), step_y % 8, 0)
+        sums[step_z + 1, slot, x] = sums[step_z + 1, slot, x] + back
+
+
+def plane_goals(shifted, x):
+    return [[shifted[1, k, slot, x] for k in range(4)] for slot in range(8)]
+
+
+def plane_kernel(pos_ref, live_ref, far_hbm, down_hbm, sums, shifted, far_ref, down_ref, sems):
+    copies = [
+        pltpu.make_async_copy(source, target, sems.at[k])
+        for k, (source, target) in enumerate(((far_hbm, far_ref), (down_hbm, down_ref)))
+    ]
+    for copy in copies:
+        copy.start()
     sums[...] = jnp.zeros_like(sums)
 
-    def fill(x, carry):
+    def plane(x, carry):
         for slot in range(8):
             values = [pos_ref[axis, slot, x] for axis in range(3)] + [live_ref[slot, x]]
             for index, step in enumerate((-1, 0, 1)):
@@ -269,36 +304,7 @@
                     moved[2] = moved[2] + F32(step)
                 for k in range(4):
                     shifted[index, k, slot, x] = moved[k]
-        return carry
-
-    lax.fori_loop(0, 4, fill, 0)
-
-    def targets(x):
-        return [[shifted[1, k, slot, x] for k in range(4)] for slot in range(8)]
-
-    def pairs(goals, x, step, totals):
-        step_x, step_y, step_z = step
-        edge = row == (7 if step_y > 0 else 0)
-        for slot in range(8):
-            source = [shifted[step_z + 1, k, slot, x] for k in range(4)]
-            if step_y:
-                source = [pltpu.roll(value, (-step_y) % 8, 0) for value in source]
-                source[1] = source[1] + F32(step_y)
-                source[3] = jnp.where(edge, F32(0.0), source[3])
-            if step_x:
-                source[0] = source[0] + F32(step_x)
-            back = None
-            for goal in range(8):
-                inverse = inverse_distance(goals[goal], source)
-                totals[goal] = totals[goal] + source[3] * inverse
-                term = goals[goal][3] * inverse
-                back = term if back is None else back + term
-            if step_y:
-                back = pltpu.roll(jnp.where(edge, F32(0.0), back), step_y % 8, 0)
-            sums[step_z + 1, slot, x] = sums[step_z + 1, slot, x] + back
-
-    def plane(x, carry):
-        goals = targets(x)
+        goals = plane_goals(shifted, x)
         totals = [jnp.zeros((8, 128), F32) for slot in range(8)]
         for slot in range(8):
             for goal in range(slot):
@@ -306,22 +312,29 @@
                 totals[goal] = totals[goal] + goals[slot][3] * inverse
                 totals[slot] = totals[slot] + goals[goal][3] * inverse
         for step in ((0, 0, 1), (0, 1, -1), (0, 1, 0), (0, 1, 1)):
-            pairs(goals, x, step, totals)
+            pair_sums(shifted, sums, goals, x, step, totals)
         for slot in range(8):
             sums[1, slot, x] = sums[1, slot, x] + totals[slot]
         return carry
 
+    lax.fori_loop(0, 4, plane, 0)
+    for copy in copies:
+        copy.wait()
+
+
+def step_kernel(sums_ref, shifted, out_ref, sums):
+    sums[...] = sums_ref[...]
+
     def planes(x, carry):
         for step_y in (-1, 0, 1):
-            goals = targets(x)
+            goals = plane_goals(shifted, x)
             totals = [sums[1, slot, x] for slot in range(8)]
             for step_z in (-1, 0, 1):
-                pairs(goals, x + 1, (1, step_y, step_z), totals)
+                pair_sums(shifted, sums, goals, x + 1, (1, step_y, step_z), totals)
             for slot in range(8):
                 sums[1, slot, x] = totals[slot]
         return carry
 
-    lax.fori_loop(0, 4, plane, 0)
     lax.fori_loop(0, 3, planes, 0)
 
     def finish(x, carry):
@@ -334,12 +347,28 @@
     lax.fori_loop(0, 4, finish, 0)
 
 
-def inner_pairs(positions, live):
+def plane_pairs(positions, live, far_operator, down_operator):
+    return pl.pallas_call(
+        plane_kernel,
+        out_shape=(
+            shape((3, 8, 4, 8, 128), F32),
+            shape((3, 4, 8, 4, 8, 128), F32),
+            shape(far_operator.shape, BF16),
+            shape(down_operator.shape, BF16),
+        ),
+        in_specs=[VMEM, VMEM, HBM, HBM],
+        out_specs=[VMEM] * 4,
+        scratch_shapes=[pltpu.SemaphoreType.DMA((2,))],
+        compiler_params=pltpu.CompilerParams(vmem_limit_bytes=16 * 1024 * 1024),
+    )(positions, live, in_hbm(far_operator), in_hbm(down_operator))
+
+
+def step_pairs(*inputs):
     return kernel_call(
-        inner_kernel,
+        step_kernel,
         (shape((8, 4, 8, 128), F32),),
-        (positions, live),
-        (pltpu.VMEM((3, 4, 8, 4, 8, 128), F32), pltpu.VMEM((3, 8, 4, 8, 128), F32)),
+        inputs,
+        (pltpu.VMEM((3, 8, 4, 8, 128), F32),),
     )[0]
 
 
@@ -500,17 +529,13 @@
                         first = shift_y * GROUP + (2 * child_x + child_y) * COEF
                         bits = (2 * bit_x + bit_y) * 256
                         stack[shift_x, first : first + COEF, bits : bits + 256] = block
-    for shift_x in range(3):
-        for k in range(8):
-            out_ref[shift_x, k * 128 : (k + 1) * 128, :] = jnp.transpose(
-                stack[shift_x, :, k * 128 : (k + 1) * 128]
-            ).astype(BF16)
+    out_ref[...] = stack[...].astype(BF16)
 
 
 def far_matrix(far_operator):
     return kernel_call(
         operator_kernel,
-        (shape((3, 1024, 3 * GROUP), BF16),),
+        (shape((3, 3 * GROUP, 1024), BF16),),
         (far_operator,),
         (pltpu.VMEM((COEF, 11520), F32), pltpu.VMEM((3, 3 * GROUP, 1024), F32)),
     )[0]
@@ -558,9 +583,22 @@
     return jnp.where(inside, lane_roll(value, -step), wrapped)
 
 
-def leaf_kernel(
-    matrix, grid_ref, below, above, low, high, low_corner, high_corner, out_ref, cells, products
+def levels_kernel(
+    place, matrix, grid_ref, six_ref, below, above, low, high, low_corner, high_corner,
+    near_three, up_three, down_three, up_ref, down_ref, out_ref,
+    cells, fives, fours, three32, windows, products, coarse, down32, downs, expand, lifted,
 ):
+    gx, gy = place[0], place[1]
+    row, col = iota((128, 128), 0), iota((128, 128), 1)
+
+    def multiply(sources, slot, half):
+        rows = slice(half * 512, half * 512 + 512)
+        total = None
+        for shift_x, source in enumerate(sources):
+            term = dot_tn(matrix[shift_x, :, rows], source)
+            total = term if total is None else total + term
+        products[slot, rows, :] = total
+
     for first, msg, corner in ((0, low, low_corner), (384, high, high_corner)):
         lanes = slice(first, first + 128)
         cells[0:GROUP, lanes] = corner[C_LEAF : C_LEAF + GROUP, :]
@@ -572,38 +610,17 @@
         cells[0:GROUP, lanes] = below[source : source + GROUP, :]
         cells[GROUP : 5 * GROUP, lanes] = grid_ref[xp * 4 * GROUP : (xp + 1) * 4 * GROUP, :]
         cells[5 * GROUP : 6 * GROUP, lanes] = above[source : source + GROUP, :]
-    for parent in range(4):
-        rows = slice(parent * GROUP, (parent + 3) * GROUP)
-        total = None
-        for shift_x in range(3):
-            lanes = slice(shift_x * 128, shift_x * 128 + 256)
-            term = dot(matrix[shift_x], cells[rows, lanes])
-            total = term if total is None else total + term
-        products[...] = total
-        for xp in range(2):
-            for bits in range(4):
-                value = z_sum(products, bits, slice(xp * 128, xp * 128 + 128), leaf_roll)
-                x, y = 2 * xp + bits // 2, 2 * parent + bits % 2
-                out_ref[pl.ds(x * 8 + y, COEF, stride=32), :] = value
-
-
-def leaf_level(*inputs):
-    return kernel_call(
-        leaf_kernel,
-        (shape((1152, 128), F32),),
-        inputs,
-        (pltpu.VMEM((6 * GROUP, 512), BF16), pltpu.VMEM((1024, 256), F32)),
-    )[0]
-
-
-def levels_kernel(
-    place, matrix, leaf_ref, six_ref, below, above, low, high, low_corner, high_corner,
-    near_three, up_three, down_three, up_ref, down_ref, out_ref,
-    fives, fours, three32, products, coarse, down32, downs, expand, lifted,
-):
-    gx, gy = place[0], place[1]
-    row, col = iota((128, 128), 0), iota((128, 128), 1)
-    size = lax.axis_size("gx")
+
+    todo = [(parent, half) for parent in range(4) for half in range(2)]
+
+    def leaf_products(count=1):
+        for parent, half in todo[:count]:
+            rows = slice(parent * GROUP, (parent + 3) * GROUP)
+            lanes = [slice(shift_x * 128, shift_x * 128 + 256) for shift_x in range(3)]
+            multiply([cells[rows, lane] for lane in lanes], parent + 1, half)
+        del todo[:count]
+
+    size = fives.shape[0] // 72
     for shift, msg, first in (
         (-1, near_three, 0), (0, near_three, 80), (1, near_three, 160),
         (-4, up_three, 0), (-3, up_three, 80), (-2, up_three, 160),
@@ -612,6 +629,7 @@
         at = pl.multiple_of(lax.rem(gx + shift + size, size) * 72, 8)
         fives[pl.ds(at, 72), :] = msg[first : first + 72, :].astype(F32)
     even_up, odd_up = up_blocks(up_ref)
+    leaf_products()
 
     def upward(grouped, split):
         children = dot(grouped.astype(BF16), split).astype(BF16)
@@ -627,14 +645,15 @@
         first = (x // 2) * GROUP + (x % 2) * 2 * COEF
         fours[first : first + COEF, :] = value
         fours[first + COEF : first + 2 * COEF, :] = lane_roll(value, 96)
+    leaf_products()
     split_four = one_hot((row == (lane // 8) * 16 + 2 * (lane % 8) + col // 64) & (lane < 16))
     for x in range(2):
         value = upward(fours[x * GROUP : (x + 1) * GROUP, :], split_four)
         three32[x * 2 * COEF : x * 2 * COEF + COEF, :] = value
         three32[x * 2 * COEF + COEF : (x + 1) * 2 * COEF, :] = lane_roll(value, 120)
+    leaf_products()
     three = dot(three32[...].astype(BF16), one_hot((row == col - 48) & (col >= 48) & (col < 56)))
     wide_low = iota((GROUP, 128), 1) < 64
-    total = None
     for shift_x in range(3):
         if shift_x == 1:
             own, other = six_ref[...].astype(F32), halo_six(below, above)
@@ -650,7 +669,6 @@
         five = fives[pl.ds(at, GROUP), :].astype(BF16)
         at = pl.multiple_of(lax.rem(gx // 4 + shift_x + 1, 2) * GROUP, 8)
         four = fours[pl.ds(at, GROUP), :].astype(BF16)
-        blocks = []
         for shift_y in range(3):
             y_five = lax.rem(gy + shift_y + 3, 4)
             y_four = lax.rem(gy // 2 + shift_y + 1, 2)
@@ -658,14 +676,15 @@
             part = part + dot(
                 four, one_hot((row == y_four * 16 + col - 32) & (col >= 32) & (col < 48))
             )
-            blocks.append(jnp.concatenate([six[shift_y], part + three], axis=1))
-        window = jnp.concatenate(blocks, axis=0).astype(BF16)
-        term = dot(matrix[shift_x], window)
-        total = term if total is None else total + term
-    products[...] = total
+            rows = slice(shift_y * GROUP, (shift_y + 1) * GROUP)
+            windows[shift_x, rows, 0:128] = six[shift_y].astype(BF16)
+            windows[shift_x, rows, 128:256] = (part + three).astype(BF16)
+    for half in range(2):
+        multiply([windows[shift_x] for shift_x in range(3)], 0, half)
+    leaf_products()
     for bits in range(4):
-        coarse[bits, 0:COEF, 0:128] = z_sum(products, bits, slice(0, 128), six_roll)
-        coarse[bits, 0:COEF, 128:256] = z_sum(products, bits, slice(128, 256), coarse_roll)
+        coarse[bits, 0:COEF, 0:128] = z_sum(products.at[0], bits, slice(0, 128), six_roll)
+        coarse[bits, 0:COEF, 128:256] = z_sum(products.at[0], bits, slice(128, 256), coarse_roll)
     eye = one_hot(iota((8 * COEF, 8 * COEF), 0) == iota((8 * COEF, 8 * COEF), 1))
     down32[...] = dot_nt(eye, down_ref[...])
     downs[...] = jnp.zeros_like(downs)
@@ -694,9 +713,11 @@
     wide = spread(value, (row == 48 + (col - 32) // 2) & (col >= 32) & (col < 48))
     bits = 2 * lax.rem(gx // 2, 2) + lax.rem(gy, 2)
     lift(wide, first_lanes)
+    leaf_products()
     value = coarse[bits, 0:COEF, right] + child(bits, first_lanes)
     wide = spread(value, (row == 32 + col // 2) & (col < 32))
     lift(wide, first_lanes)
+    leaf_products()
     wides = []
     for y in range(2):
         bits = 2 * lax.rem(gx, 2) + y
@@ -704,18 +725,25 @@
         wides.append(spread(value, (row == (col % 64) // 2) & (col // 64 == y)))
     wide = [(a.astype(F32) + b.astype(F32)).astype(BF16) for a, b in zip(*wides)]
     lift(wide, first_lanes)
+    leaf_products()
     for bits in range(4):
         value = coarse[bits, 0:COEF, 0:128] + child(bits, first_lanes)
         for y in range(2):
             for k, part in enumerate(spread(value, row == y * 64 + col // 2)):
                 at = ((bits // 2) * 4 + 2 * y + bits % 2) * 128
                 expand[k, :, at : at + 128] = part
+    leaf_products(8)
     lift([expand[k] for k in range(2)], slice(0, 1024))
-    for x in range(4):
-        for y in range(8):
-            at = ((x // 2) * 4 + y // 2) * 128
-            rows = pl.ds(x * 8 + y, COEF, stride=32)
-            out_ref[rows, :] = leaf_ref[rows, :] + child(2 * (x % 2) + y % 2, slice(at, at + 128))
+    for parent in range(4):
+        for xp in range(2):
+            at = (xp * 4 + parent) * 128
+            for bits in range(4):
+                value = z_sum(
+                    products.at[parent + 1], bits, slice(xp * 128, xp * 128 + 128), leaf_roll
+                )
+                x, y = 2 * xp + bits // 2, 2 * parent + bits % 2
+                rows = pl.ds(x * 8 + y, COEF, stride=32)
+                out_ref[rows, :] = value + child(bits, slice(at, at + 128))
 
 
 def all_levels(*inputs):
@@ -724,10 +752,12 @@
         (shape((1152, 128), F32),),
         inputs,
         (
+            pltpu.VMEM((6 * GROUP, 512), BF16),
             pltpu.VMEM((576, 128), F32),
             pltpu.VMEM((2 * GROUP, 128), F32),
             pltpu.VMEM((GROUP, 128), F32),
-            pltpu.VMEM((1024, 256), F32),
+            pltpu.VMEM((3, 3 * GROUP, 256), BF16),
+            pltpu.VMEM((5, 1024, 256), F32),
             pltpu.VMEM((4, 40, 256), F32),
             pltpu.VMEM((8 * COEF, COEF), F32),
             pltpu.VMEM((2, 160, COEF), F32),
@@ -754,31 +784,33 @@
     place = jnp.stack([lax.axis_index("gx"), lax.axis_index("gy")]).astype(jnp.int32)
     (
         grid, up_msg, down_msg, low_msg, high_msg, six, five, live,
-        positions, counts, up_operator, down_operator, far_operator,
+        positions, counts, up_operator,
     ) = prepare(
         leaf_multipoles.reshape(1152, 128), positions.reshape(768, 128), masses.reshape(256, 128),
-        counts.reshape(32, 128), up_operator.T, down_operator, far_operator,
+        counts.reshape(32, 128), up_operator.T,
     )
     positions = positions.reshape(3, 8, 4, 8, 128)
     counts = counts.reshape(4, 8, 128)
     below, above, two = moved(up_msg, 0, 1), moved(down_msg, 0, -1), moved(five, 0, 2)
     low, high = moved(high_msg, 1, 0), moved(low_msg, -1, 0)
-    inner = inner_pairs(positions, live.reshape(8, 4, 8, 128))
-    below, above, two, inner = lax.optimization_barrier((below, above, two, inner))
+    inner, shifted, far_operator, down_operator = plane_pairs(
+        positions, live.reshape(8, 4, 8, 128), far_operator, down_operator
+    )
+    matrix = far_matrix(far_operator)
+    below, above, two, inner, matrix = lax.optimization_barrier((below, above, two, inner, matrix))
     to_low, to_high = cross(place, below, above, two, five)
     low_corner, high_corner = moved(to_high, 1, 0), moved(to_low, -1, 0)
-    matrix = far_matrix(lax.optimization_barrier((far_operator, inner))[0])
+    inner = step_pairs(inner, shifted)
     inner = row_pairs(inner, positions, below, above)
-    low, high, low_corner, high_corner, inner, matrix = lax.optimization_barrier(
-        (low, high, low_corner, high_corner, inner, matrix)
+    low, high, low_corner, high_corner, inner = lax.optimization_barrier(
+        (low, high, low_corner, high_corner, inner)
     )
     three = jnp.concatenate([low_corner[C_FIVE:], to_low[C_FIVE:], high_corner[C_FIVE:]], axis=0)
     up_three, down_three = moved(three, 3, 0), moved(three, -3, 0)
     potential = face_pairs(inner, positions, counts, low, high, low_corner, high_corner)
-    leaf = leaf_level(matrix, grid, below, above, low, high, low_corner, high_corner)
-    up_three, down_three, leaf = lax.optimization_barrier((up_three, down_three, leaf))
+    up_three, down_three, potential = lax.optimization_barrier((up_three, down_three, potential))
     expansion = all_levels(
-        place, matrix, leaf, six, below, above, low, high, low_corner, high_corner,
+        place, matrix, grid, six, below, above, low, high, low_corner, high_corner,
         three, up_three, down_three, up_operator, down_operator,
     )
     return expansion.reshape(36, 4, 8, 128), potential

time: 44.3 us -> 39.9 us (0.901)
  Pallas kernels: 28.5 us -> 24.2 us
    pallas_call x8 -> x7, Pallas kernels: 28.5 us -> 21.7 us  [kernel_call(): pl.pallas_call(body, out_shape=outs, in_specs=[SMEM] * scalars + [space]...]
    pallas_call x0 -> x1, Pallas kernels: none -> 2.49 us  [plane_pairs(): pl.pallas_call(plane_kernel, out_shape=(shape((3, 8, 4, 8, 128), F32), sh...]
  transfers between devices with their start and end apart: 9 -> 9, of which waited for: 1 -> 2; matrix products, arithmetic and copies ran while one was open for 0% -> 0% of each run, Pallas kernels for 40% -> 31%
where the time goes in v2:
time: 39.9 us; the launch traced here: 39.6 us
  Pallas kernels  24.2 us (61%)
  starting transfers between devices  11.4 us (29%)
  waiting for transfers between devices  3.24 us (8%)
  between operations  0.71 us (2%)
    pallas_call x7, Pallas kernels, kernel_call(): pl.pallas_call(body, out_shape=outs, in_specs=[SMEM] * scalars + [space]...  21.7 us
    ppermute x9, starting transfers between devices, moved(): return lax.ppermute(value, ('gx', 'gy'), table)  11.4 us
    ppermute x9, waiting for transfers between devices, moved(): return lax.ppermute(value, ('gx', 'gy'), table)  3.24 us
    pallas_call x1, Pallas kernels, plane_pairs(): pl.pallas_call(plane_kernel, out_shape=(shape((3, 8, 4, 8, 128), F32), sh...  2.49 us
  transfers between devices with their start and end apart: 9, of which 2 were waited for; matrix products, arithmetic and copies ran while one was open for 0% of the time, Pallas kernels for 31%

profile of v2, /device:TPU:1, one launch (start us, length us, event | category | flops | bytes accessed | tf_op | source)
XLA Modules:
  0.0 39.6 jit_solution(8163279351127810091)
XLA Ops:
  0.6 2.6 %shard_map.86 = (bf16[1152,128]{1,0:T(8,128)(2,1)S(1)}, bf16[656,128]{1,0:T(8,128)(2,1)S(1)}, bf16[656,128]{1,0:T(8,128)(2,1)S(1)}, bf16[1232,128]{1,0:T(8,128)(...) custom-call(bf16[1152,128]{1,0:T(8,128)(2,1)} %bitcast.18, ...), custom_call_target="tpu_custom_call" | custom-call | tf_op jit(solution)/shard_map/pallas_call | solution.py:39
  3.3 2.2 %collective-permute-start = (bf16[656,128]{1,0:T(8,128)(2,1)S(1)}, bf16[656,128]{1,0:T(8,128)(2,1)S(1)}, u32[]{:S(2)}, u32[]{:S(2)}) collective-permute-start(bf16[656,128]{1,0:T(8,128)(2,1)S(1)} %get-tuple-element.32), channel_id=1, source_target_pairs={{0,1},{1,2},{2,3},{3,0},{4,5},{5,6},{6,7},{7,4},{8,9},{9,10},{10,1... | collective-permute-start | bytes 503816 | tf_op jit(solution)/shard_map/ppermute | solution.py:778
  5.5 2.1 %collective-permute-start.1 = (bf16[656,128]{1,0:T(8,128)(2,1)S(1)}, bf16[656,128]{1,0:T(8,128)(2,1)S(1)}, u32[]{:S(2)}, u32[]{:S(2)}) collective-permute-start(bf16[656,128]{1,0:T(8,128)(2,1)S(1)} %get-tuple-element.33), channel_id=1, source_target_pairs={{0,3},{1,0},{2,1},{3,2},{4,7},{5,4},{6,5},{7,6},{8,11},{9,8},{10,9... | collective-permute-start | bytes 503816 | tf_op jit(solution)/shard_map/ppermute | solution.py:778
  7.6 2.2 %collective-permute-start.3 = (bf16[1232,128]{1,0:T(8,128)(2,1)S(1)}, bf16[1232,128]{1,0:T(8,128)(2,1)S(1)}, u32[]{:S(2)}, u32[]{:S(2)}) collective-permute-start(bf16[1232,128]{1,0:T(8,128)(2,1)S(1)} %get-tuple-element.44), channel_id=1, source_target_pairs={{0,4},{1,5},{2,6},{3,7},{4,8},{5,9},{6,10},{7,11},{8,12},{9,13},{1... | collective-permute-start | bytes 946184 | tf_op jit(solution)/shard_map/ppermute | solution.py:778
  9.8 0.0 collective-permute-start.4
  9.8 0.5 %collective-permute-start.2 = (bf16[40,128]{1,0:T(8,128)(2,1)S(1)}, bf16[40,128]{1,0:T(8,128)(2,1)S(1)}, u32[]{:S(2)}, u32[]{:S(2)}) collective-permute-start(bf16[40,128]{1,0:T(8,128)(2,1)S(1)} %get-tuple-element.34.own), channel_id=1, source_target_pairs={{0,2},{1,3},{2,0},{3,1},{4,6},{5,7},{6,4},{7,5},{8,10},{9,11},{10,... | collective-permute-start | bytes 30728 | tf_op jit(solution)/shard_map/ppermute | solution.py:778
  10.3 0.1 pad_add_fusion.place
  10.4 2.5 %shard_map.87 = (f32[3,8,4,8,128]{4,3,2,1,0:T(8,128)S(1)}, f32[3,4,8,4,8,128]{5,4,3,2,1,0:T(8,128)S(1)}, bf16[36,11376]{1,0:T(8,128)(2,1)S(1)}, bf16[36,288]{1,0:T(8,128)(2,1)S(1)}) custom-call(f32[3,8,4,8,128]{4,3,2,1,0:T(8,128)S(1)} %bitcast.11, f32[8,4,8,128]{3,2,1,0:T(8,128)S(1)} %bitcast.14, bf16[36,11376]{1,0:T(8,128)(2,1)} %far_hbm.1, ...), custom_call_target="tpu_custom_call" | custom-call | tf_op jit(solution)/shard_map/pallas_call | solution.py:351
  12.9 0.6 %shard_map.88.matrix = bf16[3,432,1024]{2,1,0:T(8,128)(2,1)S(1)} custom-call(bf16[36,11376]{1,0:T(8,128)(2,1)S(1)} %get-tuple-element.38.far_ref), custom_call_target="tpu_custom_call" | custom-call | tf_op jit(solution)/shard_map/pallas_call | solution.py:39
  13.5 2.7 %collective-permute-done.2.two = bf16[40,128]{1,0:T(8,128)(2,1)S(1)} collective-permute-done((bf16[40,128]{1,0:T(8,128)(2,1)S(1)}, bf16[40,128]{1,0:T(8,128)(2,1)S(1)}, u32[]{:S(2)}, u32[]{:S(2)}) %collective-permute-start.2) | collective-permute-done | bytes 10272 | tf_op jit(solution)/shard_map/ppermute | solution.py:778
  16.2 0.0 collective-permute-done.below
  16.2 0.0 collective-permute-done.1.above
  16.2 0.7 %shard_map.89 = (bf16[640,128]{1,0:T(8,128)(2,1)S(1)}, bf16[640,128]{1,0:T(8,128)(2,1)S(1)}) custom-call(s32[2]{0:T(128)S(1)} %pad_add_fusion.place, bf16[656,128]{1,0:T(8,128)(2,1)S(1)} %collective-permute-done.below, bf16[656,128]{1,0:T(8,128)(2,1)S(1)} %collective-permute-done.1.above, bf16[40,128]{1,0:T(8,128)(2,1)S(1)} %collective-permute-done.2.two, ...), custom_call_target="tpu_custom_call" | custom-call | tf_op jit(solution)/shard_map/pallas_call | solution.py:39
  16.8 1.7 %collective-permute-start.5 = (bf16[640,128]{1,0:T(8,128)(2,1)S(1)}, bf16[640,128]{1,0:T(8,128)(2,1)S(1)}, u32[]{:S(2)}, u32[]{:S(2)}) collective-permute-start(bf16[640,128]{1,0:T(8,128)(2,1)S(1)} %get-tuple-element.47), channel_id=1, source_target_pairs={{0,4},{1,5},{2,6},{3,7},{4,8},{5,9},{6,10},{7,11},{8,12},{9,13},{1... | collective-permute-start | bytes 491528 | tf_op jit(solution)/shard_map/ppermute | solution.py:778
  18.6 0.0 collective-permute-start.6
  18.6 3.8 %shard_map.90.inner_ref = f32[8,4,8,128]{3,2,1,0:T(8,128)S(1)} custom-call(f32[3,8,4,8,128]{4,3,2,1,0:T(8,128)S(1)} %get-tuple-element.49.sums_ref, f32[3,4,8,4,8,128]{5,4,3,2,1,0:T(8,128)S(1)} %get-tuple-element.50.shifted), custom_call_target="tpu_custom_call" | custom-call | tf_op jit(solution)/shard_map/pallas_call | solution.py:39
  22.4 1.3 %shard_map.91.inner_ref = f32[8,4,8,128]{3,2,1,0:T(8,128)S(1)} custom-call(f32[8,4,8,128]{3,2,1,0:T(8,128)S(1)} %shard_map.90.inner_ref, f32[3,8,4,8,128]{4,3,2,1,0:T(8,128)S(1)} %bitcast.12, bf16[656,128]{1,0:T(8,128)(2,1)S(1)} %collective-permute-done.below, bf16[656,128]{1,0:T(8,128)(2,1)S(1)} %collective-permute-done.1.above), custom_call_target="tpu_custom_call" | custom-call | tf_op jit(solution)/shard_map/pallas_call | solution.py:39
  23.7 0.0 collective-permute-done.3.low
  23.7 0.0 collective-permute-done.5.low_corner
  23.7 0.5 %collective-permute-done.6.high_corner = bf16[640,128]{1,0:T(8,128)(2,1)S(1)} collective-permute-done((bf16[640,128]{1,0:T(8,128)(2,1)S(1)}, bf16[640,128]{1,0:T(8,128)(2,1)S(1)}, u32[]{:S(2)}, u32[]{:S(2)}) %collective-permute-start.6) | collective-permute-done | bytes 163872 | tf_op jit(solution)/shard_map/ppermute | solution.py:778
  24.3 2.2 %collective-permute-start.7 = (bf16[240,128]{1,0:T(8,128)(2,1)S(1)}, bf16[240,128]{1,0:T(8,128)(2,1)S(1)}, u32[]{:S(2)}, u32[]{:S(2)}) collective-permute-start(bf16[240,128]{1,0:T(8,128)(2,1)S(1)} %pad_maximum_fusion.near_three), channel_id=1, source_target_pairs={{0,12},{1,13},{2,14},{3,15},{4,16},{5,17},{6,18},{7,19},{8,20},{9,... | collective-permute-start | bytes 184328 | tf_op jit(solution)/shard_map/ppermute | solution.py:778
  26.5 0.5 %collective-permute-start.8 = (bf16[240,128]{1,0:T(8,128)(2,1)S(1)}, bf16[240,128]{1,0:T(8,128)(2,1)S(1)}, u32[]{:S(2)}, u32[]{:S(2)}) collective-permute-start(bf16[240,128]{1,0:T(8,128)(2,1)S(1)} %pad_maximum_fusion.near_three), channel_id=1, source_target_pairs={{0,20},{1,21},{2,22},{3,23},{4,24},{5,25},{6,26},{7,27},{8,28},{9,... | collective-permute-start | bytes 184328 | tf_op jit(solution)/shard_map/ppermute | solution.py:778
  27.0 3.3 %shard_map.92 = f32[8,4,8,128]{3,2,1,0:T(8,128)} custom-call(f32[8,4,8,128]{3,2,1,0:T(8,128)S(1)} %shard_map.91.inner_ref, f32[3,8,4,8,128]{4,3,2,1,0:T(8,128)S(1)} %bitcast.13, s32[4,8,128]{2,1,0:T(8,128)S(1)} %bitcast.15, bf16[1232,128]{1,0:T(8,128)(2,1)S(1)} %collective-permute-done.3.low, bf16[1232,128]{1,0:T(8,128)(2,1)S(1)} %collective-permute-done.4.high, ...), custom_call_target="tpu_custom_call" | custom-call | tf_op jit(solution)/shard_map/pallas_call | solution.py:39
  30.3 9.3 %shard_map.93 = f32[1152,128]{1,0:T(8,128)} custom-call(s32[2]{0:T(128)S(1)} %pad_add_fusion.place, bf16[3,432,1024]{2,1,0:T(8,128)(2,1)S(1)} %shard_map.88.matrix, bf16[1152,128]{1,0:T(8,128)(2,1)S(1)} %get-tuple-element.40.grid_ref, bf16[144,128]{1,0:T(8,128)(2,1)S(1)} %get-tuple-element.41.six_ref, bf16[656,128]{1,0:T(8,128)(2,1)S(1)} %collective-permute-done.below, ...), custom_call_target="tpu_custom_call" | custom-call | tf_op jit(solution)/shard_map/pallas_call | solution.py:39
  (7 shorter events, 0.0 us)
Async XLA Ops:
  3.3 12.9 %collective-permute-start = (bf16[656,128]{1,0:T(8,128)(2,1)S(1)}, bf16[656,128]{1,0:T(8,128)(2,1)S(1)}, u32[]{:S(2)}, u32[]{:S(2)}) collective-permute-start(bf16[656,128]{1,0:T(8,128)(2,1)S(1)} %get-tuple-element.32), channel_id=1, source_target_pairs={{0,1},{1,2},{2,3},{3,0},{4,5},{5,6},{6,7},{7,4},{8,9},{9,10},{10,1... | collective-permute-start | bytes 503816 | tf_op jit(solution)/shard_map/ppermute | solution.py:778
  5.5 10.7 %collective-permute-start.1 = (bf16[656,128]{1,0:T(8,128)(2,1)S(1)}, bf16[656,128]{1,0:T(8,128)(2,1)S(1)}, u32[]{:S(2)}, u32[]{:S(2)}) collective-permute-start(bf16[656,128]{1,0:T(8,128)(2,1)S(1)} %get-tuple-element.33), channel_id=1, source_target_pairs={{0,3},{1,0},{2,1},{3,2},{4,7},{5,4},{6,5},{7,6},{8,11},{9,8},{10,9... | collective-permute-start | bytes 503816 | tf_op jit(solution)/shard_map/ppermute | solution.py:778
  7.6 16.2 %collective-permute-start.3 = (bf16[1232,128]{1,0:T(8,128)(2,1)S(1)}, bf16[1232,128]{1,0:T(8,128)(2,1)S(1)}, u32[]{:S(2)}, u32[]{:S(2)}) collective-permute-start(bf16[1232,128]{1,0:T(8,128)(2,1)S(1)} %get-tuple-element.44), channel_id=1, source_target_pairs={{0,4},{1,5},{2,6},{3,7},{4,8},{5,9},{6,10},{7,11},{8,12},{9,13},{1... | collective-permute-start | bytes 946184 | tf_op jit(solution)/shard_map/ppermute | solution.py:778
  9.8 14.0 %collective-permute-start.4 = (bf16[1232,128]{1,0:T(8,128)(2,1)S(1)}, bf16[1232,128]{1,0:T(8,128)(2,1)S(1)}, u32[]{:S(2)}, u32[]{:S(2)}) collective-permute-start(bf16[1232,128]{1,0:T(8,128)(2,1)S(1)} %get-tuple-element.45), channel_id=1, source_target_pairs={{0,28},{1,29},{2,30},{3,31},{4,0},{5,1},{6,2},{7,3},{8,4},{9,5},{1... | collective-permute-start | bytes 946184 | tf_op jit(solution)/shard_map/ppermute | solution.py:778
  9.8 6.4 %collective-permute-start.2 = (bf16[40,128]{1,0:T(8,128)(2,1)S(1)}, bf16[40,128]{1,0:T(8,128)(2,1)S(1)}, u32[]{:S(2)}, u32[]{:S(2)}) collective-permute-start(bf16[40,128]{1,0:T(8,128)(2,1)S(1)} %get-tuple-element.34.own), channel_id=1, source_target_pairs={{0,2},{1,3},{2,0},{3,1},{4,6},{5,7},{6,4},{7,5},{8,10},{9,11},{10,... | collective-permute-start | bytes 30728 | tf_op jit(solution)/shard_map/ppermute | solution.py:778
  16.8 6.9 %collective-permute-start.5 = (bf16[640,128]{1,0:T(8,128)(2,1)S(1)}, bf16[640,128]{1,0:T(8,128)(2,1)S(1)}, u32[]{:S(2)}, u32[]{:S(2)}) collective-permute-start(bf16[640,128]{1,0:T(8,128)(2,1)S(1)} %get-tuple-element.47), channel_id=1, source_target_pairs={{0,4},{1,5},{2,6},{3,7},{4,8},{5,9},{6,10},{7,11},{8,12},{9,13},{1... | collective-permute-start | bytes 491528 | tf_op jit(solution)/shard_map/ppermute | solution.py:778
  18.6 5.7 %collective-permute-start.6 = (bf16[640,128]{1,0:T(8,128)(2,1)S(1)}, bf16[640,128]{1,0:T(8,128)(2,1)S(1)}, u32[]{:S(2)}, u32[]{:S(2)}) collective-permute-start(bf16[640,128]{1,0:T(8,128)(2,1)S(1)} %get-tuple-element.48), channel_id=1, source_target_pairs={{0,28},{1,29},{2,30},{3,31},{4,0},{5,1},{6,2},{7,3},{8,4},{9,5},{1... | collective-permute-start | bytes 491528 | tf_op jit(solution)/shard_map/ppermute | solution.py:778
  24.3 6.0 %collective-permute-start.7 = (bf16[240,128]{1,0:T(8,128)(2,1)S(1)}, bf16[240,128]{1,0:T(8,128)(2,1)S(1)}, u32[]{:S(2)}, u32[]{:S(2)}) collective-permute-start(bf16[240,128]{1,0:T(8,128)(2,1)S(1)} %pad_maximum_fusion.near_three), channel_id=1, source_target_pairs={{0,12},{1,13},{2,14},{3,15},{4,16},{5,17},{6,18},{7,19},{8,20},{9,... | collective-permute-start | bytes 184328 | tf_op jit(solution)/shard_map/ppermute | solution.py:778
  26.5 3.8 %collective-permute-start.8 = (bf16[240,128]{1,0:T(8,128)(2,1)S(1)}, bf16[240,128]{1,0:T(8,128)(2,1)S(1)}, u32[]{:S(2)}, u32[]{:S(2)}) collective-permute-start(bf16[240,128]{1,0:T(8,128)(2,1)S(1)} %pad_maximum_fusion.near_three), channel_id=1, source_target_pairs={{0,20},{1,21},{2,22},{3,23},{4,24},{5,25},{6,26},{7,27},{8,28},{9,... | collective-permute-start | bytes 184328 | tf_op jit(solution)/shard_map/ppermute | solution.py:778

commit v3 on v2

--- a/solution.py
+++ b/solution.py
@@ -14,14 +14,14 @@
 BF16 = jnp.bfloat16
 COEF = 36
 GROUP = 4 * COEF
-Y_LEAF = 256
+Y_LEAF = 128 + 96
 Y_SIX = Y_LEAF + 2 * GROUP
 Y_FIVE = Y_SIX + GROUP // 2
 Y_ROWS = Y_FIVE + 40
-X_LEAF = 512
+X_LEAF = 256 + 192
 X_SIX = X_LEAF + 4 * GROUP
 X_ROWS = X_SIX + GROUP
-C_LEAF = 128
+C_LEAF = 2 * 56
 C_SIX = C_LEAF + 2 * GROUP
 C_FIVE = C_SIX + GROUP
 C_ROWS = C_FIVE + 80
@@ -129,7 +129,8 @@
             rows.append(live_ref[pl.ds(x * 8 + y, 8, stride=32), :])
         high, low = parts(jnp.concatenate(rows, axis=0))
         msg[0:128, :] = high
-        msg[128:256, :] = low
+        for x in range(4):
+            msg[128 + 24 * x : 152 + 24 * x, :] = low[32 * x : 32 * x + 24]
     for msg, x in ((low_msg, 0), (high_msg, 3)):
         for slot in range(8):
             for axis in range(3):
@@ -139,7 +140,8 @@
             near32[pl.ds(24 + slot, 8, stride=32), :] = live_ref[start : start + 8, :]
         high, low = parts(near32[...])
         msg[0:256, :] = high
-        msg[256:512, :] = low
+        for y in range(8):
+            msg[256 + 24 * y : 280 + 24 * y, :] = low[32 * y : 32 * y + 24]
     low_half = iota((COEF, 128), 1) < 64
     even_up, odd_up = up_blocks(up_ref)
     row, col = iota((128, 128), 0), iota((128, 128), 1)
@@ -232,10 +234,9 @@
     halo = halo_six(below, above).astype(BF16)
     for msg, x, xp in ((to_low, 0, 0), (to_high, 3, 1)):
         for side, ref in enumerate((below, above)):
-            for half in range(2):
-                source = half * 128 + x * 32
-                first = side * 64 + half * 32
-                msg[first : first + 32, :] = ref[source : source + 32, :]
+            first = side * 56
+            msg[first : first + 32, :] = ref[32 * x : 32 * x + 32, :]
+            msg[first + 32 : first + 56, :] = ref[128 + 24 * x : 152 + 24 * x, :]
             source, first = Y_LEAF + xp * GROUP, C_LEAF + side * GROUP
             msg[first : first + GROUP, :] = ref[source : source + GROUP, :]
         msg[C_SIX:C_FIVE, :] = halo
@@ -284,6 +285,16 @@
 
 def plane_goals(shifted, x):
     return [[shifted[1, k, slot, x] for k in range(4)] for slot in range(8)]
+
+
+def step_pairs(shifted, sums, x):
+    for step_y in (-1, 0, 1):
+        goals = plane_goals(shifted, x)
+        totals = [sums[1, slot, x] for slot in range(8)]
+        for step_z in (-1, 0, 1):
+            pair_sums(shifted, sums, goals, x + 1, (1, step_y, step_z), totals)
+        for slot in range(8):
+            sums[1, slot, x] = totals[slot]
 
 
 def plane_kernel(pos_ref, live_ref, far_hbm, down_hbm, sums, shifted, far_ref, down_ref, sems):
@@ -318,33 +329,14 @@
         return carry
 
     lax.fori_loop(0, 4, plane, 0)
+
+    def step(x, carry):
+        step_pairs(shifted, sums, x)
+        return carry
+
+    lax.fori_loop(0, 2, step, 0)
     for copy in copies:
         copy.wait()
-
-
-def step_kernel(sums_ref, shifted, out_ref, sums):
-    sums[...] = sums_ref[...]
-
-    def planes(x, carry):
-        for step_y in (-1, 0, 1):
-            goals = plane_goals(shifted, x)
-            totals = [sums[1, slot, x] for slot in range(8)]
-            for step_z in (-1, 0, 1):
-                pair_sums(shifted, sums, goals, x + 1, (1, step_y, step_z), totals)
-            for slot in range(8):
-                sums[1, slot, x] = totals[slot]
-        return carry
-
-    lax.fori_loop(0, 3, planes, 0)
-
-    def finish(x, carry):
-        for slot in range(8):
-            out_ref[slot, x] = (
-                sums[1, slot, x] + lane_roll(sums[0, slot, x], -1) + lane_roll(sums[2, slot, x], 1)
-            )
-        return carry
-
-    lax.fori_loop(0, 4, finish, 0)
 
 
 def plane_pairs(positions, live, far_operator, down_operator):
@@ -363,112 +355,122 @@
     )(positions, live, in_hbm(far_operator), in_hbm(down_operator))
 
 
-def step_pairs(*inputs):
-    return kernel_call(
-        step_kernel,
-        (shape((8, 4, 8, 128), F32),),
-        inputs,
-        (pltpu.VMEM((3, 8, 4, 8, 128), F32),),
-    )[0]
-
-
-def gather(shifted, goals, totals):
-    def body(index, carry):
-        carry = list(carry)
+def joined(target, msg, high, low, count):
+    for cell in range(count):
+        first = 32 * cell
+        whole = msg[high + first : high + first + 32, :].astype(F32)
+        rest = msg[low + 24 * cell : low + 24 * cell + 24, :].astype(F32)
+        target[first : first + 24, :] = whole[0:24] + rest
+        target[first + 24 : first + 32, :] = whole[24:32]
+
+
+def add_sources(fetch, shifted, goals, totals):
+    for slot in range(8):
+        values = [fetch(k, slot) for k in range(4)]
+        for step in (-1, 0, 1):
+            moved = [lane_roll(value, -step) for value in values]
+            if step:
+                moved[2] = moved[2] + F32(step)
+            for k in range(4):
+                shifted[step + 1, k, slot] = moved[k]
+    totals = list(totals)
+    for step in range(3):
         for slot in range(8):
-            source = [shifted[index, k, slot] for k in range(4)]
+            source = [shifted[step, k, slot] for k in range(4)]
             for goal in range(8):
-                carry[goal] = carry[goal] + source[3] * inverse_distance(goals[goal], source)
-        return tuple(carry)
-
-    return lax.fori_loop(0, 9, body, tuple(totals))
-
-
-def rows_kernel(inner_ref, pos_ref, below, above, out_ref, near32, shifted):
-    row = iota((8, 128), 0)
-    for index, msg in enumerate((below, above)):
-        near32[index] = msg[0:128, :].astype(F32) + msg[128:256, :].astype(F32)
-    turn = jnp.where(row >= 4, F32(1.0), F32(-1.0))
-    none = jnp.zeros((1, 128), F32)
+                totals[goal] = totals[goal] + source[3] * inverse_distance(goals[goal], source)
+    return tuple(totals)
+
+
+def rows_kernel(
+    inner_ref, pos_ref, count_ref, below, above, low_corner, high_corner, out_ref,
+    sources, shifted, added,
+):
+    turn = jnp.where(iota((8, 128), 0) >= 4, F32(1.0), F32(-1.0))
+    for side, msg in enumerate((below, above)):
+        first = side * 128
+        joined(sources.at[1, pl.ds(first, 128)], msg, 0, 128, 4)
+        high = side * 56
+        joined(sources.at[0, pl.ds(first, 32)], low_corner, high, high + 32, 1)
+        sources[0, first + 32 : first + 128, :] = sources[1, first : first + 96, :]
+        sources[2, first : first + 96, :] = sources[1, first + 32 : first + 128, :]
+        joined(sources.at[2, pl.ds(first + 96, 32)], high_corner, high, high + 32, 1)
+    goals = []
     for slot in range(8):
-        for k in range(4):
-            source = [
-                [none] + [near32[side, pl.ds(x * 32 + 8 * k + slot, 1), :] for x in range(4)] + [none]
-                for side in range(2)
+        at = [(axis * 8 + slot) * 32 for axis in range(3)]
+        goals.append(
+            [
+                jnp.concatenate(
+                    [pos_ref[pl.ds(a, 4, stride=8), :], pos_ref[pl.ds(a + 7, 4, stride=8), :]], axis=0
+                )
+                for a in at
             ]
-            for step_x in range(3):
-                value = jnp.concatenate(
-                    source[0][step_x : step_x + 4] + source[1][step_x : step_x + 4], axis=0
-                )
-                if k == 0:
-                    value = value + F32(step_x - 1)
-                if k == 1:
-                    value = value + turn
-                for step_z in range(3):
-                    moved = lane_roll(value, 1 - step_z)
-                    if k == 2:
-                        moved = moved + F32(step_z - 1)
-                    shifted[step_x * 3 + step_z, k, slot] = moved
-
-    def edge_rows(ref, lead):
-        return jnp.concatenate(
-            [ref[lead + (x, pl.ds(0, 1))] for x in range(4)]
-            + [ref[lead + (x, pl.ds(7, 1))] for x in range(4)],
-            axis=0,
         )
 
-    goals = [[edge_rows(pos_ref, (axis, slot)) for axis in range(3)] for slot in range(8)]
-    totals = gather(shifted, goals, [jnp.zeros((8, 128), F32) for slot in range(8)])
-    out_ref[...] = inner_ref[...]
+    def body(step_x, totals):
+        def fetch(k, slot):
+            value = sources[step_x, pl.ds(8 * k + slot, 8, stride=32), :]
+            if k == 0:
+                value = value + (step_x - 1).astype(F32)
+            return value + turn if k == 1 else value
+
+        return add_sources(fetch, shifted, goals, totals)
+
+    totals = lax.fori_loop(0, 3, body, tuple(jnp.zeros((8, 128), F32) for slot in range(8)))
+    added[...] = jnp.zeros_like(added)
     for slot in range(8):
-        for x in range(4):
-            for y, r in ((0, x), (7, x + 4)):
-                out_ref[slot, x, pl.ds(y, 1)] = out_ref[slot, x, pl.ds(y, 1)] + totals[slot][r : r + 1]
-
-
-def faces_kernel(
-    inner_ref, pos_ref, count_ref, low, high, low_corner, high_corner, out_ref, sides, shifted, sums
-):
-    for index, (msg, corner) in enumerate(((low, low_corner), (high, high_corner))):
-        sides[index, 0:32, :] = corner[0:32, :].astype(F32) + corner[32:64, :].astype(F32)
-        sides[index, 32:288, :] = msg[0:256, :].astype(F32) + msg[256:512, :].astype(F32)
-        sides[index, 288:320, :] = corner[64:96, :].astype(F32) + corner[96:128, :].astype(F32)
+        added[pl.ds(slot * 32, 4, stride=8), :] = totals[slot][0:4]
+        added[pl.ds(slot * 32 + 7, 4, stride=8), :] = totals[slot][4:8]
+    count = count_ref[...]
+    for slot in range(8):
+        rows = slice(slot * 32, slot * 32 + 32)
+        total = inner_ref[rows, :] + added[rows, :]
+        out_ref[rows, :] = jnp.where(count > slot, -total / 8, F32(0.0))
+
+
+def faces_kernel(sums_ref, shifted_ref, pos_ref, low, high, out_ref, sides, shifted, sums):
+    sums[...] = sums_ref[...]
+    step_pairs(shifted_ref, sums, 2)
+    for x in range(4):
+        for slot in range(8):
+            out_ref[slot, x] = (
+                sums[1, slot, x] + lane_roll(sums[0, slot, x], -1) + lane_roll(sums[2, slot, x], 1)
+            )
+    sides[...] = jnp.zeros_like(sides)
+    for index, msg in enumerate((low, high)):
+        joined(sides.at[index, pl.ds(32, 256)], msg, 0, 256, 8)
 
     def face(index, carry):
-        for slot in range(8):
-            for step_y in range(3):
-                values = [
-                    sides[index, pl.ds(step_y * 32 + 8 * k + slot, 8, stride=32), :]
-                    for k in range(4)
-                ]
-                values[0] = values[0] + (2 * index - 1).astype(F32)
-                values[1] = values[1] + F32(step_y - 1)
-                for step_z in range(3):
-                    moved = [lane_roll(value, 1 - step_z) for value in values]
-                    moved[2] = moved[2] + F32(step_z - 1)
-                    for k in range(4):
-                        shifted[step_y * 3 + step_z, k, slot] = moved[k]
         x = 3 * index
         goals = [[pos_ref[axis, slot, x] for axis in range(3)] for slot in range(8)]
-        totals = gather(shifted, goals, [inner_ref[slot, x] for slot in range(8)])
+
+        def body(step_y, totals):
+            def fetch(k, slot):
+                value = sides[index, pl.ds(step_y * 32 + 8 * k + slot, 8, stride=32), :]
+                if k == 0:
+                    value = value + (2 * index - 1).astype(F32)
+                return value + (step_y - 1).astype(F32) if k == 1 else value
+
+            return add_sources(fetch, shifted, goals, totals)
+
+        totals = lax.fori_loop(0, 3, body, tuple(out_ref[slot, x] for slot in range(8)))
         for slot in range(8):
-            sums[slot, x] = totals[slot]
+            out_ref[slot, x] = totals[slot]
         return carry
 
     lax.fori_loop(0, 2, face, 0)
-    for x in (1, 2):
-        for slot in range(8):
-            sums[slot, x] = inner_ref[slot, x]
-    for slot in range(8):
-        out_ref[slot] = jnp.where(count_ref[...] > slot, -sums[slot] / 8, F32(0.0))
 
 
 def row_pairs(*inputs):
     return kernel_call(
         rows_kernel,
-        (shape((8, 4, 8, 128), F32),),
+        (shape((256, 128), F32),),
         inputs,
-        (pltpu.VMEM((2, 128, 128), F32), pltpu.VMEM((9, 4, 8, 8, 128), F32)),
+        (
+            pltpu.VMEM((3, 256, 128), F32),
+            pltpu.VMEM((3, 4, 8, 8, 128), F32),
+            pltpu.VMEM((256, 128), F32),
+        ),
     )[0]
 
 
@@ -479,8 +481,8 @@
         inputs,
         (
             pltpu.VMEM((2, 320, 128), F32),
-            pltpu.VMEM((9, 4, 8, 8, 128), F32),
-            pltpu.VMEM((8, 4, 8, 128), F32),
+            pltpu.VMEM((3, 4, 8, 8, 128), F32),
+            pltpu.VMEM((3, 8, 4, 8, 128), F32),
         ),
     )[0]
 
@@ -541,12 +543,12 @@
     )[0]
 
 
-def z_sum(products, bits, lanes, roll):
-    odd = iota((COEF, 128), 1) % 2 == 1
+def z_sum(products, bits, lanes, first):
+    odd = iota((COEF, 128), 1) % 2 != first
     total = None
     for step in range(-3, 4):
-        first = bits * 256 + (step + 3) * COEF
-        value = roll(products[first : first + COEF, lanes], step)
+        start = bits * 256 + (step + 3) * COEF
+        value = lane_roll(products[start : start + COEF, lanes], -step)
         if step == 3:
             value = jnp.where(odd, F32(0.0), value)
         if step == -3:
@@ -555,49 +557,44 @@
     return total
 
 
-def leaf_roll(value, step):
-    return lane_roll(value, -step)
-
-
-def six_roll(value, step):
-    if not step:
-        return value
-    cell = iota(value.shape, 1) % 64 + step
-    inside = (cell >= 0) & (cell < 64)
-    return jnp.where(inside, lane_roll(value, -step), lane_roll(value, 64 - step))
-
-
-def coarse_roll(value, step):
-    if not step:
-        return value
-    lane = iota(value.shape, 1)
-    period = jnp.where(lane < 32, 32, jnp.where(lane < 48, 16, 8))
-    cell = jnp.where(lane < 32, lane, jnp.where(lane < 48, lane - 32, lane - 48))
-    inside = (cell + step >= 0) & (cell + step < period)
-    sign = 1 if step > 0 else -1
-    wrapped = jnp.where(
-        period == 32,
-        lane_roll(value, sign * 32 - step),
-        jnp.where(period == 16, lane_roll(value, sign * 16 - step), lane_roll(value, sign * 8 - step)),
-    )
-    return jnp.where(inside, lane_roll(value, -step), wrapped)
+def multiply(matrix, rows, sources):
+    total = None
+    for shift_x, source in enumerate(sources):
+        term = dot_tn(matrix[shift_x, :, rows], source)
+        total = term if total is None else total + term
+    return total
+
+
+def windows_x(cells, parent):
+    rows = slice(parent * GROUP, (parent + 3) * GROUP)
+    return [cells[rows, shift_x * 128 : shift_x * 128 + 256] for shift_x in range(3)]
+
+
+def middle_kernel(matrix, grid_ref, low, high, products, cells):
+    cells[:, 0:128] = low[X_LEAF:X_SIX, :]
+    cells[:, 128:256] = grid_ref[0 : 4 * GROUP, :]
+    cells[:, 256:384] = grid_ref[4 * GROUP : 8 * GROUP, :]
+    cells[:, 384:512] = high[X_LEAF:X_SIX, :]
+    for parent in range(2):
+        products[parent] = multiply(matrix, slice(0, 1024), windows_x(cells, parent))
+
+
+def middle_products(*inputs):
+    return kernel_call(
+        middle_kernel,
+        (shape((2, 1024, 256), F32),),
+        inputs,
+        (pltpu.VMEM((4 * GROUP, 512), BF16),),
+    )[0]
 
 
 def levels_kernel(
-    place, matrix, grid_ref, six_ref, below, above, low, high, low_corner, high_corner,
+    place, matrix, middle, grid_ref, six_ref, below, above, low, high, low_corner, high_corner,
     near_three, up_three, down_three, up_ref, down_ref, out_ref,
     cells, fives, fours, three32, windows, products, coarse, down32, downs, expand, lifted,
 ):
     gx, gy = place[0], place[1]
     row, col = iota((128, 128), 0), iota((128, 128), 1)
-
-    def multiply(sources, slot, half):
-        rows = slice(half * 512, half * 512 + 512)
-        total = None
-        for shift_x, source in enumerate(sources):
-            term = dot_tn(matrix[shift_x, :, rows], source)
-            total = term if total is None else total + term
-        products[slot, rows, :] = total
 
     for first, msg, corner in ((0, low, low_corner), (384, high, high_corner)):
         lanes = slice(first, first + 128)
@@ -611,13 +608,12 @@
         cells[GROUP : 5 * GROUP, lanes] = grid_ref[xp * 4 * GROUP : (xp + 1) * 4 * GROUP, :]
         cells[5 * GROUP : 6 * GROUP, lanes] = above[source : source + GROUP, :]
 
-    todo = [(parent, half) for parent in range(4) for half in range(2)]
+    todo = [(side, half) for side in range(2) for half in range(2)]
 
     def leaf_products(count=1):
-        for parent, half in todo[:count]:
-            rows = slice(parent * GROUP, (parent + 3) * GROUP)
-            lanes = [slice(shift_x * 128, shift_x * 128 + 256) for shift_x in range(3)]
-            multiply([cells[rows, lane] for lane in lanes], parent + 1, half)
+        for side, half in todo[:count]:
+            rows = slice(half * 512, half * 512 + 512)
+            products[side + 1, rows, :] = multiply(matrix, rows, windows_x(cells, 3 * side))
         del todo[:count]
 
     size = fives.shape[0] // 72
@@ -652,39 +648,40 @@
         three32[x * 2 * COEF : x * 2 * COEF + COEF, :] = value
         three32[x * 2 * COEF + COEF : (x + 1) * 2 * COEF, :] = lane_roll(value, 120)
     leaf_products()
-    three = dot(three32[...].astype(BF16), one_hot((row == col - 48) & (col >= 48) & (col < 56)))
-    wide_low = iota((GROUP, 128), 1) < 64
+    def wrapped(first, base, size):
+        cell = lax.rem(col - first - 3 + size, size)
+        return one_hot((row == base + cell) & (col >= first) & (col < first + size + 6))
+
+    three = dot(three32[...].astype(BF16), wrapped(92, 0, 8))
+    six_lanes = [wrapped(0, 0, 64), wrapped(0, 64, 64)]
     for shift_x in range(3):
         if shift_x == 1:
-            own, other = six_ref[...].astype(F32), halo_six(below, above)
+            own, other = six_ref[...], halo_six(below, above).astype(BF16)
         else:
-            own = (low if shift_x == 0 else high)[X_SIX:X_ROWS, :].astype(F32)
-            other = (low_corner if shift_x == 0 else high_corner)[C_SIX:C_FIVE, :].astype(F32)
-        six = [
-            lane_roll(jnp.where(wide_low, own, other), 64),
-            own,
-            lane_roll(jnp.where(wide_low, other, own), 64),
-        ]
+            own = (low if shift_x == 0 else high)[X_SIX:X_ROWS, :]
+            other = (low_corner if shift_x == 0 else high_corner)[C_SIX:C_FIVE, :]
         at = pl.multiple_of(lax.rem(gx // 2 + shift_x + 3, 4) * GROUP, 8)
         five = fives[pl.ds(at, GROUP), :].astype(BF16)
         at = pl.multiple_of(lax.rem(gx // 4 + shift_x + 1, 2) * GROUP, 8)
         four = fours[pl.ds(at, GROUP), :].astype(BF16)
         for shift_y in range(3):
+            left = dot(other if shift_y == 0 else own, six_lanes[0 if shift_y == 1 else 1])
+            right = dot(other if shift_y == 2 else own, six_lanes[1 if shift_y == 1 else 0])
             y_five = lax.rem(gy + shift_y + 3, 4)
             y_four = lax.rem(gy // 2 + shift_y + 1, 2)
-            part = dot(five, one_hot((row == y_five * 32 + col) & (col < 32)))
-            part = part + dot(
-                four, one_hot((row == y_four * 16 + col - 32) & (col >= 32) & (col < 48))
-            )
+            left = left + dot(five, wrapped(70, y_five * 32, 32))
+            right = right + dot(four, wrapped(70, y_four * 16, 16)) + three
             rows = slice(shift_y * GROUP, (shift_y + 1) * GROUP)
-            windows[shift_x, rows, 0:128] = six[shift_y].astype(BF16)
-            windows[shift_x, rows, 128:256] = (part + three).astype(BF16)
+            windows[shift_x, rows, 0:128] = left.astype(BF16)
+            windows[shift_x, rows, 128:256] = right.astype(BF16)
     for half in range(2):
-        multiply([windows[shift_x] for shift_x in range(3)], 0, half)
+        rows = slice(half * 512, half * 512 + 512)
+        products[0, rows, :] = multiply(matrix, rows, [windows[shift_x] for shift_x in range(3)])
     leaf_products()
+    coarse[...] = jnp.zeros_like(coarse)
     for bits in range(4):
-        coarse[bits, 0:COEF, 0:128] = z_sum(products.at[0], bits, slice(0, 128), six_roll)
-        coarse[bits, 0:COEF, 128:256] = z_sum(products.at[0], bits, slice(128, 256), coarse_roll)
+        for lanes in (slice(0, 128), slice(128, 256)):
+            coarse[bits * 40 : bits * 40 + COEF, lanes] = z_sum(products.at[0], bits, lanes, 1)
     eye = one_hot(iota((8 * COEF, 8 * COEF), 0) == iota((8 * COEF, 8 * COEF), 1))
     down32[...] = dot_nt(eye, down_ref[...])
     downs[...] = jnp.zeros_like(downs)
@@ -697,53 +694,50 @@
     def spread(value, mask):
         return [dot(part, one_hot(mask)).astype(BF16) for part in parts(value)]
 
-    def lift(wide, lanes):
+    def lift(wide, lanes, first):
         halves = [dot(value, wide[0]) + dot(value, wide[1]) for value in operators]
-        lifted[:, lanes] = jnp.where(iota(halves[0].shape, 1) % 2 == 1, halves[1], halves[0])
-
-    def child(bits, lanes):
-        first = bits * 40 if isinstance(bits, int) else pl.multiple_of(bits * 40, 8)
-        return lifted[pl.ds(first, COEF), lanes]
-
-    first_lanes = slice(0, 128)
-
-    right = slice(128, 256)
+        even = iota(halves[0].shape, 1) % 2 == first
+        lifted[:, lanes] = jnp.where(even, halves[0], halves[1])
+
+    def block(bits):
+        return pl.ds(bits * 40 if isinstance(bits, int) else pl.multiple_of(bits * 40, 8), COEF)
+
+    left, right, both = slice(0, 128), slice(128, 256), slice(0, 256)
     bits = 2 * lax.rem(gx // 4, 2) + lax.rem(gy // 2, 2)
-    value = coarse[bits, 0:COEF, right]
-    wide = spread(value, (row == 48 + (col - 32) // 2) & (col >= 32) & (col < 48))
+    value = coarse[block(bits), right]
+    wide = spread(value, (row == 95 + (col - 73) // 2) & (col >= 73) & (col < 89))
+    lift(wide, left, 1)
+    leaf_products()
     bits = 2 * lax.rem(gx // 2, 2) + lax.rem(gy, 2)
-    lift(wide, first_lanes)
-    leaf_products()
-    value = coarse[bits, 0:COEF, right] + child(bits, first_lanes)
-    wide = spread(value, (row == 32 + col // 2) & (col < 32))
-    lift(wide, first_lanes)
+    value = coarse[block(bits), right] + lifted[block(bits), left]
+    wide = spread(value, (row == 73 + (col - 73) // 2) & (col >= 73) & (col < 105))
+    lift(wide, left, 1)
     leaf_products()
     wides = []
     for y in range(2):
         bits = 2 * lax.rem(gx, 2) + y
-        value = coarse[bits, 0:COEF, right] + child(bits, first_lanes)
-        wides.append(spread(value, (row == (col % 64) // 2) & (col // 64 == y)))
-    wide = [(a.astype(F32) + b.astype(F32)).astype(BF16) for a, b in zip(*wides)]
-    lift(wide, first_lanes)
+        value = coarse[block(bits), left] + lifted[block(bits), left]
+        wides.append(spread(value, (row == 73 + (col - 3) // 2) & (col >= 3) & (col < 67)))
+    lift([jnp.concatenate(pair, axis=1) for pair in zip(*wides)], both, 1)
     leaf_products()
-    for bits in range(4):
-        value = coarse[bits, 0:COEF, 0:128] + child(bits, first_lanes)
+    doubled = one_hot(row == 3 + col // 2)
+    for k, part in enumerate(parts(coarse[...] + lifted[:, both])):
         for y in range(2):
-            for k, part in enumerate(spread(value, row == y * 64 + col // 2)):
+            wide = dot(part[:, y * 128 : y * 128 + 128], doubled)
+            for bits in range(4):
                 at = ((bits // 2) * 4 + 2 * y + bits % 2) * 128
-                expand[k, :, at : at + 128] = part
+                expand[k, :, at : at + 128] = wide[bits * 40 : bits * 40 + COEF].astype(BF16)
     leaf_products(8)
-    lift([expand[k] for k in range(2)], slice(0, 1024))
+    lift([expand[k] for k in range(2)], slice(0, 1024), 0)
     for parent in range(4):
+        source = middle.at[parent - 1] if parent in (1, 2) else products.at[1 + parent // 3]
         for xp in range(2):
             at = (xp * 4 + parent) * 128
             for bits in range(4):
-                value = z_sum(
-                    products.at[parent + 1], bits, slice(xp * 128, xp * 128 + 128), leaf_roll
-                )
+                value = z_sum(source, bits, slice(xp * 128, xp * 128 + 128), 0)
                 x, y = 2 * xp + bits // 2, 2 * parent + bits % 2
                 rows = pl.ds(x * 8 + y, COEF, stride=32)
-                out_ref[rows, :] = value + child(bits, slice(at, at + 128))
+                out_ref[rows, :] = value + lifted[block(bits), at : at + 128]
 
 
 def all_levels(*inputs):
@@ -757,8 +751,8 @@
             pltpu.VMEM((2 * GROUP, 128), F32),
             pltpu.VMEM((GROUP, 128), F32),
             pltpu.VMEM((3, 3 * GROUP, 256), BF16),
-            pltpu.VMEM((5, 1024, 256), F32),
-            pltpu.VMEM((4, 40, 256), F32),
+            pltpu.VMEM((3, 1024, 256), F32),
+            pltpu.VMEM((160, 256), F32),
             pltpu.VMEM((8 * COEF, COEF), F32),
             pltpu.VMEM((2, 160, COEF), F32),
             pltpu.VMEM((2, COEF, 1024), BF16),
@@ -790,7 +784,6 @@
         counts.reshape(32, 128), up_operator.T,
     )
     positions = positions.reshape(3, 8, 4, 8, 128)
-    counts = counts.reshape(4, 8, 128)
     below, above, two = moved(up_msg, 0, 1), moved(down_msg, 0, -1), moved(five, 0, 2)
     low, high = moved(high_msg, 1, 0), moved(low_msg, -1, 0)
     inner, shifted, far_operator, down_operator = plane_pairs(
@@ -800,20 +793,23 @@
     below, above, two, inner, matrix = lax.optimization_barrier((below, above, two, inner, matrix))
     to_low, to_high = cross(place, below, above, two, five)
     low_corner, high_corner = moved(to_high, 1, 0), moved(to_low, -1, 0)
-    inner = step_pairs(inner, shifted)
-    inner = row_pairs(inner, positions, below, above)
-    low, high, low_corner, high_corner, inner = lax.optimization_barrier(
-        (low, high, low_corner, high_corner, inner)
-    )
+    inner = face_pairs(inner, shifted, positions, low, high)
+    low_corner, high_corner, inner = lax.optimization_barrier((low_corner, high_corner, inner))
     three = jnp.concatenate([low_corner[C_FIVE:], to_low[C_FIVE:], high_corner[C_FIVE:]], axis=0)
     up_three, down_three = moved(three, 3, 0), moved(three, -3, 0)
-    potential = face_pairs(inner, positions, counts, low, high, low_corner, high_corner)
-    up_three, down_three, potential = lax.optimization_barrier((up_three, down_three, potential))
+    potential = row_pairs(
+        inner.reshape(256, 128), positions.reshape(768, 128), counts, below, above, low_corner,
+        high_corner,
+    )
+    middle = middle_products(lax.optimization_barrier((matrix, low_corner))[0], grid, low, high)
+    up_three, down_three, potential, middle = lax.optimization_barrier(
+        (up_three, down_three, potential, middle)
+    )
     expansion = all_levels(
-        place, matrix, grid, six, below, above, low, high, low_corner, high_corner,
+        place, matrix, middle, grid, six, below, above, low, high, low_corner, high_corner,
         three, up_three, down_three, up_operator, down_operator,
     )
-    return expansion.reshape(36, 4, 8, 128), potential
+    return expansion.reshape(36, 4, 8, 128), potential.reshape(8, 4, 8, 128)
 
 
 def extended(cells, sides, width):

time: 39.9 us -> 38.6 us (0.967)
  waiting for transfers between devices: 3.24 us -> 2.75 us
  Pallas kernels: 24.2 us -> 23.8 us
    pallas_call x7, Pallas kernels: 21.7 us -> 19 us  [kernel_call(): pl.pallas_call(body, out_shape=outs, in_specs=[SMEM] * scalars + [space]...]
    pallas_call x1, Pallas kernels: 2.49 us -> 4.77 us  [plane_pairs(): pl.pallas_call(plane_kernel, out_shape=(shape((3, 8, 4, 8, 128), F32), sh...]
    ppermute x9, waiting for transfers between devices: 3.24 us -> 2.75 us  [moved(): return lax.ppermute(value, ('gx', 'gy'), table)]
  transfers between devices with their start and end apart: 9 -> 9, of which waited for: 2 -> 2; matrix products, arithmetic and copies ran while one was open for 0% -> 0% of each run, Pallas kernels for 31% -> 35%
where the time goes in v3:
time: 38.6 us; the launch traced here: 38.5 us
  Pallas kernels  23.8 us (62%)
  starting transfers between devices  11.2 us (29%)
  waiting for transfers between devices  2.75 us (7%)
  between operations  0.72 us (2%)
    pallas_call x7, Pallas kernels, kernel_call(): pl.pallas_call(body, out_shape=outs, in_specs=[SMEM] * scalars + [space]...  19 us
    ppermute x9, starting transfers between devices, moved(): return lax.ppermute(value, ('gx', 'gy'), table)  11.2 us
    pallas_call x1, Pallas kernels, plane_pairs(): pl.pallas_call(plane_kernel, out_shape=(shape((3, 8, 4, 8, 128), F32), sh...  4.77 us
    ppermute x9, waiting for transfers between devices, moved(): return lax.ppermute(value, ('gx', 'gy'), table)  2.75 us
  transfers between devices with their start and end apart: 9, of which 2 were waited for; matrix products, arithmetic and copies ran while one was open for 0% of the time, Pallas kernels for 35%

profile of v3, /device:TPU:1, one launch (start us, length us, event | category | flops | bytes accessed | tf_op | source)
XLA Modules:
  0.0 38.5 jit_solution(5865853873602299172)
XLA Ops:
  0.6 2.6 %shard_map.86 = (bf16[1152,128]{1,0:T(8,128)(2,1)S(1)}, bf16[624,128]{1,0:T(8,128)(2,1)S(1)}, bf16[624,128]{1,0:T(8,128)(2,1)S(1)}, bf16[1168,128]{1,0:T(8,128)(...) custom-call(bf16[1152,128]{1,0:T(8,128)(2,1)} %bitcast.18, ...), custom_call_target="tpu_custom_call" | custom-call | tf_op jit(solution)/shard_map/pallas_call | solution.py:39
  3.3 2.2 %collective-permute-start = (bf16[624,128]{1,0:T(8,128)(2,1)S(1)}, bf16[624,128]{1,0:T(8,128)(2,1)S(1)}, u32[]{:S(2)}, u32[]{:S(2)}) collective-permute-start(bf16[624,128]{1,0:T(8,128)(2,1)S(1)} %get-tuple-element.32), channel_id=1, source_target_pairs={{0,1},{1,2},{2,3},{3,0},{4,5},{5,6},{6,7},{7,4},{8,9},{9,10},{10,1... | collective-permute-start | bytes 479240 | tf_op jit(solution)/shard_map/ppermute | solution.py:772
  5.4 2.1 %collective-permute-start.1 = (bf16[624,128]{1,0:T(8,128)(2,1)S(1)}, bf16[624,128]{1,0:T(8,128)(2,1)S(1)}, u32[]{:S(2)}, u32[]{:S(2)}) collective-permute-start(bf16[624,128]{1,0:T(8,128)(2,1)S(1)} %get-tuple-element.33), channel_id=1, source_target_pairs={{0,3},{1,0},{2,1},{3,2},{4,7},{5,4},{6,5},{7,6},{8,11},{9,8},{10,9... | collective-permute-start | bytes 479240 | tf_op jit(solution)/shard_map/ppermute | solution.py:772
  7.5 2.2 %collective-permute-start.5 = (bf16[1168,128]{1,0:T(8,128)(2,1)S(1)}, bf16[1168,128]{1,0:T(8,128)(2,1)S(1)}, u32[]{:S(2)}, u32[]{:S(2)}) collective-permute-start(bf16[1168,128]{1,0:T(8,128)(2,1)S(1)} %get-tuple-element.47), channel_id=1, source_target_pairs={{0,4},{1,5},{2,6},{3,7},{4,8},{5,9},{6,10},{7,11},{8,12},{9,13},{1... | collective-permute-start | bytes 897032 | tf_op jit(solution)/shard_map/ppermute | solution.py:772
  9.7 0.0 collective-permute-start.6
  9.7 0.5 %collective-permute-start.2 = (bf16[40,128]{1,0:T(8,128)(2,1)S(1)}, bf16[40,128]{1,0:T(8,128)(2,1)S(1)}, u32[]{:S(2)}, u32[]{:S(2)}) collective-permute-start(bf16[40,128]{1,0:T(8,128)(2,1)S(1)} %get-tuple-element.34.own), channel_id=1, source_target_pairs={{0,2},{1,3},{2,0},{3,1},{4,6},{5,7},{6,4},{7,5},{8,10},{9,11},{10,... | collective-permute-start | bytes 30728 | tf_op jit(solution)/shard_map/ppermute | solution.py:772
  10.3 0.1 pad_add_fusion.place
  10.3 4.8 %shard_map.87 = (f32[3,8,4,8,128]{4,3,2,1,0:T(8,128)S(1)}, f32[3,4,8,4,8,128]{5,4,3,2,1,0:T(8,128)S(1)}, bf16[36,11376]{1,0:T(8,128)(2,1)S(1)}, bf16[36,288]{1,0:T(8,128)(2,1)S(1)}) custom-call(f32[3,8,4,8,128]{4,3,2,1,0:T(8,128)S(1)} %bitcast.12, f32[8,4,8,128]{3,2,1,0:T(8,128)S(1)} %bitcast.15, bf16[36,11376]{1,0:T(8,128)(2,1)} %far_hbm.1, ...), custom_call_target="tpu_custom_call" | custom-call | tf_op jit(solution)/shard_map/pallas_call | solution.py:343
  15.1 0.6 %shard_map.88.matrix = bf16[3,432,1024]{2,1,0:T(8,128)(2,1)S(1)} custom-call(bf16[36,11376]{1,0:T(8,128)(2,1)S(1)} %get-tuple-element.38.far_ref), custom_call_target="tpu_custom_call" | custom-call | tf_op jit(solution)/shard_map/pallas_call | solution.py:39
  15.7 0.1 collective-permute-done.2.two
  15.8 0.7 %shard_map.89 = (bf16[624,128]{1,0:T(8,128)(2,1)S(1)}, bf16[624,128]{1,0:T(8,128)(2,1)S(1)}) custom-call(s32[2]{0:T(128)S(1)} %pad_add_fusion.place, bf16[624,128]{1,0:T(8,128)(2,1)S(1)} %collective-permute-done.below, bf16[624,128]{1,0:T(8,128)(2,1)S(1)} %collective-permute-done.1.above, bf16[40,128]{1,0:T(8,128)(2,1)S(1)} %collective-permute-done.2.two, ...), custom_call_target="tpu_custom_call" | custom-call | tf_op jit(solution)/shard_map/pallas_call | solution.py:39
  16.5 2.0 %collective-permute-start.3 = (bf16[624,128]{1,0:T(8,128)(2,1)S(1)}, bf16[624,128]{1,0:T(8,128)(2,1)S(1)}, u32[]{:S(2)}, u32[]{:S(2)}) collective-permute-start(bf16[624,128]{1,0:T(8,128)(2,1)S(1)} %get-tuple-element.43), channel_id=1, source_target_pairs={{0,4},{1,5},{2,6},{3,7},{4,8},{5,9},{6,10},{7,11},{8,12},{9,13},{1... | collective-permute-start | bytes 479240 | tf_op jit(solution)/shard_map/ppermute | solution.py:772
  18.5 0.0 collective-permute-start.4
  18.5 0.0 collective-permute-done.6.high
  18.5 3.6 %shard_map.90 = f32[8,4,8,128]{3,2,1,0:T(8,128)S(1)} custom-call(f32[3,8,4,8,128]{4,3,2,1,0:T(8,128)S(1)} %get-tuple-element.45.sums_ref, f32[3,4,8,4,8,128]{5,4,3,2,1,0:T(8,128)S(1)} %get-tuple-element.46.shifted_ref, f32[3,8,4,8,128]{4,3,2,1,0:T(8,128)S(1)} %bitcast.13, bf16[1168,128]{1,0:T(8,128)(2,1)S(1)} %collective-permute-done.5.low, ...), custom_call_target="tpu_custom_call" | custom-call | tf_op jit(solution)/shard_map/pallas_call | solution.py:39
  22.2 0.0 collective-permute-done.3.low_corner
  22.2 2.7 %collective-permute-done.4.high_corner = bf16[624,128]{1,0:T(8,128)(2,1)S(1)} collective-permute-done((bf16[624,128]{1,0:T(8,128)(2,1)S(1)}, bf16[624,128]{1,0:T(8,128)(2,1)S(1)}, u32[]{:S(2)}, u32[]{:S(2)}) %collective-permute-start.4) | collective-permute-done | bytes 159776 | tf_op jit(solution)/shard_map/ppermute | solution.py:772
  24.9 0.1 collective-permute-start.8
  25.0 2.0 %collective-permute-start.7 = (bf16[240,128]{1,0:T(8,128)(2,1)S(1)}, bf16[240,128]{1,0:T(8,128)(2,1)S(1)}, u32[]{:S(2)}, u32[]{:S(2)}) collective-permute-start(bf16[240,128]{1,0:T(8,128)(2,1)S(1)} %pad_maximum_fusion.near_three), channel_id=1, source_target_pairs={{0,12},{1,13},{2,14},{3,15},{4,16},{5,17},{6,18},{7,19},{8,20},{9,... | collective-permute-start | bytes 184328 | tf_op jit(solution)/shard_map/ppermute | solution.py:772
  27.0 1.9 %shard_map.91 = f32[256,128]{1,0:T(8,128)} custom-call(f32[256,128]{1,0:T(8,128)S(1)} %bitcast.14, f32[768,128]{1,0:T(8,128)S(1)} %get-tuple-element.35.pos_ref, s32[32,128]{1,0:T(8,128)S(1)} %get-tuple-element.52.count_ref, bf16[624,128]{1,0:T(8,128)(2,1)S(1)} %collective-permute-done.below, bf16[624,128]{1,0:T(8,128)(2,1)S(1)} %collective-permute-done.1.above, ...), custom_call_target="tpu_custom_call" | custom-call | tf_op jit(solution)/shard_map/pallas_call | solution.py:39
  28.9 2.0 %shard_map.92.middle = f32[2,1024,256]{2,1,0:T(8,128)S(1)} custom-call(bf16[3,432,1024]{2,1,0:T(8,128)(2,1)S(1)} %shard_map.88.matrix, bf16[1152,128]{1,0:T(8,128)(2,1)S(1)} %get-tuple-element.54.grid_ref, bf16[1168,128]{1,0:T(8,128)(2,1)S(1)} %collective-permute-done.5.low, bf16[1168,128]{1,0:T(8,128)(2,1)S(1)} %collective-permute-done.6.high), custom_call_target="tpu_custom_call" | custom-call | tf_op jit(solution)/shard_map/pallas_call | solution.py:39
  30.9 0.0 collective-permute-done.8.down_three
  30.9 0.0 collective-permute-done.7.up_three
  30.9 7.6 %shard_map.93 = f32[1152,128]{1,0:T(8,128)} custom-call(s32[2]{0:T(128)S(1)} %pad_add_fusion.place, bf16[3,432,1024]{2,1,0:T(8,128)(2,1)S(1)} %shard_map.88.matrix, f32[2,1024,256]{2,1,0:T(8,128)S(1)} %shard_map.92.middle, bf16[1152,128]{1,0:T(8,128)(2,1)S(1)} %get-tuple-element.54.grid_ref, bf16[144,128]{1,0:T(8,128)(2,1)S(1)} %get-tuple-element.56.six_ref, ...), custom_call_target="tpu_custom_call" | custom-call | tf_op jit(solution)/shard_map/pallas_call | solution.py:39
  (7 shorter events, 0.0 us)
Async XLA Ops:
  3.3 12.5 %collective-permute-start = (bf16[624,128]{1,0:T(8,128)(2,1)S(1)}, bf16[624,128]{1,0:T(8,128)(2,1)S(1)}, u32[]{:S(2)}, u32[]{:S(2)}) collective-permute-start(bf16[624,128]{1,0:T(8,128)(2,1)S(1)} %get-tuple-element.32), channel_id=1, source_target_pairs={{0,1},{1,2},{2,3},{3,0},{4,5},{5,6},{6,7},{7,4},{8,9},{9,10},{10,1... | collective-permute-start | bytes 479240 | tf_op jit(solution)/shard_map/ppermute | solution.py:772
  5.4 10.4 %collective-permute-start.1 = (bf16[624,128]{1,0:T(8,128)(2,1)S(1)}, bf16[624,128]{1,0:T(8,128)(2,1)S(1)}, u32[]{:S(2)}, u32[]{:S(2)}) collective-permute-start(bf16[624,128]{1,0:T(8,128)(2,1)S(1)} %get-tuple-element.33), channel_id=1, source_target_pairs={{0,3},{1,0},{2,1},{3,2},{4,7},{5,4},{6,5},{7,6},{8,11},{9,8},{10,9... | collective-permute-start | bytes 479240 | tf_op jit(solution)/shard_map/ppermute | solution.py:772
  7.5 11.0 %collective-permute-start.5 = (bf16[1168,128]{1,0:T(8,128)(2,1)S(1)}, bf16[1168,128]{1,0:T(8,128)(2,1)S(1)}, u32[]{:S(2)}, u32[]{:S(2)}) collective-permute-start(bf16[1168,128]{1,0:T(8,128)(2,1)S(1)} %get-tuple-element.47), channel_id=1, source_target_pairs={{0,4},{1,5},{2,6},{3,7},{4,8},{5,9},{6,10},{7,11},{8,12},{9,13},{1... | collective-permute-start | bytes 897032 | tf_op jit(solution)/shard_map/ppermute | solution.py:772
  9.7 8.8 %collective-permute-start.6 = (bf16[1168,128]{1,0:T(8,128)(2,1)S(1)}, bf16[1168,128]{1,0:T(8,128)(2,1)S(1)}, u32[]{:S(2)}, u32[]{:S(2)}) collective-permute-start(bf16[1168,128]{1,0:T(8,128)(2,1)S(1)} %get-tuple-element.48), channel_id=1, source_target_pairs={{0,28},{1,29},{2,30},{3,31},{4,0},{5,1},{6,2},{7,3},{8,4},{9,5},{1... | collective-permute-start | bytes 897032 | tf_op jit(solution)/shard_map/ppermute | solution.py:772
  9.7 6.1 %collective-permute-start.2 = (bf16[40,128]{1,0:T(8,128)(2,1)S(1)}, bf16[40,128]{1,0:T(8,128)(2,1)S(1)}, u32[]{:S(2)}, u32[]{:S(2)}) collective-permute-start(bf16[40,128]{1,0:T(8,128)(2,1)S(1)} %get-tuple-element.34.own), channel_id=1, source_target_pairs={{0,2},{1,3},{2,0},{3,1},{4,6},{5,7},{6,4},{7,5},{8,10},{9,11},{10,... | collective-permute-start | bytes 30728 | tf_op jit(solution)/shard_map/ppermute | solution.py:772
  16.5 5.7 %collective-permute-start.3 = (bf16[624,128]{1,0:T(8,128)(2,1)S(1)}, bf16[624,128]{1,0:T(8,128)(2,1)S(1)}, u32[]{:S(2)}, u32[]{:S(2)}) collective-permute-start(bf16[624,128]{1,0:T(8,128)(2,1)S(1)} %get-tuple-element.43), channel_id=1, source_target_pairs={{0,4},{1,5},{2,6},{3,7},{4,8},{5,9},{6,10},{7,11},{8,12},{9,13},{1... | collective-permute-start | bytes 479240 | tf_op jit(solution)/shard_map/ppermute | solution.py:772
  18.5 6.3 %collective-permute-start.4 = (bf16[624,128]{1,0:T(8,128)(2,1)S(1)}, bf16[624,128]{1,0:T(8,128)(2,1)S(1)}, u32[]{:S(2)}, u32[]{:S(2)}) collective-permute-start(bf16[624,128]{1,0:T(8,128)(2,1)S(1)} %get-tuple-element.44), channel_id=1, source_target_pairs={{0,28},{1,29},{2,30},{3,31},{4,0},{5,1},{6,2},{7,3},{8,4},{9,5},{1... | collective-permute-start | bytes 479240 | tf_op jit(solution)/shard_map/ppermute | solution.py:772
  24.9 6.0 %collective-permute-start.8 = (bf16[240,128]{1,0:T(8,128)(2,1)S(1)}, bf16[240,128]{1,0:T(8,128)(2,1)S(1)}, u32[]{:S(2)}, u32[]{:S(2)}) collective-permute-start(bf16[240,128]{1,0:T(8,128)(2,1)S(1)} %pad_maximum_fusion.near_three), channel_id=1, source_target_pairs={{0,20},{1,21},{2,22},{3,23},{4,24},{5,25},{6,26},{7,27},{8,28},{9,... | collective-permute-start | bytes 184328 | tf_op jit(solution)/shard_map/ppermute | solution.py:772
  25.0 5.9 %collective-permute-start.7 = (bf16[240,128]{1,0:T(8,128)(2,1)S(1)}, bf16[240,128]{1,0:T(8,128)(2,1)S(1)}, u32[]{:S(2)}, u32[]{:S(2)}) collective-permute-start(bf16[240,128]{1,0:T(8,128)(2,1)S(1)} %pad_maximum_fusion.near_three), channel_id=1, source_target_pairs={{0,12},{1,13},{2,14},{3,15},{4,16},{5,17},{6,18},{7,19},{8,20},{9,... | collective-permute-start | bytes 184328 | tf_op jit(solution)/shard_map/ppermute | solution.py:772

commit v4 on v3

--- a/solution.py
+++ b/solution.py
@@ -35,12 +35,12 @@
     return jax.ShapeDtypeStruct(dims, dtype)
 
 
-def kernel_call(body, outs, inputs, scratch=(), scalars=0, space=VMEM, limit=20):
+def kernel_call(body, outs, inputs, scratch=(), scalars=0, space=VMEM, target=VMEM, limit=20):
     return pl.pallas_call(
         body,
         out_shape=outs,
         in_specs=[SMEM] * scalars + [space] * (len(inputs) - scalars),
-        out_specs=[VMEM] * len(outs),
+        out_specs=[target] * len(outs),
         scratch_shapes=list(scratch),
         compiler_params=pltpu.CompilerParams(vmem_limit_bytes=limit * 1024 * 1024),
     )(*inputs)
@@ -66,6 +66,10 @@
     return jnp.where(mask, F32(1.0), F32(0.0)).astype(BF16)
 
 
+def pick(rows, source):
+    return one_hot(iota((rows, source.shape[1]), 0) == source)
+
+
 def parts(value):
     high = value.astype(BF16)
     return high, (value - high.astype(F32)).astype(BF16)
@@ -76,18 +80,18 @@
 
 
 def up_blocks(up_ref):
-    row, col = iota((8 * COEF, GROUP), 0), iota((8 * COEF, GROUP), 1)
+    col = iota((1, GROUP), 1)
+    block = jnp.where(col < 2 * COEF, jnp.where(col < COEF, 0, 1), jnp.where(col < 3 * COEF, 2, 3))
     return [
-        dot(up_ref[...], one_hot(row == (col // COEF * 2 + bit) * COEF + col % COEF)).astype(BF16)
-        for bit in range(2)
+        dot(up_ref[...], pick(8 * COEF, col + (block + bit) * COEF)).astype(BF16) for bit in range(2)
     ]
 
 
 def prep_kernel(
     leaf_hbm, pos_hbm, mass_hbm, count_hbm, up_hbm,
     grid_ref, up_msg, down_msg, low_msg, high_msg, six_ref, five_ref, live_ref,
-    pos_ref, count_ref, up_ref,
-    leaf_ref, mass_ref, m32, x32, six32, near32, sems,
+    pos_ref, count_ref, halves_ref,
+    up_ref, leaf_ref, mass_ref, m32, x32, six32, near32, sems,
 ):
     copies = [
         pltpu.make_async_copy(source, target, sems.at[k])
@@ -101,12 +105,12 @@
     for copy in copies:
         copy.start()
     copies[0].wait()
-    m32[...] = leaf_ref[...].astype(F32)
+    m32[0:1152, :] = leaf_ref[...].astype(F32)
     for x in range(4):
         for y in range(8):
             start = ((x // 2) * 4 + y // 2) * GROUP + (2 * (x % 2) + y % 2) * COEF
             x32[start : start + COEF, :] = m32[pl.ds(x * 8 + y, COEF, stride=32), :]
-    grid = x32[...].astype(BF16)
+    grid = x32[0:1152, :].astype(BF16)
     grid_ref[...] = grid
     for msg, parent in ((up_msg, 3), (down_msg, 0)):
         for xp in range(2):
@@ -144,8 +148,9 @@
             msg[256 + 24 * y : 280 + 24 * y, :] = low[32 * y : 32 * y + 24]
     low_half = iota((COEF, 128), 1) < 64
     even_up, odd_up = up_blocks(up_ref)
-    row, col = iota((128, 128), 0), iota((128, 128), 1)
-    split_z = one_hot(row == 2 * (col % 64) + col // 64)
+    halves_ref[0], halves_ref[1] = even_up, odd_up
+    col = iota((1, 128), 1)
+    split_z = pick(128, 2 * (col % 64) + col // 64)
     split = dot(grid, split_z).astype(BF16)
     columns = jnp.concatenate([split[k * GROUP : (k + 1) * GROUP] for k in range(8)], axis=1)
     even, odd = dot(even_up, columns), dot(odd_up, columns)
@@ -156,7 +161,7 @@
             far_part = lane_roll(even[:, second : second + 128], 64) + odd[:, second : second + 128]
             start = (2 * xp + y) * COEF
             six32[start : start + COEF, :] = jnp.where(low_half, near_part, far_part)
-    six = six32[...].astype(BF16)
+    six = six32[0:GROUP, :].astype(BF16)
     six_ref[...] = six
     low_msg[X_SIX:X_ROWS, :] = six
     high_msg[X_SIX:X_ROWS, :] = six
@@ -164,7 +169,7 @@
     first, second = six32[0:72, :], six32[72:144, :]
     up_msg[Y_SIX:Y_FIVE, :] = jnp.where(left, lane_roll(first, 64), second).astype(BF16)
     down_msg[Y_SIX:Y_FIVE, :] = jnp.where(left, first, lane_roll(second, 64)).astype(BF16)
-    split_six = one_hot(row == ((col // 32) % 2) * 64 + 2 * (col % 32) + col // 64)
+    split_six = pick(128, ((col // 32) % 2) * 64 + 2 * (col % 32) + col // 64)
     split = dot(six, split_six).astype(BF16)
     five = dot(even_up, split) + lane_roll(dot(odd_up, split), 64)
     five = jnp.concatenate([five, jnp.zeros((4, 128), F32)], axis=0).astype(BF16)
@@ -192,15 +197,16 @@
             shape((256, 128), F32),
             shape((768, 128), F32),
             shape((32, 128), jnp.int32),
-            shape(up_operator.shape, BF16),
+            shape((2, COEF, GROUP), BF16),
         ),
         [in_hbm(value) for value in inputs],
         (
+            pltpu.VMEM(up_operator.shape, BF16),
             pltpu.VMEM((1152, 128), BF16),
             pltpu.VMEM((256, 128), F32),
-            pltpu.VMEM((1152, 128), F32),
-            pltpu.VMEM((1152, 128), F32),
-            pltpu.VMEM((GROUP, 128), F32),
+            pltpu.VMEM((1280, 128), F32),
+            pltpu.VMEM((1160, 128), F32),
+            pltpu.VMEM((GROUP + 8, 128), F32),
             pltpu.VMEM((256, 128), F32),
             pltpu.SemaphoreType.DMA((5,)),
         ),
@@ -384,7 +390,7 @@
 
 def rows_kernel(
     inner_ref, pos_ref, count_ref, below, above, low_corner, high_corner, out_ref,
-    sources, shifted, added,
+    sources, shifted, added, places,
 ):
     turn = jnp.where(iota((8, 128), 0) >= 4, F32(1.0), F32(-1.0))
     for side, msg in enumerate((below, above)):
@@ -395,13 +401,14 @@
         sources[0, first + 32 : first + 128, :] = sources[1, first : first + 96, :]
         sources[2, first : first + 96, :] = sources[1, first + 32 : first + 128, :]
         joined(sources.at[2, pl.ds(first + 96, 32)], high_corner, high, high + 32, 1)
+    places[0:768, :] = pos_ref[...]
     goals = []
     for slot in range(8):
         at = [(axis * 8 + slot) * 32 for axis in range(3)]
         goals.append(
             [
                 jnp.concatenate(
-                    [pos_ref[pl.ds(a, 4, stride=8), :], pos_ref[pl.ds(a + 7, 4, stride=8), :]], axis=0
+                    [places[pl.ds(a, 4, stride=8), :], places[pl.ds(a + 7, 4, stride=8), :]], axis=0
                 )
                 for a in at
             ]
@@ -469,7 +476,8 @@
         (
             pltpu.VMEM((3, 256, 128), F32),
             pltpu.VMEM((3, 4, 8, 8, 128), F32),
-            pltpu.VMEM((256, 128), F32),
+            pltpu.VMEM((320, 128), F32),
+            pltpu.VMEM((832, 128), F32),
         ),
     )[0]
 
@@ -497,14 +505,14 @@
 
 
 def operator_kernel(far_ref, out_ref, far32, stack):
-    far32[:, 0:11264] = far_ref[:, 0:11264].astype(F32)
-    far32[:, 11264:11520] = jnp.zeros((COEF, 256), F32)
-    far32[:, 11264:11376] = far_ref[:, 11264:11376].astype(F32)
+    far32[0:COEF, 0:11264] = far_ref[:, 0:11264].astype(F32)
+    far32[:, 11264:11520] = jnp.zeros((40, 256), F32)
+    far32[0:COEF, 11264:11376] = far_ref[:, 11264:11376].astype(F32)
     lane = iota((COEF, 256), 1)
 
     def window(start):
         base = start // 128 * 128
-        value = far32[:, base : base + 384]
+        value = far32[0:COEF, base : base + 384]
         shift = start - base
         return (pltpu.roll(value, 384 - shift, 1) if shift else value)[:, 0:256]
 
@@ -531,7 +539,7 @@
                         first = shift_y * GROUP + (2 * child_x + child_y) * COEF
                         bits = (2 * bit_x + bit_y) * 256
                         stack[shift_x, first : first + COEF, bits : bits + 256] = block
-    out_ref[...] = stack[...].astype(BF16)
+    out_ref[...] = stack[:, 0 : 3 * GROUP, :].astype(BF16)
 
 
 def far_matrix(far_operator):
@@ -539,7 +547,7 @@
         operator_kernel,
         (shape((3, 3 * GROUP, 1024), BF16),),
         (far_operator,),
-        (pltpu.VMEM((COEF, 11520), F32), pltpu.VMEM((3, 3 * GROUP, 1024), F32)),
+        (pltpu.VMEM((40, 11520), F32), pltpu.VMEM((3, 3 * GROUP + 8, 1024), F32)),
     )[0]
 
 
@@ -590,11 +598,12 @@
 
 def levels_kernel(
     place, matrix, middle, grid_ref, six_ref, below, above, low, high, low_corner, high_corner,
-    near_three, up_three, down_three, up_ref, down_ref, out_ref,
+    near_three, up_three, down_three, halves_ref, down_ref, out_ref,
     cells, fives, fours, three32, windows, products, coarse, down32, downs, expand, lifted,
+    leaving, sems,
 ):
     gx, gy = place[0], place[1]
-    row, col = iota((128, 128), 0), iota((128, 128), 1)
+    col = iota((1, 128), 1)
 
     for first, msg, corner in ((0, low, low_corner), (384, high, high_corner)):
         lanes = slice(first, first + 128)
@@ -624,7 +633,7 @@
     ):
         at = pl.multiple_of(lax.rem(gx + shift + size, size) * 72, 8)
         fives[pl.ds(at, 72), :] = msg[first : first + 72, :].astype(F32)
-    even_up, odd_up = up_blocks(up_ref)
+    even_up, odd_up = halves_ref[0], halves_ref[1]
     leaf_products()
 
     def upward(grouped, split):
@@ -633,8 +642,8 @@
         return value.astype(BF16).astype(F32)
 
     lane = col % 64
-    split_five = one_hot(
-        (row == ((lane // 16 % 2) * 2 + lane // 32) * 32 + 2 * (lane % 16) + col // 64)
+    split_five = pick(
+        128, ((lane // 16 % 2) * 2 + lane // 32) * 32 + 2 * (lane % 16) + col // 64
     )
     for x in range(4):
         value = upward(fives[x * GROUP : (x + 1) * GROUP, :], split_five)
@@ -642,18 +651,22 @@
         fours[first : first + COEF, :] = value
         fours[first + COEF : first + 2 * COEF, :] = lane_roll(value, 96)
     leaf_products()
-    split_four = one_hot((row == (lane // 8) * 16 + 2 * (lane % 8) + col // 64) & (lane < 16))
+    split_four = pick(
+        128, jnp.where(lane < 16, (lane // 8) * 16 + 2 * (lane % 8) + col // 64, -1)
+    )
     for x in range(2):
         value = upward(fours[x * GROUP : (x + 1) * GROUP, :], split_four)
         three32[x * 2 * COEF : x * 2 * COEF + COEF, :] = value
         three32[x * 2 * COEF + COEF : (x + 1) * 2 * COEF, :] = lane_roll(value, 120)
     leaf_products()
     def wrapped(first, base, size):
-        cell = lax.rem(col - first - 3 + size, size)
-        return one_hot((row == base + cell) & (col >= first) & (col < first + size + 6))
-
-    three = dot(three32[...].astype(BF16), wrapped(92, 0, 8))
+        cell = (col - first - 3 + size) & (size - 1)
+        return pick(128, jnp.where((col >= first) & (col < first + size + 6), base + cell, -1))
+
+    three = dot(three32[0:GROUP, :].astype(BF16), wrapped(92, 0, 8))
     six_lanes = [wrapped(0, 0, 64), wrapped(0, 64, 64)]
+    five_lanes = [wrapped(70, lax.rem(gy + step + 3, 4) * 32, 32) for step in range(3)]
+    four_lanes = [wrapped(70, lax.rem(gy // 2 + step + 1, 2) * 16, 16) for step in range(3)]
     for shift_x in range(3):
         if shift_x == 1:
             own, other = six_ref[...], halo_six(below, above).astype(BF16)
@@ -667,10 +680,8 @@
         for shift_y in range(3):
             left = dot(other if shift_y == 0 else own, six_lanes[0 if shift_y == 1 else 1])
             right = dot(other if shift_y == 2 else own, six_lanes[1 if shift_y == 1 else 0])
-            y_five = lax.rem(gy + shift_y + 3, 4)
-            y_four = lax.rem(gy // 2 + shift_y + 1, 2)
-            left = left + dot(five, wrapped(70, y_five * 32, 32))
-            right = right + dot(four, wrapped(70, y_four * 16, 16)) + three
+            left = left + dot(five, five_lanes[shift_y])
+            right = right + dot(four, four_lanes[shift_y]) + three
             rows = slice(shift_y * GROUP, (shift_y + 1) * GROUP)
             windows[shift_x, rows, 0:128] = left.astype(BF16)
             windows[shift_x, rows, 128:256] = right.astype(BF16)
@@ -682,8 +693,8 @@
     for bits in range(4):
         for lanes in (slice(0, 128), slice(128, 256)):
             coarse[bits * 40 : bits * 40 + COEF, lanes] = z_sum(products.at[0], bits, lanes, 1)
-    eye = one_hot(iota((8 * COEF, 8 * COEF), 0) == iota((8 * COEF, 8 * COEF), 1))
-    down32[...] = dot_nt(eye, down_ref[...])
+    eye = pick(8 * COEF, iota((1, 8 * COEF), 1))
+    down32[0 : 8 * COEF, :] = dot_nt(eye, down_ref[...])
     downs[...] = jnp.zeros_like(downs)
     for bits in range(4):
         for bit in range(2):
@@ -691,8 +702,10 @@
             downs[bit, bits * 40 : bits * 40 + COEF, :] = down32[first : first + COEF, :]
     operators = [downs[bit].astype(BF16) for bit in range(2)]
 
-    def spread(value, mask):
-        return [dot(part, one_hot(mask)).astype(BF16) for part in parts(value)]
+    def spread(value, first, start, count):
+        inside = (col >= start) & (col < start + count)
+        taken = pick(128, jnp.where(inside, first + (col - start) // 2, -1))
+        return [dot(part, taken).astype(BF16) for part in parts(value)]
 
     def lift(wide, lanes, first):
         halves = [dot(value, wide[0]) + dot(value, wide[1]) for value in operators]
@@ -705,60 +718,71 @@
     left, right, both = slice(0, 128), slice(128, 256), slice(0, 256)
     bits = 2 * lax.rem(gx // 4, 2) + lax.rem(gy // 2, 2)
     value = coarse[block(bits), right]
-    wide = spread(value, (row == 95 + (col - 73) // 2) & (col >= 73) & (col < 89))
+    wide = spread(value, 95, 73, 16)
     lift(wide, left, 1)
     leaf_products()
     bits = 2 * lax.rem(gx // 2, 2) + lax.rem(gy, 2)
     value = coarse[block(bits), right] + lifted[block(bits), left]
-    wide = spread(value, (row == 73 + (col - 73) // 2) & (col >= 73) & (col < 105))
+    wide = spread(value, 73, 73, 32)
     lift(wide, left, 1)
     leaf_products()
     wides = []
     for y in range(2):
         bits = 2 * lax.rem(gx, 2) + y
         value = coarse[block(bits), left] + lifted[block(bits), left]
-        wides.append(spread(value, (row == 73 + (col - 3) // 2) & (col >= 3) & (col < 67)))
+        wides.append(spread(value, 73, 3, 64))
     lift([jnp.concatenate(pair, axis=1) for pair in zip(*wides)], both, 1)
     leaf_products()
-    doubled = one_hot(row == 3 + col // 2)
+    doubled = pick(128, 3 + col // 2)
     for k, part in enumerate(parts(coarse[...] + lifted[:, both])):
         for y in range(2):
             wide = dot(part[:, y * 128 : y * 128 + 128], doubled)
             for bits in range(4):
                 at = ((bits // 2) * 4 + 2 * y + bits % 2) * 128
-                expand[k, :, at : at + 128] = wide[bits * 40 : bits * 40 + COEF].astype(BF16)
+                expand[k, 0:COEF, at : at + 128] = wide[bits * 40 : bits * 40 + COEF].astype(BF16)
     leaf_products(8)
-    lift([expand[k] for k in range(2)], slice(0, 1024), 0)
-    for parent in range(4):
-        source = middle.at[parent - 1] if parent in (1, 2) else products.at[1 + parent // 3]
-        for xp in range(2):
+    lift([expand[k, 0:COEF, :] for k in range(2)], slice(0, 1024), 0)
+    copies = []
+    for x in range(4):
+        xp = x // 2
+        for y in range(8):
+            parent, bits = y // 2, 2 * (x % 2) + y % 2
+            source = middle.at[parent - 1] if parent in (1, 2) else products.at[1 + parent // 3]
+            value = z_sum(source, bits, slice(xp * 128, xp * 128 + 128), 0)
             at = (xp * 4 + parent) * 128
-            for bits in range(4):
-                value = z_sum(source, bits, slice(xp * 128, xp * 128 + 128), 0)
-                x, y = 2 * xp + bits // 2, 2 * parent + bits % 2
-                rows = pl.ds(x * 8 + y, COEF, stride=32)
-                out_ref[rows, :] = value + lifted[block(bits), at : at + 128]
+            leaving[x, pl.ds(y, COEF, stride=8), :] = value + lifted[block(bits), at : at + 128]
+        copies.append(
+            pltpu.make_async_copy(
+                leaving.at[x, pl.ds(0, 8 * COEF)].reshape(COEF, 8, 128), out_ref.at[:, x], sems.at[x]
+            )
+        )
+        copies[-1].start()
+    for copy in copies:
+        copy.wait()
 
 
 def all_levels(*inputs):
     return kernel_call(
         levels_kernel,
-        (shape((1152, 128), F32),),
+        (shape((COEF, 4, 8, 128), F32),),
         inputs,
         (
             pltpu.VMEM((6 * GROUP, 512), BF16),
             pltpu.VMEM((576, 128), F32),
-            pltpu.VMEM((2 * GROUP, 128), F32),
-            pltpu.VMEM((GROUP, 128), F32),
+            pltpu.VMEM((2 * GROUP + 8, 128), F32),
+            pltpu.VMEM((GROUP + 8, 128), F32),
             pltpu.VMEM((3, 3 * GROUP, 256), BF16),
             pltpu.VMEM((3, 1024, 256), F32),
             pltpu.VMEM((160, 256), F32),
-            pltpu.VMEM((8 * COEF, COEF), F32),
+            pltpu.VMEM((8 * COEF + 8, COEF), F32),
             pltpu.VMEM((2, 160, COEF), F32),
-            pltpu.VMEM((2, COEF, 1024), BF16),
+            pltpu.VMEM((2, 40, 1024), BF16),
             pltpu.VMEM((160, 1024), F32),
+            pltpu.VMEM((4, 8 * COEF + 32, 128), F32),
+            pltpu.SemaphoreType.DMA((4,)),
         ),
         scalars=1,
+        target=HBM,
     )[0]
 
 
@@ -778,7 +802,7 @@
     place = jnp.stack([lax.axis_index("gx"), lax.axis_index("gy")]).astype(jnp.int32)
     (
         grid, up_msg, down_msg, low_msg, high_msg, six, five, live,
-        positions, counts, up_operator,
+        positions, counts, up_halves,
     ) = prepare(
         leaf_multipoles.reshape(1152, 128), positions.reshape(768, 128), masses.reshape(256, 128),
         counts.reshape(32, 128), up_operator.T,
@@ -807,9 +831,9 @@
     )
     expansion = all_levels(
         place, matrix, middle, grid, six, below, above, low, high, low_corner, high_corner,
-        three, up_three, down_three, up_operator, down_operator,
-    )
-    return expansion.reshape(36, 4, 8, 128), potential.reshape(8, 4, 8, 128)
+        three, up_three, down_three, up_halves, down_operator,
+    )
+    return expansion, potential.reshape(8, 4, 8, 128)
 
 
 def extended(cells, sides, width):

time: 38.6 us -> 38.5 us (level)
  Pallas kernels: 23.8 us -> 23.4 us
  transfers between devices with their start and end apart: 9 -> 9, of which waited for: 2 -> 2; matrix products, arithmetic and copies ran while one was open for 0% -> 0% of each run, Pallas kernels for 35% -> 36%
where the time goes in v4:
time: 38.5 us; the launch traced here: 38.3 us
  Pallas kernels  23.4 us (61%)
  starting transfers between devices  11.2 us (29%)
  waiting for transfers between devices  2.75 us (7%)
  between operations  0.88 us (2%)
    pallas_call x7, Pallas kernels, kernel_call(): pl.pallas_call(body, out_shape=outs, in_specs=[SMEM] * scalars + [space]...  18.7 us
    ppermute x9, starting transfers between devices, moved(): return lax.ppermute(value, ('gx', 'gy'), table)  11.2 us
    pallas_call x1, Pallas kernels, plane_pairs(): pl.pallas_call(plane_kernel, out_shape=(shape((3, 8, 4, 8, 128), F32), sh...  4.77 us
    ppermute x9, waiting for transfers between devices, moved(): return lax.ppermute(value, ('gx', 'gy'), table)  2.75 us
  transfers between devices with their start and end apart: 9, of which 2 were waited for; matrix products, arithmetic and copies ran while one was open for 0% of the time, Pallas kernels for 36%

profile of v4, /device:TPU:1, one launch (start us, length us, event | category | flops | bytes accessed | tf_op | source)
XLA Modules:
  0.0 38.3 jit_solution(11883419057354560526)
XLA Ops:
  0.6 2.7 %shard_map.86 = (bf16[1152,128]{1,0:T(8,128)(2,1)S(1)}, bf16[624,128]{1,0:T(8,128)(2,1)S(1)}, bf16[624,128]{1,0:T(8,128)(2,1)S(1)}, bf16[1168,128]{1,0:T(8,128)(...) custom-call(bf16[1152,128]{1,0:T(8,128)(2,1)} %bitcast.16, ...), custom_call_target="tpu_custom_call" | custom-call | tf_op jit(solution)/shard_map/pallas_call | solution.py:39
  3.3 2.2 %collective-permute-start = (bf16[624,128]{1,0:T(8,128)(2,1)S(1)}, bf16[624,128]{1,0:T(8,128)(2,1)S(1)}, u32[]{:S(2)}, u32[]{:S(2)}) collective-permute-start(bf16[624,128]{1,0:T(8,128)(2,1)S(1)} %get-tuple-element.32), channel_id=1, source_target_pairs={{0,1},{1,2},{2,3},{3,0},{4,5},{5,6},{6,7},{7,4},{8,9},{9,10},{10,1... | collective-permute-start | bytes 479240 | tf_op jit(solution)/shard_map/ppermute | solution.py:796
  5.5 2.1 %collective-permute-start.1 = (bf16[624,128]{1,0:T(8,128)(2,1)S(1)}, bf16[624,128]{1,0:T(8,128)(2,1)S(1)}, u32[]{:S(2)}, u32[]{:S(2)}) collective-permute-start(bf16[624,128]{1,0:T(8,128)(2,1)S(1)} %get-tuple-element.33), channel_id=1, source_target_pairs={{0,3},{1,0},{2,1},{3,2},{4,7},{5,4},{6,5},{7,6},{8,11},{9,8},{10,9... | collective-permute-start | bytes 479240 | tf_op jit(solution)/shard_map/ppermute | solution.py:796
  7.6 2.2 %collective-permute-start.5 = (bf16[1168,128]{1,0:T(8,128)(2,1)S(1)}, bf16[1168,128]{1,0:T(8,128)(2,1)S(1)}, u32[]{:S(2)}, u32[]{:S(2)}) collective-permute-start(bf16[1168,128]{1,0:T(8,128)(2,1)S(1)} %get-tuple-element.47), channel_id=1, source_target_pairs={{0,4},{1,5},{2,6},{3,7},{4,8},{5,9},{6,10},{7,11},{8,12},{9,13},{1... | collective-permute-start | bytes 897032 | tf_op jit(solution)/shard_map/ppermute | solution.py:796
  9.8 0.0 collective-permute-start.6
  9.8 0.5 %collective-permute-start.2 = (bf16[40,128]{1,0:T(8,128)(2,1)S(1)}, bf16[40,128]{1,0:T(8,128)(2,1)S(1)}, u32[]{:S(2)}, u32[]{:S(2)}) collective-permute-start(bf16[40,128]{1,0:T(8,128)(2,1)S(1)} %get-tuple-element.34.own), channel_id=1, source_target_pairs={{0,2},{1,3},{2,0},{3,1},{4,6},{5,7},{6,4},{7,5},{8,10},{9,11},{10,... | collective-permute-start | bytes 30728 | tf_op jit(solution)/shard_map/ppermute | solution.py:796
  10.3 0.1 pad_add_fusion.place
  10.4 4.8 %shard_map.87 = (f32[3,8,4,8,128]{4,3,2,1,0:T(8,128)S(1)}, f32[3,4,8,4,8,128]{5,4,3,2,1,0:T(8,128)S(1)}, bf16[36,11376]{1,0:T(8,128)(2,1)S(1)}, bf16[36,288]{1,0:T(8,128)(2,1)S(1)}) custom-call(f32[3,8,4,8,128]{4,3,2,1,0:T(8,128)S(1)} %bitcast.11, f32[8,4,8,128]{3,2,1,0:T(8,128)S(1)} %bitcast.14, bf16[36,11376]{1,0:T(8,128)(2,1)} %far_hbm.1, ...), custom_call_target="tpu_custom_call" | custom-call | tf_op jit(solution)/shard_map/pallas_call | solution.py:349
  15.1 0.6 %shard_map.88.matrix = bf16[3,432,1024]{2,1,0:T(8,128)(2,1)S(1)} custom-call(bf16[36,11376]{1,0:T(8,128)(2,1)S(1)} %get-tuple-element.38.far_ref), custom_call_target="tpu_custom_call" | custom-call | tf_op jit(solution)/shard_map/pallas_call | solution.py:39
  15.8 0.1 collective-permute-done.2.two
  15.8 0.0 collective-permute-done.below
  15.8 0.0 collective-permute-done.1.above
  15.8 0.7 %shard_map.89 = (bf16[624,128]{1,0:T(8,128)(2,1)S(1)}, bf16[624,128]{1,0:T(8,128)(2,1)S(1)}) custom-call(s32[2]{0:T(128)S(1)} %pad_add_fusion.place, bf16[624,128]{1,0:T(8,128)(2,1)S(1)} %collective-permute-done.below, bf16[624,128]{1,0:T(8,128)(2,1)S(1)} %collective-permute-done.1.above, bf16[40,128]{1,0:T(8,128)(2,1)S(1)} %collective-permute-done.2.two, ...), custom_call_target="tpu_custom_call" | custom-call | tf_op jit(solution)/shard_map/pallas_call | solution.py:39
  16.5 2.0 %collective-permute-start.3 = (bf16[624,128]{1,0:T(8,128)(2,1)S(1)}, bf16[624,128]{1,0:T(8,128)(2,1)S(1)}, u32[]{:S(2)}, u32[]{:S(2)}) collective-permute-start(bf16[624,128]{1,0:T(8,128)(2,1)S(1)} %get-tuple-element.43), channel_id=1, source_target_pairs={{0,4},{1,5},{2,6},{3,7},{4,8},{5,9},{6,10},{7,11},{8,12},{9,13},{1... | collective-permute-start | bytes 479240 | tf_op jit(solution)/shard_map/ppermute | solution.py:796
  18.5 0.0 collective-permute-start.4
  18.5 0.0 collective-permute-done.5.low
  18.6 3.6 %shard_map.90 = f32[8,4,8,128]{3,2,1,0:T(8,128)S(1)} custom-call(f32[3,8,4,8,128]{4,3,2,1,0:T(8,128)S(1)} %get-tuple-element.45.sums_ref, f32[3,4,8,4,8,128]{5,4,3,2,1,0:T(8,128)S(1)} %get-tuple-element.46.shifted_ref, f32[3,8,4,8,128]{4,3,2,1,0:T(8,128)S(1)} %bitcast.12, bf16[1168,128]{1,0:T(8,128)(2,1)S(1)} %collective-permute-done.5.low, ...), custom_call_target="tpu_custom_call" | custom-call | tf_op jit(solution)/shard_map/pallas_call | solution.py:39
  22.2 2.7 %collective-permute-done.4.high_corner = bf16[624,128]{1,0:T(8,128)(2,1)S(1)} collective-permute-done((bf16[624,128]{1,0:T(8,128)(2,1)S(1)}, bf16[624,128]{1,0:T(8,128)(2,1)S(1)}, u32[]{:S(2)}, u32[]{:S(2)}) %collective-permute-start.4) | collective-permute-done | bytes 159776 | tf_op jit(solution)/shard_map/ppermute | solution.py:796
  24.9 0.1 collective-permute-start.8
  25.0 2.0 %collective-permute-start.7 = (bf16[240,128]{1,0:T(8,128)(2,1)S(1)}, bf16[240,128]{1,0:T(8,128)(2,1)S(1)}, u32[]{:S(2)}, u32[]{:S(2)}) collective-permute-start(bf16[240,128]{1,0:T(8,128)(2,1)S(1)} %pad_maximum_fusion.near_three), channel_id=1, source_target_pairs={{0,12},{1,13},{2,14},{3,15},{4,16},{5,17},{6,18},{7,19},{8,20},{9,... | collective-permute-start | bytes 184328 | tf_op jit(solution)/shard_map/ppermute | solution.py:796
  27.0 2.0 %shard_map.91 = f32[256,128]{1,0:T(8,128)} custom-call(f32[256,128]{1,0:T(8,128)S(1)} %bitcast.13, f32[768,128]{1,0:T(8,128)S(1)} %get-tuple-element.35.pos_ref, s32[32,128]{1,0:T(8,128)S(1)} %get-tuple-element.52.count_ref, bf16[624,128]{1,0:T(8,128)(2,1)S(1)} %collective-permute-done.below, bf16[624,128]{1,0:T(8,128)(2,1)S(1)} %collective-permute-done.1.above, ...), custom_call_target="tpu_custom_call" | custom-call | tf_op jit(solution)/shard_map/pallas_call | solution.py:39
  29.0 2.0 %shard_map.92.middle = f32[2,1024,256]{2,1,0:T(8,128)S(1)} custom-call(bf16[3,432,1024]{2,1,0:T(8,128)(2,1)S(1)} %shard_map.88.matrix, bf16[1152,128]{1,0:T(8,128)(2,1)S(1)} %get-tuple-element.54.grid_ref, bf16[1168,128]{1,0:T(8,128)(2,1)S(1)} %collective-permute-done.5.low, bf16[1168,128]{1,0:T(8,128)(2,1)S(1)} %collective-permute-done.6.high), custom_call_target="tpu_custom_call" | custom-call | tf_op jit(solution)/shard_map/pallas_call | solution.py:39
  31.0 0.0 collective-permute-done.8.down_three
  31.0 7.2 %shard_map.93 = f32[36,4,8,128]{3,2,1,0:T(8,128)} custom-call(s32[2]{0:T(128)S(1)} %pad_add_fusion.place, bf16[3,432,1024]{2,1,0:T(8,128)(2,1)S(1)} %shard_map.88.matrix, f32[2,1024,256]{2,1,0:T(8,128)S(1)} %shard_map.92.middle, bf16[1152,128]{1,0:T(8,128)(2,1)S(1)} %get-tuple-element.54.grid_ref, bf16[144,128]{1,0:T(8,128)(2,1)S(1)} %get-tuple-element.56.six_ref, ...), custom_call_target="tpu_custom_call" | custom-call | tf_op jit(solution)/shard_map/pallas_call | solution.py:39
  (7 shorter events, 0.0 us)
Async XLA Ops:
  3.3 12.5 %collective-permute-start = (bf16[624,128]{1,0:T(8,128)(2,1)S(1)}, bf16[624,128]{1,0:T(8,128)(2,1)S(1)}, u32[]{:S(2)}, u32[]{:S(2)}) collective-permute-start(bf16[624,128]{1,0:T(8,128)(2,1)S(1)} %get-tuple-element.32), channel_id=1, source_target_pairs={{0,1},{1,2},{2,3},{3,0},{4,5},{5,6},{6,7},{7,4},{8,9},{9,10},{10,1... | collective-permute-start | bytes 479240 | tf_op jit(solution)/shard_map/ppermute | solution.py:796
  5.5 10.4 %collective-permute-start.1 = (bf16[624,128]{1,0:T(8,128)(2,1)S(1)}, bf16[624,128]{1,0:T(8,128)(2,1)S(1)}, u32[]{:S(2)}, u32[]{:S(2)}) collective-permute-start(bf16[624,128]{1,0:T(8,128)(2,1)S(1)} %get-tuple-element.33), channel_id=1, source_target_pairs={{0,3},{1,0},{2,1},{3,2},{4,7},{5,4},{6,5},{7,6},{8,11},{9,8},{10,9... | collective-permute-start | bytes 479240 | tf_op jit(solution)/shard_map/ppermute | solution.py:796
  7.6 11.0 %collective-permute-start.5 = (bf16[1168,128]{1,0:T(8,128)(2,1)S(1)}, bf16[1168,128]{1,0:T(8,128)(2,1)S(1)}, u32[]{:S(2)}, u32[]{:S(2)}) collective-permute-start(bf16[1168,128]{1,0:T(8,128)(2,1)S(1)} %get-tuple-element.47), channel_id=1, source_target_pairs={{0,4},{1,5},{2,6},{3,7},{4,8},{5,9},{6,10},{7,11},{8,12},{9,13},{1... | collective-permute-start | bytes 897032 | tf_op jit(solution)/shard_map/ppermute | solution.py:796
  9.8 8.8 %collective-permute-start.6 = (bf16[1168,128]{1,0:T(8,128)(2,1)S(1)}, bf16[1168,128]{1,0:T(8,128)(2,1)S(1)}, u32[]{:S(2)}, u32[]{:S(2)}) collective-permute-start(bf16[1168,128]{1,0:T(8,128)(2,1)S(1)} %get-tuple-element.48), channel_id=1, source_target_pairs={{0,28},{1,29},{2,30},{3,31},{4,0},{5,1},{6,2},{7,3},{8,4},{9,5},{1... | collective-permute-start | bytes 897032 | tf_op jit(solution)/shard_map/ppermute | solution.py:796
  9.8 6.1 %collective-permute-start.2 = (bf16[40,128]{1,0:T(8,128)(2,1)S(1)}, bf16[40,128]{1,0:T(8,128)(2,1)S(1)}, u32[]{:S(2)}, u32[]{:S(2)}) collective-permute-start(bf16[40,128]{1,0:T(8,128)(2,1)S(1)} %get-tuple-element.34.own), channel_id=1, source_target_pairs={{0,2},{1,3},{2,0},{3,1},{4,6},{5,7},{6,4},{7,5},{8,10},{9,11},{10,... | collective-permute-start | bytes 30728 | tf_op jit(solution)/shard_map/ppermute | solution.py:796
  16.5 5.7 %collective-permute-start.3 = (bf16[624,128]{1,0:T(8,128)(2,1)S(1)}, bf16[624,128]{1,0:T(8,128)(2,1)S(1)}, u32[]{:S(2)}, u32[]{:S(2)}) collective-permute-start(bf16[624,128]{1,0:T(8,128)(2,1)S(1)} %get-tuple-element.43), channel_id=1, source_target_pairs={{0,4},{1,5},{2,6},{3,7},{4,8},{5,9},{6,10},{7,11},{8,12},{9,13},{1... | collective-permute-start | bytes 479240 | tf_op jit(solution)/shard_map/ppermute | solution.py:796
  18.5 6.3 %collective-permute-start.4 = (bf16[624,128]{1,0:T(8,128)(2,1)S(1)}, bf16[624,128]{1,0:T(8,128)(2,1)S(1)}, u32[]{:S(2)}, u32[]{:S(2)}) collective-permute-start(bf16[624,128]{1,0:T(8,128)(2,1)S(1)} %get-tuple-element.44), channel_id=1, source_target_pairs={{0,28},{1,29},{2,30},{3,31},{4,0},{5,1},{6,2},{7,3},{8,4},{9,5},{1... | collective-permute-start | bytes 479240 | tf_op jit(solution)/shard_map/ppermute | solution.py:796
  24.9 6.1 %collective-permute-start.8 = (bf16[240,128]{1,0:T(8,128)(2,1)S(1)}, bf16[240,128]{1,0:T(8,128)(2,1)S(1)}, u32[]{:S(2)}, u32[]{:S(2)}) collective-permute-start(bf16[240,128]{1,0:T(8,128)(2,1)S(1)} %pad_maximum_fusion.near_three), channel_id=1, source_target_pairs={{0,20},{1,21},{2,22},{3,23},{4,24},{5,25},{6,26},{7,27},{8,28},{9,... | collective-permute-start | bytes 184328 | tf_op jit(solution)/shard_map/ppermute | solution.py:796
  25.0 6.0 %collective-permute-start.7 = (bf16[240,128]{1,0:T(8,128)(2,1)S(1)}, bf16[240,128]{1,0:T(8,128)(2,1)S(1)}, u32[]{:S(2)}, u32[]{:S(2)}) collective-permute-start(bf16[240,128]{1,0:T(8,128)(2,1)S(1)} %pad_maximum_fusion.near_three), channel_id=1, source_target_pairs={{0,12},{1,13},{2,14},{3,15},{4,16},{5,17},{6,18},{7,19},{8,20},{9,... | collective-permute-start | bytes 184328 | tf_op jit(solution)/shard_map/ppermute | solution.py:796

commit v5 on v4

--- a/solution.py
+++ b/solution.py
@@ -119,33 +119,7 @@
             ]
     low_msg[X_LEAF:X_SIX, :] = grid_ref[0 : 4 * GROUP, :]
     high_msg[X_LEAF:X_SIX, :] = grid_ref[4 * GROUP : 8 * GROUP, :]
-    for copy in copies[1:]:
-        copy.wait()
-    count = count_ref[...]
-    for slot in range(8):
-        live_ref[slot * 32 : slot * 32 + 32, :] = jnp.where(
-            count > slot, mass_ref[slot * 32 : slot * 32 + 32, :], F32(0.0)
-        )
-    for msg, y in ((up_msg, 7), (down_msg, 0)):
-        rows = []
-        for x in range(4):
-            rows.append(pos_ref[pl.ds(x * 8 + y, 24, stride=32), :])
-            rows.append(live_ref[pl.ds(x * 8 + y, 8, stride=32), :])
-        high, low = parts(jnp.concatenate(rows, axis=0))
-        msg[0:128, :] = high
-        for x in range(4):
-            msg[128 + 24 * x : 152 + 24 * x, :] = low[32 * x : 32 * x + 24]
-    for msg, x in ((low_msg, 0), (high_msg, 3)):
-        for slot in range(8):
-            for axis in range(3):
-                start = (axis * 8 + slot) * 32 + x * 8
-                near32[pl.ds(axis * 8 + slot, 8, stride=32), :] = pos_ref[start : start + 8, :]
-            start = slot * 32 + x * 8
-            near32[pl.ds(24 + slot, 8, stride=32), :] = live_ref[start : start + 8, :]
-        high, low = parts(near32[...])
-        msg[0:256, :] = high
-        for y in range(8):
-            msg[256 + 24 * y : 280 + 24 * y, :] = low[32 * y : 32 * y + 24]
+    copies[4].wait()
     low_half = iota((COEF, 128), 1) < 64
     even_up, odd_up = up_blocks(up_ref)
     halves_ref[0], halves_ref[1] = even_up, odd_up
@@ -176,6 +150,33 @@
     five_ref[...] = five
     for msg in (up_msg, down_msg):
         msg[Y_FIVE:Y_ROWS, :] = five
+    for copy in copies[1:4]:
+        copy.wait()
+    count = count_ref[...]
+    for slot in range(8):
+        live_ref[slot * 32 : slot * 32 + 32, :] = jnp.where(
+            count > slot, mass_ref[slot * 32 : slot * 32 + 32, :], F32(0.0)
+        )
+    for msg, y in ((up_msg, 7), (down_msg, 0)):
+        rows = []
+        for x in range(4):
+            rows.append(pos_ref[pl.ds(x * 8 + y, 24, stride=32), :])
+            rows.append(live_ref[pl.ds(x * 8 + y, 8, stride=32), :])
+        high, low = parts(jnp.concatenate(rows, axis=0))
+        msg[0:128, :] = high
+        for x in range(4):
+            msg[128 + 24 * x : 152 + 24 * x, :] = low[32 * x : 32 * x + 24]
+    for msg, x in ((low_msg, 0), (high_msg, 3)):
+        for slot in range(8):
+            for axis in range(3):
+                start = (axis * 8 + slot) * 32 + x * 8
+                near32[pl.ds(axis * 8 + slot, 8, stride=32), :] = pos_ref[start : start + 8, :]
+            start = slot * 32 + x * 8
+            near32[pl.ds(24 + slot, 8, stride=32), :] = live_ref[start : start + 8, :]
+        high, low = parts(near32[...])
+        msg[0:256, :] = high
+        for y in range(8):
+            msg[256 + 24 * y : 280 + 24 * y, :] = low[32 * y : 32 * y + 24]
 
 
 def in_hbm(value):
@@ -578,22 +579,27 @@
     return [cells[rows, shift_x * 128 : shift_x * 128 + 256] for shift_x in range(3)]
 
 
-def middle_kernel(matrix, grid_ref, low, high, products, cells):
+def middle_kernel(matrix, grid_ref, low, high, potential, products, out_ref, cells, sem):
+    leaving = pltpu.make_async_copy(potential, out_ref, sem)
+    leaving.start()
     cells[:, 0:128] = low[X_LEAF:X_SIX, :]
     cells[:, 128:256] = grid_ref[0 : 4 * GROUP, :]
     cells[:, 256:384] = grid_ref[4 * GROUP : 8 * GROUP, :]
     cells[:, 384:512] = high[X_LEAF:X_SIX, :]
     for parent in range(2):
         products[parent] = multiply(matrix, slice(0, 1024), windows_x(cells, parent))
+    leaving.wait()
 
 
 def middle_products(*inputs):
-    return kernel_call(
+    return pl.pallas_call(
         middle_kernel,
-        (shape((2, 1024, 256), F32),),
-        inputs,
-        (pltpu.VMEM((4 * GROUP, 512), BF16),),
-    )[0]
+        out_shape=(shape((2, 1024, 256), F32), shape((256, 128), F32)),
+        in_specs=[VMEM] * 5,
+        out_specs=[VMEM, HBM],
+        scratch_shapes=[pltpu.VMEM((4 * GROUP, 512), BF16), pltpu.SemaphoreType.DMA],
+        compiler_params=pltpu.CompilerParams(vmem_limit_bytes=20 * 1024 * 1024),
+    )(*inputs)
 
 
 def levels_kernel(
@@ -825,7 +831,7 @@
         inner.reshape(256, 128), positions.reshape(768, 128), counts, below, above, low_corner,
         high_corner,
     )
-    middle = middle_products(lax.optimization_barrier((matrix, low_corner))[0], grid, low, high)
+    middle, potential = middle_products(matrix, grid, low, high, potential)
     up_three, down_three, potential, middle = lax.optimization_barrier(
         (up_three, down_three, potential, middle)
     )

time: 38.5 us -> 37.8 us (0.982)
  Pallas kernels: 23.4 us -> 22.8 us
    pallas_call x7 -> x6, Pallas kernels: 18.7 us -> 16 us  [kernel_call(): pl.pallas_call(body, out_shape=outs, in_specs=[SMEM] * scalars + [space]...]
    pallas_call x0 -> x1, Pallas kernels: none -> 1.98 us  [middle_products(): pl.pallas_call(middle_kernel, out_shape=(shape((2, 1024, 256), F32), shap...]
  transfers between devices with their start and end apart: 9 -> 9, of which waited for: 2 -> 2; matrix products, arithmetic and copies ran while one was open for 0% -> 0% of each run, Pallas kernels for 36% -> 34%
where the time goes in v5:
time: 37.8 us; the launch traced here: 37.7 us
  Pallas kernels  22.8 us (60%)
  starting transfers between devices  11.1 us (29%)
  waiting for transfers between devices  2.77 us (7%)
  between operations  0.89 us (2%)
    pallas_call x6, Pallas kernels, kernel_call(): pl.pallas_call(body, out_shape=outs, in_specs=[SMEM] * scalars + [space]...  16 us
    ppermute x9, starting transfers between devices, moved(): return lax.ppermute(value, ('gx', 'gy'), table)  11.1 us
    pallas_call x1, Pallas kernels, plane_pairs(): pl.pallas_call(plane_kernel, out_shape=(shape((3, 8, 4, 8, 128), F32), sh...  4.76 us
    ppermute x9, waiting for transfers between devices, moved(): return lax.ppermute(value, ('gx', 'gy'), table)  2.77 us
    pallas_call x1, Pallas kernels, middle_products(): pl.pallas_call(middle_kernel, out_shape=(shape((2, 1024, 256), F32), shap...  1.98 us
  transfers between devices with their start and end apart: 9, of which 2 were waited for; matrix products, arithmetic and copies ran while one was open for 0% of the time, Pallas kernels for 34%

profile of v5, /device:TPU:1, one launch (start us, length us, event | category | flops | bytes accessed | tf_op | source)
XLA Modules:
  0.0 37.7 jit_solution(16053275529877209088)
XLA Ops:
  0.6 2.6 %shard_map.86 = (bf16[1152,128]{1,0:T(8,128)(2,1)S(1)}, bf16[624,128]{1,0:T(8,128)(2,1)S(1)}, bf16[624,128]{1,0:T(8,128)(2,1)S(1)}, bf16[1168,128]{1,0:T(8,128)(...) custom-call(bf16[1152,128]{1,0:T(8,128)(2,1)} %bitcast.16, ...), custom_call_target="tpu_custom_call" | custom-call | tf_op jit(solution)/shard_map/pallas_call | solution.py:39
  3.3 2.2 %collective-permute-start = (bf16[624,128]{1,0:T(8,128)(2,1)S(1)}, bf16[624,128]{1,0:T(8,128)(2,1)S(1)}, u32[]{:S(2)}, u32[]{:S(2)}) collective-permute-start(bf16[624,128]{1,0:T(8,128)(2,1)S(1)} %get-tuple-element.33), channel_id=1, source_target_pairs={{0,1},{1,2},{2,3},{3,0},{4,5},{5,6},{6,7},{7,4},{8,9},{9,10},{10,1... | collective-permute-start | bytes 479240 | tf_op jit(solution)/shard_map/ppermute | solution.py:802
  5.5 2.1 %collective-permute-start.1 = (bf16[624,128]{1,0:T(8,128)(2,1)S(1)}, bf16[624,128]{1,0:T(8,128)(2,1)S(1)}, u32[]{:S(2)}, u32[]{:S(2)}) collective-permute-start(bf16[624,128]{1,0:T(8,128)(2,1)S(1)} %get-tuple-element.34), channel_id=1, source_target_pairs={{0,3},{1,0},{2,1},{3,2},{4,7},{5,4},{6,5},{7,6},{8,11},{9,8},{10,9... | collective-permute-start | bytes 479240 | tf_op jit(solution)/shard_map/ppermute | solution.py:802
  7.6 2.2 %collective-permute-start.5 = (bf16[1168,128]{1,0:T(8,128)(2,1)S(1)}, bf16[1168,128]{1,0:T(8,128)(2,1)S(1)}, u32[]{:S(2)}, u32[]{:S(2)}) collective-permute-start(bf16[1168,128]{1,0:T(8,128)(2,1)S(1)} %get-tuple-element.48), channel_id=1, source_target_pairs={{0,4},{1,5},{2,6},{3,7},{4,8},{5,9},{6,10},{7,11},{8,12},{9,13},{1... | collective-permute-start | bytes 897032 | tf_op jit(solution)/shard_map/ppermute | solution.py:802
  9.8 0.0 collective-permute-start.6
  9.8 0.5 %collective-permute-start.2 = (bf16[40,128]{1,0:T(8,128)(2,1)S(1)}, bf16[40,128]{1,0:T(8,128)(2,1)S(1)}, u32[]{:S(2)}, u32[]{:S(2)}) collective-permute-start(bf16[40,128]{1,0:T(8,128)(2,1)S(1)} %get-tuple-element.35.own), channel_id=1, source_target_pairs={{0,2},{1,3},{2,0},{3,1},{4,6},{5,7},{6,4},{7,5},{8,10},{9,11},{10,... | collective-permute-start | bytes 30728 | tf_op jit(solution)/shard_map/ppermute | solution.py:802
  10.3 0.1 pad_add_fusion.place
  10.4 4.8 %shard_map.87 = (f32[3,8,4,8,128]{4,3,2,1,0:T(8,128)S(1)}, f32[3,4,8,4,8,128]{5,4,3,2,1,0:T(8,128)S(1)}, bf16[36,11376]{1,0:T(8,128)(2,1)S(1)}, bf16[36,288]{1,0:T(8,128)(2,1)S(1)}) custom-call(f32[3,8,4,8,128]{4,3,2,1,0:T(8,128)S(1)} %bitcast.11, f32[8,4,8,128]{3,2,1,0:T(8,128)S(1)} %bitcast.14, bf16[36,11376]{1,0:T(8,128)(2,1)} %far_hbm.1, ...), custom_call_target="tpu_custom_call" | custom-call | tf_op jit(solution)/shard_map/pallas_call | solution.py:350
  15.1 0.6 %shard_map.88.matrix = bf16[3,432,1024]{2,1,0:T(8,128)(2,1)S(1)} custom-call(bf16[36,11376]{1,0:T(8,128)(2,1)S(1)} %get-tuple-element.39.far_ref), custom_call_target="tpu_custom_call" | custom-call | tf_op jit(solution)/shard_map/pallas_call | solution.py:39
  15.7 0.1 collective-permute-done.2.two
  15.8 0.0 collective-permute-done.below
  15.8 0.0 collective-permute-done.1.above
  15.8 0.7 %shard_map.89 = (bf16[624,128]{1,0:T(8,128)(2,1)S(1)}, bf16[624,128]{1,0:T(8,128)(2,1)S(1)}) custom-call(s32[2]{0:T(128)S(1)} %pad_add_fusion.place, bf16[624,128]{1,0:T(8,128)(2,1)S(1)} %collective-permute-done.below, bf16[624,128]{1,0:T(8,128)(2,1)S(1)} %collective-permute-done.1.above, bf16[40,128]{1,0:T(8,128)(2,1)S(1)} %collective-permute-done.2.two, ...), custom_call_target="tpu_custom_call" | custom-call | tf_op jit(solution)/shard_map/pallas_call | solution.py:39
  16.5 2.0 %collective-permute-start.3 = (bf16[624,128]{1,0:T(8,128)(2,1)S(1)}, bf16[624,128]{1,0:T(8,128)(2,1)S(1)}, u32[]{:S(2)}, u32[]{:S(2)}) collective-permute-start(bf16[624,128]{1,0:T(8,128)(2,1)S(1)} %get-tuple-element.44), channel_id=1, source_target_pairs={{0,4},{1,5},{2,6},{3,7},{4,8},{5,9},{6,10},{7,11},{8,12},{9,13},{1... | collective-permute-start | bytes 479240 | tf_op jit(solution)/shard_map/ppermute | solution.py:802
  18.5 0.0 collective-permute-done.5.low
  18.5 0.0 collective-permute-done.6.high
  18.5 3.6 %shard_map.90 = f32[8,4,8,128]{3,2,1,0:T(8,128)S(1)} custom-call(f32[3,8,4,8,128]{4,3,2,1,0:T(8,128)S(1)} %get-tuple-element.46.sums_ref, f32[3,4,8,4,8,128]{5,4,3,2,1,0:T(8,128)S(1)} %get-tuple-element.47.shifted_ref, f32[3,8,4,8,128]{4,3,2,1,0:T(8,128)S(1)} %bitcast.12, bf16[1168,128]{1,0:T(8,128)(2,1)S(1)} %collective-permute-done.5.low, ...), custom_call_target="tpu_custom_call" | custom-call | tf_op jit(solution)/shard_map/pallas_call | solution.py:39
  22.2 2.7 %collective-permute-done.4.high_corner = bf16[624,128]{1,0:T(8,128)(2,1)S(1)} collective-permute-done((bf16[624,128]{1,0:T(8,128)(2,1)S(1)}, bf16[624,128]{1,0:T(8,128)(2,1)S(1)}, u32[]{:S(2)}, u32[]{:S(2)}) %collective-permute-start.4) | collective-permute-done | bytes 159776 | tf_op jit(solution)/shard_map/ppermute | solution.py:802
  24.9 0.1 collective-permute-start.8
  25.0 2.0 %collective-permute-start.7 = (bf16[240,128]{1,0:T(8,128)(2,1)S(1)}, bf16[240,128]{1,0:T(8,128)(2,1)S(1)}, u32[]{:S(2)}, u32[]{:S(2)}) collective-permute-start(bf16[240,128]{1,0:T(8,128)(2,1)S(1)} %pad_maximum_fusion.near_three), channel_id=1, source_target_pairs={{0,12},{1,13},{2,14},{3,15},{4,16},{5,17},{6,18},{7,19},{8,20},{9,... | collective-permute-start | bytes 184328 | tf_op jit(solution)/shard_map/ppermute | solution.py:802
  27.0 1.3 %shard_map.91.potential = f32[256,128]{1,0:T(8,128)S(1)} custom-call(f32[256,128]{1,0:T(8,128)S(1)} %bitcast.13, f32[768,128]{1,0:T(8,128)S(1)} %get-tuple-element.36.pos_ref, s32[32,128]{1,0:T(8,128)S(1)} %get-tuple-element.54.count_ref, bf16[624,128]{1,0:T(8,128)(2,1)S(1)} %collective-permute-done.below, ...), custom_call_target="tpu_custom_call" | custom-call | tf_op jit(solution)/shard_map/pallas_call | solution.py:39
  28.3 2.0 %shard_map.92 = (f32[2,1024,256]{2,1,0:T(8,128)S(1)}, f32[256,128]{1,0:T(8,128)}) custom-call(bf16[3,432,1024]{2,1,0:T(8,128)(2,1)S(1)} %shard_map.88.matrix, bf16[1152,128]{1,0:T(8,128)(2,1)S(1)} %get-tuple-element.52.grid_ref, bf16[1168,128]{1,0:T(8,128)(2,1)S(1)} %collective-permute-done.5.low, bf16[1168,128]{1,0:T(8,128)(2,1)S(1)} %collective-permute-done.6.high, ...), custom_call_target="tpu_custom_call" | custom-call | tf_op jit(solution)/shard_map/pallas_call | solution.py:595
  30.3 0.0 collective-permute-done.7.up_three
  30.3 7.2 %shard_map.93 = f32[36,4,8,128]{3,2,1,0:T(8,128)} custom-call(s32[2]{0:T(128)S(1)} %pad_add_fusion.place, bf16[3,432,1024]{2,1,0:T(8,128)(2,1)S(1)} %shard_map.88.matrix, f32[2,1024,256]{2,1,0:T(8,128)S(1)} %get-tuple-element.57.middle, bf16[1152,128]{1,0:T(8,128)(2,1)S(1)} %get-tuple-element.52.grid_ref, bf16[144,128]{1,0:T(8,128)(2,1)S(1)} %get-tuple-element.58.six_ref, ...), custom_call_target="tpu_custom_call" | custom-call | tf_op jit(solution)/shard_map/pallas_call | solution.py:39
  (7 shorter events, 0.0 us)
Async XLA Ops:
  3.3 12.5 %collective-permute-start = (bf16[624,128]{1,0:T(8,128)(2,1)S(1)}, bf16[624,128]{1,0:T(8,128)(2,1)S(1)}, u32[]{:S(2)}, u32[]{:S(2)}) collective-permute-start(bf16[624,128]{1,0:T(8,128)(2,1)S(1)} %get-tuple-element.33), channel_id=1, source_target_pairs={{0,1},{1,2},{2,3},{3,0},{4,5},{5,6},{6,7},{7,4},{8,9},{9,10},{10,1... | collective-permute-start | bytes 479240 | tf_op jit(solution)/shard_map/ppermute | solution.py:802
  5.5 10.4 %collective-permute-start.1 = (bf16[624,128]{1,0:T(8,128)(2,1)S(1)}, bf16[624,128]{1,0:T(8,128)(2,1)S(1)}, u32[]{:S(2)}, u32[]{:S(2)}) collective-permute-start(bf16[624,128]{1,0:T(8,128)(2,1)S(1)} %get-tuple-element.34), channel_id=1, source_target_pairs={{0,3},{1,0},{2,1},{3,2},{4,7},{5,4},{6,5},{7,6},{8,11},{9,8},{10,9... | collective-permute-start | bytes 479240 | tf_op jit(solution)/shard_map/ppermute | solution.py:802
  7.6 11.0 %collective-permute-start.5 = (bf16[1168,128]{1,0:T(8,128)(2,1)S(1)}, bf16[1168,128]{1,0:T(8,128)(2,1)S(1)}, u32[]{:S(2)}, u32[]{:S(2)}) collective-permute-start(bf16[1168,128]{1,0:T(8,128)(2,1)S(1)} %get-tuple-element.48), channel_id=1, source_target_pairs={{0,4},{1,5},{2,6},{3,7},{4,8},{5,9},{6,10},{7,11},{8,12},{9,13},{1... | collective-permute-start | bytes 897032 | tf_op jit(solution)/shard_map/ppermute | solution.py:802
  9.8 8.8 %collective-permute-start.6 = (bf16[1168,128]{1,0:T(8,128)(2,1)S(1)}, bf16[1168,128]{1,0:T(8,128)(2,1)S(1)}, u32[]{:S(2)}, u32[]{:S(2)}) collective-permute-start(bf16[1168,128]{1,0:T(8,128)(2,1)S(1)} %get-tuple-element.49), channel_id=1, source_target_pairs={{0,28},{1,29},{2,30},{3,31},{4,0},{5,1},{6,2},{7,3},{8,4},{9,5},{1... | collective-permute-start | bytes 897032 | tf_op jit(solution)/shard_map/ppermute | solution.py:802
  9.8 6.1 %collective-permute-start.2 = (bf16[40,128]{1,0:T(8,128)(2,1)S(1)}, bf16[40,128]{1,0:T(8,128)(2,1)S(1)}, u32[]{:S(2)}, u32[]{:S(2)}) collective-permute-start(bf16[40,128]{1,0:T(8,128)(2,1)S(1)} %get-tuple-element.35.own), channel_id=1, source_target_pairs={{0,2},{1,3},{2,0},{3,1},{4,6},{5,7},{6,4},{7,5},{8,10},{9,11},{10,... | collective-permute-start | bytes 30728 | tf_op jit(solution)/shard_map/ppermute | solution.py:802
  16.5 5.7 %collective-permute-start.3 = (bf16[624,128]{1,0:T(8,128)(2,1)S(1)}, bf16[624,128]{1,0:T(8,128)(2,1)S(1)}, u32[]{:S(2)}, u32[]{:S(2)}) collective-permute-start(bf16[624,128]{1,0:T(8,128)(2,1)S(1)} %get-tuple-element.44), channel_id=1, source_target_pairs={{0,4},{1,5},{2,6},{3,7},{4,8},{5,9},{6,10},{7,11},{8,12},{9,13},{1... | collective-permute-start | bytes 479240 | tf_op jit(solution)/shard_map/ppermute | solution.py:802
  18.5 6.3 %collective-permute-start.4 = (bf16[624,128]{1,0:T(8,128)(2,1)S(1)}, bf16[624,128]{1,0:T(8,128)(2,1)S(1)}, u32[]{:S(2)}, u32[]{:S(2)}) collective-permute-start(bf16[624,128]{1,0:T(8,128)(2,1)S(1)} %get-tuple-element.45), channel_id=1, source_target_pairs={{0,28},{1,29},{2,30},{3,31},{4,0},{5,1},{6,2},{7,3},{8,4},{9,5},{1... | collective-permute-start | bytes 479240 | tf_op jit(solution)/shard_map/ppermute | solution.py:802
  24.9 5.4 %collective-permute-start.8 = (bf16[240,128]{1,0:T(8,128)(2,1)S(1)}, bf16[240,128]{1,0:T(8,128)(2,1)S(1)}, u32[]{:S(2)}, u32[]{:S(2)}) collective-permute-start(bf16[240,128]{1,0:T(8,128)(2,1)S(1)} %pad_maximum_fusion.near_three), channel_id=1, source_target_pairs={{0,20},{1,21},{2,22},{3,23},{4,24},{5,25},{6,26},{7,27},{8,28},{9,... | collective-permute-start | bytes 184328 | tf_op jit(solution)/shard_map/ppermute | solution.py:802
  25.0 5.3 %collective-permute-start.7 = (bf16[240,128]{1,0:T(8,128)(2,1)S(1)}, bf16[240,128]{1,0:T(8,128)(2,1)S(1)}, u32[]{:S(2)}, u32[]{:S(2)}) collective-permute-start(bf16[240,128]{1,0:T(8,128)(2,1)S(1)} %pad_maximum_fusion.near_three), channel_id=1, source_target_pairs={{0,12},{1,13},{2,14},{3,15},{4,16},{5,17},{6,18},{7,19},{8,20},{9,... | collective-permute-start | bytes 184328 | tf_op jit(solution)/shard_map/ppermute | solution.py:802
